TPU v7x, 512 devices: a whole 4x8x8 slice. The times are simulated.
512 devices in a mesh: dp: 8 (over y_hi, core), expert: 64 (over z, x, y_lo).
Axes of the slice: x: 4, y: 8 (y_hi: 4, y_lo: 2; y = y_hi * 2 + y_lo), z: 8, core: 2. Of those that a mesh axis runs over, the one named last changes fastest.
Arguments:
- tokens: bfloat16 [65536, 3584], P(('dp', 'expert')), may hold values from -6 to 6
- cotangent: bfloat16 [65536, 3584], P(('dp', 'expert')), may hold values from -0.59765625 to 0.59765625
- route_ids: int32 [65536, 8], P(('dp', 'expert')), may hold values from 0 to 383, as said below
- gates: bfloat16 [65536, 8], P(('dp', 'expert')), may hold values from 0.099609375 to 1
- w_gate: bfloat16 [64, 3584, 128], P('expert', None, 'dp'), may hold values from -0.09375 to 0.09375
- w_up: bfloat16 [64, 3584, 128], P('expert', None, 'dp'), may hold values from -0.09375 to 0.09375
- w_down: bfloat16 [64, 3584, 128], P('expert', None, 'dp'), may hold values from -0.125 to 0.125
Outputs:
- relaid_gate: bfloat16 [64, 3584, 128], P('expert', 'dp')
- relaid_up: bfloat16 [64, 3584, 128], P('expert', 'dp')
- relaid_down: bfloat16 [64, 3584, 128], P('expert', 'dp')
- grad_gate: float32 [64, 3584, 128], P('expert', 'dp')
- grad_up: float32 [64, 3584, 128], P('expert', 'dp')
- grad_down: float32 [64, 3584, 128], P('expert', 'dp')
- token_grad: bfloat16 [65536, 3584], P(('dp', 'expert'))
- gate_grad: float32 [65536, 8], P(('dp', 'expert'))
Inputs may be any that keep to these rules, and one draw needn't show every extreme that they name: `route_ids`: each row names 8 different experts. Among the 128 rows of one device, at most 6 routes name any one expert below 4; on every device of one index of dp, one same expert below 4 is named by exactly 6 routes.
All inputs are finite; a program needn't handle non-finite values.
Results may differ from a plain program's by a relative error of at most 0.02.
Values may be sent and summed in bfloat16 or wider, within the bound.
No kernel may reach another device: no remote copies, remote signals or barrier semaphores. Data moves between devices by JAX's collectives and lax.ppermute only.
A program may use at most 128 MiB of HBM per device.

v0:
```python
import jax
import jax.numpy as jnp
from jax import lax
from jax.sharding import PartitionSpec as P

HSPLIT = 16
CAP = 6


def copies(values, experts):
    grouped = values.reshape((experts, CAP) + values.shape[1:])
    return jnp.repeat(grouped, HSPLIT, axis=0)


def forward_part(slot_tokens, gate_slab, up_slab):
    pre_gate = jnp.dot(slot_tokens, gate_slab, preferred_element_type=jnp.float32)
    pre_up = jnp.dot(slot_tokens, up_slab, preferred_element_type=jnp.float32)
    sigmoid_gate = jax.nn.sigmoid(pre_gate)
    activation = pre_gate * sigmoid_gate
    hidden = (activation * pre_up).astype(jnp.bfloat16)
    return (pre_gate, pre_up, sigmoid_gate, activation, hidden)


def shards(tokens, cotangent, route_ids, gates, w_gate, w_up, w_down):
    slabs = lax.axis_size("expert")
    experts = slabs // HSPLIT
    tok_count, features = tokens.shape
    top_count = route_ids.shape[1]
    slot_total = experts * CAP
    flat_ids = route_ids.reshape(-1)
    expert_hits = (flat_ids[:, None] == jnp.arange(experts, dtype=jnp.int32)[None, :]).astype(
        jnp.int32
    )
    earlier = jnp.cumsum(expert_hits, axis=0) - expert_hits
    slot_rank = jnp.sum(earlier * expert_hits, axis=1)
    in_slab = jnp.sum(expert_hits, axis=1) > 0
    slot_index = flat_ids * CAP + slot_rank
    table = (slot_index[:, None] == jnp.arange(slot_total, dtype=jnp.int32)[None, :]) & in_slab[
        :, None
    ]
    select = table.reshape(tok_count, top_count, slot_total)
    picked = jnp.any(select, axis=1)
    pick_half = picked.astype(jnp.bfloat16)
    token_slots = jnp.einsum(
        "tc,td->cd", pick_half, tokens, preferred_element_type=jnp.float32
    ).astype(jnp.bfloat16)
    cotan_slots = jnp.einsum(
        "tc,td->cd", pick_half, cotangent, preferred_element_type=jnp.float32
    ).astype(jnp.bfloat16)
    gate_slots = jnp.sum(
        jnp.where(select, gates[:, :, None].astype(jnp.float32), 0.0), axis=(0, 1)
    ).astype(jnp.bfloat16)
    send_tok = copies(token_slots, experts)
    send_cotan = copies(cotan_slots, experts)
    send_gate = copies(gate_slots, experts)
    new_gate, new_up, new_down = (
        lax.all_to_all(w_gate, "dp", split_axis=1, concat_axis=2, tiled=True),
        lax.all_to_all(w_up, "dp", split_axis=1, concat_axis=2, tiled=True),
        lax.all_to_all(w_down, "dp", split_axis=1, concat_axis=2, tiled=True),
    )
    full_gate, full_up, full_down = (
        lax.all_gather(new_gate, "dp", axis=1, tiled=True),
        lax.all_gather(new_up, "dp", axis=1, tiled=True),
        lax.all_gather(new_down, "dp", axis=1, tiled=True),
    )
    gate_slab = full_gate[0]
    up_slab = full_up[0]
    down_slab = full_down[0]
    recv_tok, recv_cotan, recv_gate = (
        lax.all_to_all(send_tok, "expert", split_axis=0, concat_axis=0, tiled=True),
        lax.all_to_all(send_cotan, "expert", split_axis=0, concat_axis=0, tiled=True),
        lax.all_to_all(send_gate, "expert", split_axis=0, concat_axis=0, tiled=True),
    )
    slot_tokens = recv_tok.reshape(-1, features)
    pre_gate, pre_up, sigmoid_gate, activation, hidden = forward_part(
        slot_tokens, gate_slab, up_slab
    )
    slot_cotan = recv_cotan.reshape(-1, features)
    slot_gates = recv_gate.reshape(-1).astype(jnp.float32)[:, None]
    back_proj = jnp.dot(slot_cotan, down_slab, preferred_element_type=jnp.float32)
    score_part = jnp.sum(hidden.astype(jnp.float32) * back_proj, axis=1).astype(jnp.bfloat16)
    scaled = slot_gates * back_proj
    d_gate = (scaled * pre_up * sigmoid_gate * (1.0 + pre_gate * (1.0 - sigmoid_gate))).astype(
        jnp.bfloat16
    )
    d_up = (scaled * activation).astype(jnp.bfloat16)
    hidden_gated = (slot_gates * hidden.astype(jnp.float32)).astype(jnp.bfloat16)
    partial_value = (
        jnp.einsum("rh,dh->rd", d_gate, gate_slab, preferred_element_type=jnp.float32)
        + jnp.einsum("rh,dh->rd", d_up, up_slab, preferred_element_type=jnp.float32)
    ).astype(jnp.bfloat16)
    grad_gate_part = jnp.einsum(
        "rd,rh->dh", slot_tokens, d_gate, preferred_element_type=jnp.float32
    )
    grad_up_part = jnp.einsum("rd,rh->dh", slot_tokens, d_up, preferred_element_type=jnp.float32)
    grad_down_part = jnp.einsum(
        "rd,rh->dh", slot_cotan, hidden_gated, preferred_element_type=jnp.float32
    )
    grad_gate, grad_up, grad_down = (
        lax.psum_scatter(
            grad_gate_part[None].astype(jnp.bfloat16), "dp", scatter_dimension=1, tiled=True
        ).astype(jnp.float32),
        lax.psum_scatter(
            grad_up_part[None].astype(jnp.bfloat16), "dp", scatter_dimension=1, tiled=True
        ).astype(jnp.float32),
        lax.psum_scatter(
            grad_down_part[None].astype(jnp.bfloat16), "dp", scatter_dimension=1, tiled=True
        ).astype(jnp.float32),
    )
    back_parts, back_scores = (
        lax.all_to_all(
            partial_value.reshape(slabs, CAP, features),
            "expert",
            split_axis=0,
            concat_axis=0,
            tiled=True,
        ),
        lax.all_to_all(
            score_part.reshape(slabs, CAP), "expert", split_axis=0, concat_axis=0, tiled=True
        ),
    )
    part_sum = jnp.sum(
        back_parts.reshape(experts, HSPLIT, CAP, features).astype(jnp.float32), axis=1
    )
    part_sum = part_sum.reshape(slot_total, features)
    score_sum = jnp.sum(
        back_scores.reshape(experts, HSPLIT, CAP).astype(jnp.float32), axis=1
    ).reshape(slot_total)
    token_grad = jnp.einsum(
        "tc,cd->td", picked.astype(jnp.float32), part_sum, precision=lax.Precision.HIGHEST
    ).astype(jnp.bfloat16)
    gate_grad = jnp.einsum(
        "tkc,c->tk", select.astype(jnp.float32), score_sum, precision=lax.Precision.HIGHEST
    )
    return (new_gate, new_up, new_down, grad_gate, grad_up, grad_down, token_grad, gate_grad)


def solution(mesh):
    in_specs = (
        P(("dp", "expert"), None),
        P(("dp", "expert"), None),
        P(("dp", "expert"), None),
        P(("dp", "expert"), None),
        P("expert", None, "dp"),
        P("expert", None, "dp"),
        P("expert", None, "dp"),
    )
    out_specs = (
        P("expert", "dp", None),
        P("expert", "dp", None),
        P("expert", "dp", None),
        P("expert", "dp", None),
        P("expert", "dp", None),
        P("expert", "dp", None),
        P(("dp", "expert"), None),
        P(("dp", "expert"), None),
    )
    return jax.shard_map(shards, mesh=mesh, in_specs=in_specs, out_specs=out_specs, check_vma=False)
```

profile of v0, /device:TPU:1, one launch (start us, length us, event | category | flops | bytes accessed | tf_op | source)
XLA Modules:
  0.0 505.8 jit_solution(7459007044376049819)
XLA Ops:
  12.9 15.3 %all-to-all-start.4 = ((bf16[64,1,6]{2,1,0:T(2,128)(2,1)}), bf16[64,1,6]{2,1,0:T(2,128)(2,1)S(1)}, u32[]{:S(2)}, u32[]{:S(2)}) async-start(bf16[64,1,6]{2,1,0:T(2,128)(2,1)} %copy.119), calls=%async_computation.4 | async-start | bytes 65536 | tf_op jit(solution)/shard_map/all_to_all | solution.py:72
  28.2 3.7 copy.105
  32.5 20.6 %reduce.6 = bf16[3584,16]{1,0:T(8,128)(2,1)} reduce(bf16[3584,1,16]{2,1,0:T(2,128)(2,1)S(1)} %bitcast.87, bf16[]{:T(256)} %broadcast.78), dimensions={1}, to_apply=%bitcast.58.reduce_sub_computation | reduce | bytes 229378
  53.1 2.8 reshape.176
  55.9 7.5 %all-to-all-start = ((bf16[8,2,3584]{2,1,0:T(2,128)(2,1)}), bf16[8,2,3584]{2,1,0:T(2,128)(2,1)S(1)}, u32[]{:S(2)}, u32[]{:S(2)}) async-start(bf16[8,2,3584]{2,1,0:T(2,128)(2,1)} %reshape.176), calls=%async_computation | async-start | bytes 229376 | tf_op jit(solution)/shard_map/all_to_all | solution.py:57
  65.9 20.6 %reduce.7 = bf16[3584,16]{1,0:T(8,128)(2,1)} reduce(bf16[3584,1,16]{2,1,0:T(2,128)(2,1)S(1)} %bitcast.92, bf16[]{:T(256)} %broadcast.78), dimensions={1}, to_apply=%bitcast.60.reduce_sub_computation | reduce | bytes 229378
  86.5 2.8 reshape.178
  89.3 7.8 %all-to-all-start.1 = ((bf16[8,2,3584]{2,1,0:T(2,128)(2,1)}), bf16[8,2,3584]{2,1,0:T(2,128)(2,1)S(1)}, u32[]{:S(2)}, u32[]{:S(2)}) async-start(bf16[8,2,3584]{2,1,0:T(2,128)(2,1)} %reshape.178), calls=%async_computation.1 | async-start | bytes 229376 | tf_op jit(solution)/shard_map/all_to_all | solution.py:58
  99.5 20.6 %reduce.8 = bf16[3584,16]{1,0:T(8,128)(2,1)} reduce(bf16[3584,1,16]{2,1,0:T(2,128)(2,1)S(1)} %bitcast.88, bf16[]{:T(256)} %broadcast.78), dimensions={1}, to_apply=%bitcast.62.reduce_sub_computation | reduce | bytes 229378
  120.1 2.8 reshape.180
  122.9 7.2 %all-to-all-start.2 = ((bf16[8,2,3584]{2,1,0:T(2,128)(2,1)}), bf16[8,2,3584]{2,1,0:T(2,128)(2,1)S(1)}, u32[]{:S(2)}, u32[]{:S(2)}) async-start(bf16[8,2,3584]{2,1,0:T(2,128)(2,1)} %reshape.180), calls=%async_computation.2 | async-start | bytes 229376 | tf_op jit(solution)/shard_map/all_to_all | solution.py:59
  130.5 8.1 %all-to-all-done.2 = bf16[8,2,3584]{2,1,0:T(2,128)(2,1)S(1)} async-done(((bf16[8,2,3584]{2,1,0:T(2,128)(2,1)}), bf16[8,2,3584]{2,1,0:T(2,128)(2,1)S(1)}, u32[]{:S(2)}, u32[]{:S(2)}) %all-to-all-start.2) | async-done | bytes 114720 | tf_op jit(solution)/shard_map/all_to_all | solution.py:59
  140.7 10.7 %all-to-all-start.3 = ((bf16[64,6,3584]{2,1,0:T(8,128)(2,1)}), bf16[64,6,3584]{2,1,0:T(8,128)(2,1)}, u32[]{:S(2)}, u32[]{:S(2)}) async-start(bf16[64,6,3584]{2,1,0:T(8,128)(2,1)} %bitcast.86), calls=%async_computation.3 | async-start | bytes 7340032 | tf_op jit(solution)/shard_map/all_to_all | solution.py:70
  151.7 82.8 %all-to-all-done.3 = bf16[64,6,3584]{2,1,0:T(8,128)(2,1)} async-done(((bf16[64,6,3584]{2,1,0:T(8,128)(2,1)}), bf16[64,6,3584]{2,1,0:T(8,128)(2,1)}, u32[]{:S(2)}, u32[]{:S(2)}) %all-to-all-start.3) | async-done | bytes 2752544 | tf_op jit(solution)/shard_map/all_to_all | solution.py:70
  236.7 8.6 %all-to-all-start.5 = ((bf16[64,6,3584]{2,1,0:T(8,128)(2,1)}), bf16[64,6,3584]{2,1,0:T(8,128)(2,1)}, u32[]{:S(2)}, u32[]{:S(2)}) async-start(bf16[64,6,3584]{2,1,0:T(8,128)(2,1)} %bitcast.85), calls=%async_computation.5 | async-start | bytes 7340032 | tf_op jit(solution)/shard_map/all_to_all | solution.py:71
  256.3 45.5 %all_gather.10 = bf16[1,3584,128]{2,1,0:T(8,128)(2,1)S(1)} all-gather(bf16[1,448,128]{2,1,0:T(8,128)(2,1)S(1)} %copy.126), channel_id=1, replica_groups=mesh['dp'=8,'expert'=64] {'dp'}, dimensions={1}, use_global_device_ids=true | all-gather | bytes 1032192 | tf_op jit(solution)/shard_map/all_gather | solution.py:63
  301.8 17.0 %all_gather.11 = bf16[1,3584,128]{2,1,0:T(8,128)(2,1)S(1)} all-gather(bf16[1,448,128]{2,1,0:T(8,128)(2,1)S(1)} %copy.125), channel_id=1, replica_groups=mesh['dp'=8,'expert'=64] {'dp'}, dimensions={1}, use_global_device_ids=true | all-gather | bytes 1032192 | tf_op jit(solution)/shard_map/all_gather | solution.py:62
  318.8 16.9 %all_gather.9 = bf16[1,3584,128]{2,1,0:T(8,128)(2,1)} all-gather(bf16[1,448,128]{2,1,0:T(8,128)(2,1)S(1)} %copy.127), channel_id=1, replica_groups=mesh['dp'=8,'expert'=64] {'dp'}, dimensions={1}, use_global_device_ids=true | all-gather | bytes 1032192 | tf_op jit(solution)/shard_map/all_gather | solution.py:64
  335.8 5.5 %reshape.155 = bf16[384,3584]{1,0:T(8,128)(2,1)} reshape(bf16[64,6,3584]{2,1,0:T(8,128)(2,1)} %all-to-all-done.3) | data formatting | bytes 5505024 | tf_op jit(solution)/shard_map/reshape | solution.py:74
  341.2 2.9 fusion.9
  345.1 5.5 %reshape.158 = bf16[384,3584]{1,0:T(8,128)(2,1)} reshape(bf16[64,6,3584]{2,1,0:T(8,128)(2,1)} %all-to-all-done.5) | data formatting | bytes 5505024 | tf_op jit(solution)/shard_map/reshape | solution.py:78
  350.6 3.1 fusion.14
  355.6 3.3 fusion.4
  359.6 13.3 %all-to-all-start.7 = ((bf16[64,1,6]{2,1,0:T(2,128)(2,1)}), bf16[64,1,6]{2,1,0:T(2,128)(2,1)S(1)}, u32[]{:S(2)}, u32[]{:S(2)}) async-start(bf16[64,1,6]{2,1,0:T(2,128)(2,1)} %convert_element_type.149), calls=%async_computation.10 | async-start | bytes 65536 | tf_op jit(solution)/shard_map/all_to_all | solution.py:118
  372.9 5.0 fusion
  377.9 5.4 %reshape.159 = bf16[64,6,3584]{2,1,0:T(8,128)(2,1)} reshape(bf16[384,3584]{1,0:T(8,128)(2,1)} %fusion) | data formatting | bytes 5505024 | tf_op jit(solution)/shard_map/reshape | solution.py:112
  383.3 10.9 %all-to-all-start.6 = ((bf16[64,6,3584]{2,1,0:T(8,128)(2,1)}), bf16[64,6,3584]{2,1,0:T(8,128)(2,1)}, u32[]{:S(2)}, u32[]{:S(2)}) async-start(bf16[64,6,3584]{2,1,0:T(8,128)(2,1)} %reshape.159), calls=%async_computation.9 | async-start | bytes 7340032 | tf_op jit(solution)/shard_map/all_to_all | solution.py:111
  394.3 3.7 fusion.2
  398.3 3.6 fusion.3
  404.4 44.3 %reduce-scatter.6.cloned.1.call-done = bf16[1,448,128]{2,1,0:T(8,128)(2,1)} async-done(((bf16[1,3584,128]{2,1,0:T(8,128)(2,1)}), bf16[1,448,128]{2,1,0:T(8,128)(2,1)}) %reduce-scatter.6.cloned.1.call-update) | async-done | bytes 114704 | tf_op jit(solution)/shard_map/reduce_scatter | solution.py:103
  450.3 42.4 %reduce-scatter.8.cloned.1.call-done = bf16[1,448,128]{2,1,0:T(8,128)(2,1)} async-done(((bf16[1,3584,128]{2,1,0:T(8,128)(2,1)}), bf16[1,448,128]{2,1,0:T(8,128)(2,1)}) %reduce-scatter.8.cloned.1.call-update) | async-done | bytes 114704 | tf_op jit(solution)/shard_map/reduce_scatter | solution.py:106
  494.3 2.8 convert_reduce_fusion
  (92 shorter events, 38.4 us)
Async XLA Ops:
  7.2 123.0 %copy-start = (bf16[128,3584]{1,0:T(8,128)(2,1)S(1)}, bf16[128,3584]{1,0:T(8,128)(2,1)}, u32[]{:S(2)}) copy-start(bf16[128,3584]{1,0:T(8,128)(2,1)} %param.7) | copy-start | bytes 2752516
  12.9 43.0 %all-to-all-start.4 = ((bf16[64,1,6]{2,1,0:T(2,128)(2,1)}), bf16[64,1,6]{2,1,0:T(2,128)(2,1)S(1)}, u32[]{:S(2)}, u32[]{:S(2)}) async-start(bf16[64,1,6]{2,1,0:T(2,128)(2,1)} %copy.119), calls=%async_computation.4 | async-start | bytes 65536 | tf_op jit(solution)/shard_map/all_to_all | solution.py:72
  28.2 35.2 %copy-start.7 = (bf16[1,3584,16]{1,2,0:T(8,128)(2,1)S(1)}, bf16[1,3584,16]{1,2,0:T(8,128)(2,1)}, u32[]{:S(2)}) copy-start(bf16[1,3584,16]{1,2,0:T(8,128)(2,1)} %param.12) | copy-start | bytes 344068
  55.9 33.4 %all-to-all-start = ((bf16[8,2,3584]{2,1,0:T(2,128)(2,1)}), bf16[8,2,3584]{2,1,0:T(2,128)(2,1)S(1)}, u32[]{:S(2)}, u32[]{:S(2)}) async-start(bf16[8,2,3584]{2,1,0:T(2,128)(2,1)} %reshape.176), calls=%async_computation | async-start | bytes 229376 | tf_op jit(solution)/shard_map/all_to_all | solution.py:57
  63.4 33.6 %copy-start.8 = (bf16[1,3584,16]{1,2,0:T(8,128)(2,1)S(1)}, bf16[1,3584,16]{1,2,0:T(8,128)(2,1)}, u32[]{:S(2)}) copy-start(bf16[1,3584,16]{1,2,0:T(8,128)(2,1)} %param.13) | copy-start | bytes 344068
  89.3 33.7 %all-to-all-start.1 = ((bf16[8,2,3584]{2,1,0:T(2,128)(2,1)}), bf16[8,2,3584]{2,1,0:T(2,128)(2,1)S(1)}, u32[]{:S(2)}, u32[]{:S(2)}) async-start(bf16[8,2,3584]{2,1,0:T(2,128)(2,1)} %reshape.178), calls=%async_computation.1 | async-start | bytes 229376 | tf_op jit(solution)/shard_map/all_to_all | solution.py:58
  122.9 15.7 %all-to-all-start.2 = ((bf16[8,2,3584]{2,1,0:T(2,128)(2,1)}), bf16[8,2,3584]{2,1,0:T(2,128)(2,1)S(1)}, u32[]{:S(2)}, u32[]{:S(2)}) async-start(bf16[8,2,3584]{2,1,0:T(2,128)(2,1)} %reshape.180), calls=%async_computation.2 | async-start | bytes 229376 | tf_op jit(solution)/shard_map/all_to_all | solution.py:59
  140.7 10.7 %copy-start.3 = (bf16[128,3584]{1,0:T(8,128)(2,1)S(1)}, bf16[128,3584]{1,0:T(8,128)(2,1)}, u32[]{:S(2)}) copy-start(bf16[128,3584]{1,0:T(8,128)(2,1)} %param.8) | copy-start | bytes 2752516
  140.7 93.8 %all-to-all-start.3 = ((bf16[64,6,3584]{2,1,0:T(8,128)(2,1)}), bf16[64,6,3584]{2,1,0:T(8,128)(2,1)}, u32[]{:S(2)}, u32[]{:S(2)}) async-start(bf16[64,6,3584]{2,1,0:T(8,128)(2,1)} %bitcast.86), calls=%async_computation.3 | async-start | bytes 7340032 | tf_op jit(solution)/shard_map/all_to_all | solution.py:70
  236.7 108.4 %all-to-all-start.5 = ((bf16[64,6,3584]{2,1,0:T(8,128)(2,1)}), bf16[64,6,3584]{2,1,0:T(8,128)(2,1)}, u32[]{:S(2)}, u32[]{:S(2)}) async-start(bf16[64,6,3584]{2,1,0:T(8,128)(2,1)} %bitcast.85), calls=%async_computation.5 | async-start | bytes 7340032 | tf_op jit(solution)/shard_map/all_to_all | solution.py:71
  245.3 157.5 %reduce-scatter.4.cloned.1.call-start = ((), (), s32[]{:S(2)}) async-start(), calls=%async_computation.11 | async-start | bytes 1032192 | tf_op jit(solution)/shard_map/reduce_scatter | solution.py:100
  249.1 52.7 %copy-start.4 = (bf16[1,448,128]{2,1,0:T(8,128)(2,1)}, bf16[1,448,128]{2,1,0:T(8,128)(2,1)S(1)}, u32[]{:S(2)}) copy-start(bf16[1,448,128]{2,1,0:T(8,128)(2,1)S(1)} %copy.125) | copy-start | bytes 344068
  252.7 49.1 %copy-start.5 = (bf16[1,448,128]{2,1,0:T(8,128)(2,1)}, bf16[1,448,128]{2,1,0:T(8,128)(2,1)S(1)}, u32[]{:S(2)}) copy-start(bf16[1,448,128]{2,1,0:T(8,128)(2,1)S(1)} %copy.126) | copy-start | bytes 344068
  256.3 85.0 %copy-start.6 = (bf16[1,448,128]{2,1,0:T(8,128)(2,1)}, bf16[1,448,128]{2,1,0:T(8,128)(2,1)S(1)}, u32[]{:S(2)}) copy-start(bf16[1,448,128]{2,1,0:T(8,128)(2,1)S(1)} %copy.127) | copy-start | bytes 344068
  341.2 2.9 copy-start.1
  350.6 3.1 copy-start.2
  359.6 23.7 %all-to-all-start.7 = ((bf16[64,1,6]{2,1,0:T(2,128)(2,1)}), bf16[64,1,6]{2,1,0:T(2,128)(2,1)S(1)}, u32[]{:S(2)}, u32[]{:S(2)}) async-start(bf16[64,1,6]{2,1,0:T(2,128)(2,1)} %convert_element_type.149), calls=%async_computation.10 | async-start | bytes 65536 | tf_op jit(solution)/shard_map/all_to_all | solution.py:118
  383.3 111.0 %all-to-all-start.6 = ((bf16[64,6,3584]{2,1,0:T(8,128)(2,1)}), bf16[64,6,3584]{2,1,0:T(8,128)(2,1)}, u32[]{:S(2)}, u32[]{:S(2)}) async-start(bf16[64,6,3584]{2,1,0:T(8,128)(2,1)} %reshape.159), calls=%async_computation.9 | async-start | bytes 7340032 | tf_op jit(solution)/shard_map/all_to_all | solution.py:111
  394.2 54.5 %reduce-scatter.6.cloned.1.call-start = ((), (), s32[]{:S(2)}) async-start(), calls=%async_computation.12 | async-start | bytes 1032192 | tf_op jit(solution)/shard_map/reduce_scatter | solution.py:103
  398.0 94.7 %reduce-scatter.8.cloned.1.call-start = ((), (), s32[]{:S(2)}) async-start(), calls=%async_computation.13 | async-start | bytes 1032192 | tf_op jit(solution)/shard_map/reduce_scatter | solution.py:106
Sparse Core Ops, SparseCore 0:
  359.0 43.1 reduce-scatter.3
  405.2 43.4 reduce-scatter.5
  451.5 41.1 reduce-scatter.7
where the time goes:
time: 514 us; the launch traced here: 506 us
  waiting for transfers between devices  178 us (35%)
  starting transfers between devices  81.5 us (16%)
  blocking collectives  79.4 us (15%)
  other arithmetic  72.6 us (14%)
  local copies, waits for them, and re-layouts  52.7 us (10%)
  matrix products  27.4 us (5%)
  between operations  14.4 us (3%)
    all_to_all x1, waiting for transfers between devices, shards(): lax.all_to_all(send_tok, 'expert', split_axis=0, concat_axis=0, tiled=True)  82.8 us
    unnamed x4, other arithmetic  61.9 us
    all_gather x1, blocking collectives, shards(): lax.all_gather(new_up, 'dp', axis=1, tiled=True)  45.5 us
    reduce_scatter x1, waiting for transfers between devices, shards(): lax.psum_scatter(grad_up_part[None].astype(jnp.bfloat16), 'dp', scatter_d...  44.3 us
    reduce_scatter x1, waiting for transfers between devices, shards(): lax.psum_scatter(grad_down_part[None].astype(jnp.bfloat16), 'dp', scatter...  42.4 us
    unnamed x32, local copies, waits for them, and re-layouts  23 us
    all_gather x1, blocking collectives, shards(): lax.all_gather(new_gate, 'dp', axis=1, tiled=True)  17 us
    all_gather x1, blocking collectives, shards(): lax.all_gather(new_down, 'dp', axis=1, tiled=True)  16.9 us
  transfers between devices with their start and end apart: 11, of which 4 were waited for; matrix products, arithmetic and copies ran while one was open for 24% of the time, Pallas kernels for 0%

commit v1 on v0

v1 whole, which is shorter than its diff:
```python
import jax
import jax.numpy as jnp
from jax import lax
from jax.sharding import Mesh
from jax.sharding import PartitionSpec as P

HSPLIT = 16
CAP = 6
PAD = 8
EXPERTS = 4
LANES = 128
DP = ("yh", "core")
COLOR_A = ("zl", "yl", "x")
BF = jnp.bfloat16
F32 = jnp.float32


def spread(block, axes):
    count = lax.axis_size(axes)
    copies = jnp.broadcast_to(block[None], (count,) + block.shape)
    got = lax.all_to_all(copies, axes, split_axis=0, concat_axis=0, tiled=True)
    return got.reshape((count * block.shape[0],) + block.shape[1:])


def dot(eq, a, b):
    return jnp.einsum(eq, a, b, preferred_element_type=F32)


def shards(tokens, cotangent, route_ids, gates, w_gate, w_up, w_down):
    tok_count, features = tokens.shape
    hidden_dev = w_gate.shape[2]

    mine = jnp.concatenate([w_gate[0].T, w_up[0].T, w_down[0].T], axis=0)
    gathered = lax.all_gather(mine, DP, axis=0, tiled=True)
    n_dp = lax.axis_size(DP)
    gathered = gathered.reshape(n_dp, 3, hidden_dev, features)

    ids = route_ids.T
    gates_t = gates.T.astype(F32)
    experts = jnp.arange(EXPERTS, dtype=jnp.int32)
    hits = ids[None] == experts[:, None, None]
    token_hit = jnp.any(hits, axis=1)
    before = (
        jnp.arange(tok_count)[:, None] < jnp.arange(tok_count)[None, :]
    ).astype(BF)
    rank = dot("et,tu->eu", token_hit.astype(BF), before)
    slots = jnp.arange(PAD, dtype=jnp.int32)
    pick = token_hit[:, None, :] & (rank.astype(jnp.int32)[:, None, :] == slots[None, :, None])
    gate_of = jnp.sum(jnp.where(hits, gates_t[None], 0.0), axis=1)
    gate_slots = jnp.sum(jnp.where(pick, gate_of[:, None, :], 0.0), axis=2)
    pick_rows = pick.reshape(EXPERTS * PAD, tok_count).astype(BF)
    tok_slots = dot("ct,td->cd", pick_rows, tokens).astype(BF)
    cot_slots = dot("ct,td->cd", pick_rows, cotangent).astype(BF)
    gate_cols = jnp.broadcast_to(gate_slots.astype(BF).reshape(-1, 1), (EXPERTS * PAD, LANES))
    rows = jnp.concatenate([tok_slots, gate_cols, cot_slots], axis=1)
    rows = rows.reshape(EXPERTS, PAD, -1)
    rows = lax.all_to_all(rows, "ex", split_axis=0, concat_axis=0, tiled=True)
    rows = rows.reshape(EXPERTS * PAD, -1)
    kept = jnp.arange(EXPERTS * CAP)
    keep = (
        (kept // CAP * PAD + kept % CAP)[:, None] == jnp.arange(EXPERTS * PAD)[None, :]
    ).astype(BF)
    wide = features + LANES
    tok_rows = dot("kc,cd->kd", keep, rows[:, :wide]).astype(BF)
    cot_rows = dot("kc,cd->kd", keep, rows[:, wide:]).astype(BF)

    tok_half = spread(tok_rows, "x")
    cot_half = spread(cot_rows, ("zl", "yl"))
    slot_all = spread(tok_half, ("zl", "yl"))
    slot_cotan = spread(cot_half, "x")
    slot_tokens = slot_all[:, :features]
    slot_gates = slot_all[:, features : features + 1].astype(F32)

    block = EXPERTS * CAP

    def to_tok_order(values):
        v = values.reshape(4, 4, block, values.shape[-1])
        return jnp.swapaxes(v, 0, 1).reshape(values.shape)

    slab = [gathered[:, j].reshape(n_dp * hidden_dev, features) for j in range(3)]
    gate_slab, up_slab, down_slab = slab
    pre_gate = dot("rd,hd->rh", slot_tokens, gate_slab)
    pre_up = dot("rd,hd->rh", slot_tokens, up_slab)
    sigmoid_gate = jax.nn.sigmoid(pre_gate)
    activation = pre_gate * sigmoid_gate
    hidden = (activation * pre_up).astype(BF)
    back_proj = to_tok_order(dot("rd,hd->rh", slot_cotan, down_slab))
    score = jnp.sum(hidden.astype(F32) * back_proj, axis=1, keepdims=True).astype(BF)
    scaled = slot_gates * back_proj
    d_gate = (scaled * pre_up * sigmoid_gate * (1.0 + pre_gate * (1.0 - sigmoid_gate))).astype(BF)
    d_up = (scaled * activation).astype(BF)
    hidden_gated = to_tok_order((slot_gates * hidden.astype(F32)).astype(BF))

    grads = jnp.stack(
        [
            dot("rd,rh->dh", slot_tokens, d_gate).astype(BF).reshape(n_dp, -1, LANES),
            dot("rd,rh->dh", slot_tokens, d_up).astype(BF).reshape(n_dp, -1, LANES),
            dot("rd,rh->dh", slot_cotan, hidden_gated).astype(BF).reshape(n_dp, -1, LANES),
        ],
        axis=1,
    )
    grads = lax.psum_scatter(grads, DP, scatter_dimension=0, tiled=True)[0].astype(F32)

    partial = (
        dot("rh,hd->rd", d_gate, gate_slab) + dot("rh,hd->rd", d_up, up_slab)
    ).astype(BF)
    back = jnp.concatenate([partial, jnp.broadcast_to(score, (score.shape[0], LANES))], axis=1)
    back = back.reshape(HSPLIT, block, -1)
    back = lax.all_to_all(back, COLOR_A, split_axis=0, concat_axis=0, tiled=True)
    back = back.reshape(HSPLIT * block, -1)
    fold = jnp.tile(keep.T, (1, HSPLIT))
    summed = dot("ck,kd->cd", fold, back)
    score_sum = summed[:, features:]
    high = lax.reduce_precision(score_sum, 8, 7)
    lane = jnp.arange(LANES)[None, :]
    score_cols = jnp.where(lane < LANES // 2, high, score_sum - high)
    home = jnp.concatenate([summed[:, :features], score_cols], axis=1).astype(BF)
    home = lax.all_to_all(
        home.reshape(EXPERTS, PAD, -1), "ex", split_axis=0, concat_axis=0, tiled=True
    ).reshape(EXPERTS * PAD, -1)
    token_grad = dot("ct,cd->td", pick_rows, home[:, :features]).astype(BF)
    pair = home[:, features:].astype(F32)
    score_slots = (pair[:, :1] + pair[:, LANES // 2 : LANES // 2 + 1]).reshape(EXPERTS, PAD, 1)
    score_token = jnp.sum(jnp.where(pick, score_slots, 0.0), axis=1)
    gate_grad = jnp.sum(jnp.where(hits, score_token[:, None, :], 0.0), axis=0).T

    start = lax.axis_index(DP) * (features // n_dp)
    relaid = [
        lax.dynamic_slice_in_dim(w, start, features // n_dp, axis=1).T[None] for w in slab
    ]
    return (*relaid, grads[0:1], grads[1:2], grads[2:3], token_grad, gate_grad)


def solution(mesh):
    fine = Mesh(
        mesh.devices.reshape(4, 2, 4, 2, 4, 2), ("yh", "core", "ex", "zl", "x", "yl")
    )
    expert = ("ex", "zl", "x", "yl")
    rows = P(DP + expert, None)
    weights = P(expert, None, DP)
    laid = P(expert, DP, None)
    return jax.shard_map(
        shards,
        mesh=fine,
        in_specs=(rows,) * 4 + (weights,) * 3,
        out_specs=(laid,) * 6 + (rows,) * 2,
        check_vma=False,
    )
```

time: 514 us -> 240 us (0.47)
  blocking collectives: 79.4 us -> 16.1 us
  other arithmetic: 72.6 us -> 11.3 us
  waiting for transfers between devices: 178 us -> 119 us
  starting transfers between devices: 81.5 us -> 39.2 us
  local copies, waits for them, and re-layouts: 52.7 us -> 12.2 us
    all_gather x3 -> x0, blocking collectives: 79.4 us -> none  [the longest x1 45.5 us: shards(): lax.all_gather(new_up, 'dp', axis=1, tiled=True)]
    reduce_scatter x3 -> x1, waiting for transfers between devices: 86.7 us -> 9.74 us  [shards(): lax.psum_scatter(grads, DP, scatter_dimension=0, tiled=True)[0].astype(F32)]
    unnamed x4 -> x0, other arithmetic: 61.9 us -> none
    all_to_all x8 -> x6, starting transfers between devices: 81.2 us -> 39.1 us  [the longest x3 13.4 us: spread(): got = lax.all_to_all(copies, axes, split_axis=0, concat_axis=0, tiled=True)]
    unnamed x32 -> x15, local copies, waits for them, and re-layouts: 23 us -> 2.33 us
    all_gather x0 -> x1, waiting for transfers between devices: none -> 17.7 us  [shards(): gathered = lax.all_gather(mine, DP, axis=0, tiled=True)]
    reshape x7 -> x1, local copies, waits for them, and re-layouts: 16.7 us -> 0.01 us  [to_tok_order(): v = values.reshape(4, 4, block, values.shape[-1])]
    all_to_all x0 -> x1, blocking collectives: none -> 16.1 us  [spread(): got = lax.all_to_all(copies, axes, split_axis=0, concat_axis=0, tiled=True)]
  transfers between devices with their start and end apart: 11 -> 8, of which waited for: 4 -> 7; matrix products, arithmetic and copies ran while one was open for 24% -> 11% of each run, Pallas kernels for 0% -> 0%
where the time goes in v1:
time: 240 us; the launch traced here: 236 us
  waiting for transfers between devices  119 us (50%)
  starting transfers between devices  39.2 us (16%)
  matrix products  24.4 us (10%)
  blocking collectives  16.1 us (7%)
  between operations  14.3 us (6%)
  local copies, waits for them, and re-layouts  12.2 us (5%)
  other arithmetic  11.3 us (5%)
    all_to_all x3, waiting for transfers between devices, spread(): got = lax.all_to_all(copies, axes, split_axis=0, concat_axis=0, tiled=True)  53.1 us
    all_to_all x1, waiting for transfers between devices, shards(): lax.all_to_all(back, COLOR_A, split_axis=0, concat_axis=0, tiled=True)  27.7 us
    dot_general x15, matrix products, dot(): return jnp.einsum(eq, a, b, preferred_element_type=F32)  24.4 us
    all_gather x1, waiting for transfers between devices, shards(): gathered = lax.all_gather(mine, DP, axis=0, tiled=True)  17.7 us
    all_to_all x1, blocking collectives, spread(): got = lax.all_to_all(copies, axes, split_axis=0, concat_axis=0, tiled=True)  16.1 us
    all_to_all x3, starting transfers between devices, spread(): got = lax.all_to_all(copies, axes, split_axis=0, concat_axis=0, tiled=True)  13.4 us
    all_to_all x1, starting transfers between devices, shards(): rows = lax.all_to_all(rows, 'ex', split_axis=0, concat_axis=0, tiled=True)  10.8 us
    all_to_all x1, waiting for transfers between devices, shards(): rows = lax.all_to_all(rows, 'ex', split_axis=0, concat_axis=0, tiled=True)  10.8 us
  transfers between devices with their start and end apart: 8, of which 7 were waited for; matrix products, arithmetic and copies ran while one was open for 11% of the time, Pallas kernels for 0%

profile of v1, /device:TPU:1, one launch (start us, length us, event | category | flops | bytes accessed | tf_op | source)
XLA Modules:
  0.0 236.5 jit_solution(4835335759364838620)
XLA Ops:
  10.0 1.5 convolution_convert_fusion.5
  12.4 10.8 %all-to-all-start = ((bf16[4,8,7296]{2,1,0:T(8,128)(2,1)}), bf16[4,8,7296]{2,1,0:T(8,128)(2,1)S(1)}, u32[]{:S(2)}, u32[]{:S(2)}) async-start(bf16[4,8,7296]{2,1,0:T(8,128)(2,1)} %maximum_bitcast_fusion), calls=%async_computation | async-start | bytes 933888 | tf_op jit(solution)/shard_map/all_to_all | solution.py:57
  23.3 10.8 %all-to-all-done = bf16[4,8,7296]{2,1,0:T(8,128)(2,1)S(1)} async-done(((bf16[4,8,7296]{2,1,0:T(8,128)(2,1)}), bf16[4,8,7296]{2,1,0:T(8,128)(2,1)S(1)}, u32[]{:S(2)}, u32[]{:S(2)}) %all-to-all-start) | async-done | bytes 466976 | tf_op jit(solution)/shard_map/all_to_all | solution.py:57
  34.4 0.9 broadcast_in_dim.114
  35.3 4.0 %all-to-all-start.1 = ((bf16[4,24,3712]{2,1,0:T(8,128)(2,1)}), bf16[4,24,3712]{2,1,0:T(8,128)(2,1)S(1)}, u32[]{:S(2)}, u32[]{:S(2)}) async-start(bf16[4,24,3712]{2,1,0:T(8,128)(2,1)} %broadcast_in_dim.114), calls=%async_computation.1 | async-start | bytes 1425408 | tf_op jit(solution)/shard_map/all_to_all | solution.py:21
  39.5 7.7 %all-to-all-done.1 = bf16[4,24,3712]{2,1,0:T(8,128)(2,1)S(1)} async-done(((bf16[4,24,3712]{2,1,0:T(8,128)(2,1)}), bf16[4,24,3712]{2,1,0:T(8,128)(2,1)S(1)}, u32[]{:S(2)}, u32[]{:S(2)}) %all-to-all-start.1) | async-done | bytes 712736 | tf_op jit(solution)/shard_map/all_to_all | solution.py:21
  47.3 16.1 %all_to_all.35 = bf16[4,24,3584]{2,1,0:T(8,128)(2,1)S(1)} all-to-all(bf16[4,24,3584]{2,1,0:T(8,128)(2,1)S(1)} %broadcast_in_dim.117), channel_id=1, replica_groups=mesh['yh'=4,'core'=2,'ex'=4,'zl'=2,'x'=4,'yl'=2] {'zl','yl'}, dimensions={0} | all-to-all | bytes 1376256 | tf_op jit(solution)/shard_map/all_to_all | solution.py:21
  63.4 1.8 broadcast_in_dim.119
  65.1 4.7 %all-to-all-start.4 = ((bf16[4,96,3584]{2,1,0:T(8,128)(2,1)}), bf16[4,96,3584]{2,1,0:T(8,128)(2,1)}, u32[]{:S(2)}, u32[]{:S(2)}) async-start(bf16[4,96,3584]{2,1,0:T(8,128)(2,1)} %broadcast_in_dim.119), calls=%async_computation.4 | async-start | bytes 5505024 | tf_op jit(solution)/shard_map/all_to_all | solution.py:21
  70.8 28.2 %all-to-all-done.4 = bf16[4,96,3584]{2,1,0:T(8,128)(2,1)} async-done(((bf16[4,96,3584]{2,1,0:T(8,128)(2,1)}), bf16[4,96,3584]{2,1,0:T(8,128)(2,1)}, u32[]{:S(2)}, u32[]{:S(2)}) %all-to-all-start.4) | async-done | bytes 2752544 | tf_op jit(solution)/shard_map/all_to_all | solution.py:21
  99.0 1.8 broadcast_in_dim.116
  100.7 4.6 %all-to-all-start.2 = ((bf16[4,96,3712]{2,1,0:T(8,128)(2,1)}), bf16[4,96,3712]{2,1,0:T(8,128)(2,1)}, u32[]{:S(2)}, u32[]{:S(2)}) async-start(bf16[4,96,3712]{2,1,0:T(8,128)(2,1)} %broadcast_in_dim.116), calls=%async_computation.2 | async-start | bytes 5701632 | tf_op jit(solution)/shard_map/all_to_all | solution.py:21
  105.4 17.7 %all-gather.2.cloned.1.call-done = bf16[384,3584]{1,0:T(8,128)(2,1)} async-done(((bf16[48,3584]{1,0:T(8,128)(2,1)}), bf16[384,3584]{1,0:T(8,128)(2,1)}) %all-gather.2.cloned.1.call-update) | async-done | bytes 2752528 | tf_op jit(solution)/shard_map/all_gather | solution.py:34
  123.0 2.9 %fusion.54 = (bf16[8,1,16,3584]{3,2,1,0:T(8,128)(2,1)S(1)}, bf16[8,1,16,3584]{3,2,1,0:T(8,128)(2,1)S(1)}, bf16[8,1,16,3584]{3,2,1,0:T(8,128)(2,1)}) fusion(bf16[8,3,16,3584]{3,2,1,0:T(8,128)(2,1)} %bitcast.116), kind=kLoop, calls=%fused_computation.100 | loop fusion | bytes 5505024 | tf_op jit(solution)/shard_map/slice | solution.py:80
  125.9 2.6 %convolution_bitcast_fusion.1 = f32[4,4,24,128]{3,2,0,1:T(8,128)S(1)} fusion(bf16[4,4,24,3584]{3,2,1,0:T(8,128)(2,1)} %bitcast.25, bf16[128,3584,1,1]{1,0,3,2:T(8,128)(2,1)S(1)} %bitcast.110), kind=kOutput, calls=%fused_computation.21 | convolution fusion | flops 352321536 | bytes 3866624 | tf_op jit(solution)/shard_map/rd,hd->rh/dot_general | solution.py:26
  128.6 17.1 %all-to-all-done.2 = bf16[4,96,3712]{2,1,0:T(8,128)(2,1)} async-done(((bf16[4,96,3712]{2,1,0:T(8,128)(2,1)}), bf16[4,96,3712]{2,1,0:T(8,128)(2,1)}, u32[]{:S(2)}, u32[]{:S(2)}) %all-to-all-start.2) | async-done | bytes 2850848 | tf_op jit(solution)/shard_map/all_to_all | solution.py:21
  145.7 1.0 convert_reduce_fusion
  146.7 2.9 %fusion.5 = f32[384,128]{1,0:T(8,128)S(1)} fusion(bf16[128,3584]{1,0:T(8,128)(2,1)} %bitcast.112, bf16[384,3712]{1,0:T(8,128)(2,1)} %bitcast.23), kind=kOutput, calls=%fused_computation.17 | convolution fusion | flops 352321536 | bytes 3866624 | tf_op jit(solution)/shard_map/rd,hd->rh/dot_general | solution.py:26
  149.6 2.8 %fusion.16 = (bf16[384]{0:T(512)(128)(2,1)S(1)}, bf16[384,128]{1,0:T(8,128)(2,1)S(1)}, bf16[384,128]{1,0:T(8,128)(2,1)S(1)}, bf16[384,128]{1,0:T(8,128)(2,1)S(1)}) fusion(f32[4,4,24,128]{3,2,1,0:T(8,128)S(1)} %copy.40, f32[384,128]{1,0:T(8,128)S(1)} %fusion.5, f32[384]{0:T(512)S(1)} %convert_reduce_fusion, bf16[128,3584]{1,0:T(8,128)(2,1)S(1)} %bitcast.107, ...), kind=kOutput, calls=%fused_computation.39 | convolution fusion | flops 353255040 | bytes 4360448 | tf_op jit(solution)/shard_map/rd,hd->rh/dot_general | solution.py:26
  154.3 1.8 pad_maximum_fusion
  156.1 6.2 %all-to-all-start.5 = ((bf16[16,24,3712]{2,1,0:T(8,128)(2,1)}), bf16[16,24,3712]{2,1,0:T(8,128)(2,1)}, u32[]{:S(2)}, u32[]{:S(2)}) async-start(bf16[16,24,3712]{2,1,0:T(8,128)(2,1)} %bitcast.105), calls=%async_computation.6 | async-start | bytes 5701632 | tf_op jit(solution)/shard_map/all_to_all | solution.py:109
  162.5 2.7 %convolution_convert_fusion.2 = bf16[3584,128]{1,0:T(8,128)(2,1)S(1)} fusion(bf16[384,128]{1,0:T(8,128)(2,1)S(1)} %get-tuple-element.49, bf16[384,3712]{1,0:T(8,128)(2,1)} %bitcast.23), kind=kOutput, calls=%fused_computation.6 | convolution fusion | flops 352780288 | bytes 3768320 | tf_op jit(solution)/shard_map/rd,rh->dh/dot_general | solution.py:26
  165.2 2.7 %convolution_convert_fusion.3 = bf16[3584,128]{1,0:T(8,128)(2,1)S(1)} fusion(bf16[384,128]{1,0:T(8,128)(2,1)S(1)} %get-tuple-element.48, bf16[384,3712]{1,0:T(8,128)(2,1)} %bitcast.23), kind=kOutput, calls=%fused_computation.7 | convolution fusion | flops 352780288 | bytes 3768320 | tf_op jit(solution)/shard_map/rd,rh->dh/dot_general | solution.py:26
  167.9 2.7 %convolution_convert_fusion.1 = bf16[3584,128]{1,0:T(8,128)(2,1)S(1)} fusion(bf16[384,3584]{1,0:T(8,128)(2,1)} %bitcast.34, bf16[384,128]{1,0:T(8,128)(2,1)S(1)} %bitcast.125), kind=kOutput, calls=%fused_computation.5 | convolution fusion | flops 352780288 | bytes 3768320 | tf_op jit(solution)/shard_map/rd,rh->dh/dot_general | solution.py:26
  170.6 1.8 pad_maximum_fusion.1
  172.6 1.0 dynamic-slice_bitcast_fusion.2
  174.4 27.7 %all-to-all-done.5 = bf16[16,24,3712]{2,1,0:T(8,128)(2,1)} async-done(((bf16[16,24,3712]{2,1,0:T(8,128)(2,1)}), bf16[16,24,3712]{2,1,0:T(8,128)(2,1)}, u32[]{:S(2)}, u32[]{:S(2)}) %all-to-all-start.5) | async-done | bytes 2850848 | tf_op jit(solution)/shard_map/all_to_all | solution.py:109
  202.0 2.4 %convolution_bitcast_fusion = f32[32,3712]{1,0:T(8,128)S(1)} fusion(bf16[16,24,3712]{2,1,0:T(8,128)(2,1)} %all-to-all-done.5, bf16[32,24]{0,1:T(8,128)(2,1)S(1)} %fusion.30), kind=kOutput, calls=%fused_computation.8 | convolution fusion | flops 91226112 | bytes 3327488 | tf_op jit(solution)/shard_map/ck,kd->cd/dot_general | solution.py:26
  205.2 8.7 %all-to-all-start.6 = ((bf16[4,8,3712]{2,1,0:T(8,128)(2,1)}), bf16[4,8,3712]{2,1,0:T(8,128)(2,1)S(1)}, u32[]{:S(2)}, u32[]{:S(2)}) async-start(bf16[4,8,3712]{2,1,0:T(8,128)(2,1)} %pad_maximum_fusion.3), calls=%async_computation.7 | async-start | bytes 475136 | tf_op jit(solution)/shard_map/all_to_all | solution.py:118
  215.6 9.7 %reduce-scatter.2.cloned.1.call-done = bf16[1,3,448,128]{3,2,1,0:T(8,128)(2,1)} async-done(((bf16[8,3,448,128]{3,2,1,0:T(8,128)(2,1)}), bf16[1,3,448,128]{3,2,1,0:T(8,128)(2,1)}) %reduce-scatter.2.cloned.1.call-update) | async-done | bytes 344080 | tf_op jit(solution)/shard_map/reduce_scatter | solution.py:102
  225.4 1.0 convert_element_type.108
  227.2 1.4 convolution_convert_fusion
  (52 shorter events, 12.2 us)
Async XLA Ops:
  7.2 2.6 %copy-start = (bf16[128,3584]{1,0:T(8,128)(2,1)S(1)}, bf16[128,3584]{1,0:T(8,128)(2,1)}, u32[]{:S(2)}) copy-start(bf16[128,3584]{1,0:T(8,128)(2,1)} %param.8) | copy-start | bytes 2752516
  12.4 21.7 %all-to-all-start = ((bf16[4,8,7296]{2,1,0:T(8,128)(2,1)}), bf16[4,8,7296]{2,1,0:T(8,128)(2,1)S(1)}, u32[]{:S(2)}, u32[]{:S(2)}) async-start(bf16[4,8,7296]{2,1,0:T(8,128)(2,1)} %maximum_bitcast_fusion), calls=%async_computation | async-start | bytes 933888 | tf_op jit(solution)/shard_map/all_to_all | solution.py:57
  35.3 12.0 %all-to-all-start.1 = ((bf16[4,24,3712]{2,1,0:T(8,128)(2,1)}), bf16[4,24,3712]{2,1,0:T(8,128)(2,1)S(1)}, u32[]{:S(2)}, u32[]{:S(2)}) async-start(bf16[4,24,3712]{2,1,0:T(8,128)(2,1)} %broadcast_in_dim.114), calls=%async_computation.1 | async-start | bytes 1425408 | tf_op jit(solution)/shard_map/all_to_all | solution.py:21
  65.1 4.8 %copy-start.2 = (bf16[1,3584,16]{1,2,0:T(8,128)(2,1)S(1)}, bf16[1,3584,16]{1,2,0:T(8,128)(2,1)}, u32[]{:S(2)}) copy-start(bf16[1,3584,16]{1,2,0:T(8,128)(2,1)} %param.13) | copy-start | bytes 344068
  65.1 4.8 %copy-start.3 = (bf16[1,3584,16]{1,2,0:T(8,128)(2,1)S(1)}, bf16[1,3584,16]{1,2,0:T(8,128)(2,1)}, u32[]{:S(2)}) copy-start(bf16[1,3584,16]{1,2,0:T(8,128)(2,1)} %param.12) | copy-start | bytes 344068
  65.1 4.8 %copy-start.4 = (bf16[1,3584,16]{1,2,0:T(8,128)(2,1)S(1)}, bf16[1,3584,16]{1,2,0:T(8,128)(2,1)}, u32[]{:S(2)}) copy-start(bf16[1,3584,16]{1,2,0:T(8,128)(2,1)} %param.11) | copy-start | bytes 344068
  65.1 33.8 %all-to-all-start.4 = ((bf16[4,96,3584]{2,1,0:T(8,128)(2,1)}), bf16[4,96,3584]{2,1,0:T(8,128)(2,1)}, u32[]{:S(2)}, u32[]{:S(2)}) async-start(bf16[4,96,3584]{2,1,0:T(8,128)(2,1)} %broadcast_in_dim.119), calls=%async_computation.4 | async-start | bytes 5505024 | tf_op jit(solution)/shard_map/all_to_all | solution.py:21
  69.9 53.2 %all-gather.2.cloned.1.call-start = ((), (), s32[]{:S(2)}) async-start(), calls=%async_computation.8 | async-start | bytes 3096576 | tf_op jit(solution)/shard_map/all_gather | solution.py:34
  100.7 45.0 %all-to-all-start.2 = ((bf16[4,96,3712]{2,1,0:T(8,128)(2,1)}), bf16[4,96,3712]{2,1,0:T(8,128)(2,1)}, u32[]{:S(2)}, u32[]{:S(2)}) async-start(bf16[4,96,3712]{2,1,0:T(8,128)(2,1)} %broadcast_in_dim.116), calls=%async_computation.2 | async-start | bytes 5701632 | tf_op jit(solution)/shard_map/all_to_all | solution.py:21
  149.6 2.8 %copy-start.1 = (bf16[8,1,16,3584]{3,2,1,0:T(8,128)(2,1)S(1)}, bf16[8,1,16,3584]{3,2,1,0:T(8,128)(2,1)}, u32[]{:S(2)}) copy-start(bf16[8,1,16,3584]{3,2,1,0:T(8,128)(2,1)} %get-tuple-element.44) | copy-start | bytes 2752516
  156.1 45.9 %all-to-all-start.5 = ((bf16[16,24,3712]{2,1,0:T(8,128)(2,1)}), bf16[16,24,3712]{2,1,0:T(8,128)(2,1)}, u32[]{:S(2)}, u32[]{:S(2)}) async-start(bf16[16,24,3712]{2,1,0:T(8,128)(2,1)} %bitcast.105), calls=%async_computation.6 | async-start | bytes 5701632 | tf_op jit(solution)/shard_map/all_to_all | solution.py:109
  162.3 63.0 %reduce-scatter.2.cloned.1.call-start = ((), (), s32[]{:S(2)}) async-start(), calls=%async_computation.9 | async-start | bytes 3096576 | tf_op jit(solution)/shard_map/reduce_scatter | solution.py:102
  204.5 24.5 %copy-start.5 = (s32[128,8]{0,1:T(8,128)S(1)}, s32[128,8]{0,1:T(8,128)}, u32[]{:S(2)}) copy-start(s32[128,8]{0,1:T(8,128)} %param.9) | copy-start | bytes 12292
  205.2 22.0 %all-to-all-start.6 = ((bf16[4,8,3712]{2,1,0:T(8,128)(2,1)}), bf16[4,8,3712]{2,1,0:T(8,128)(2,1)S(1)}, u32[]{:S(2)}, u32[]{:S(2)}) async-start(bf16[4,8,3712]{2,1,0:T(8,128)(2,1)} %pad_maximum_fusion.3), calls=%async_computation.7 | async-start | bytes 475136 | tf_op jit(solution)/shard_map/all_to_all | solution.py:118
Sparse Core Ops, SparseCore 0:
  73.4 49.5 all-gather.1
  172.6 52.7 reduce-scatter.1

commit v2 on v1

--- a/solution.py
+++ b/solution.py
@@ -20,6 +20,40 @@
     copies = jnp.broadcast_to(block[None], (count,) + block.shape)
     got = lax.all_to_all(copies, axes, split_axis=0, concat_axis=0, tiled=True)
     return got.reshape((count * block.shape[0],) + block.shape[1:])
+
+
+def put(total, block, at):
+    return lax.dynamic_update_slice_in_dim(total, block[None], at, axis=0)
+
+
+def spread_square(block):
+    z, y = lax.axis_index("zl"), lax.axis_index("yl")
+    me = 2 * z + y
+    total = put(jnp.zeros((4,) + block.shape, block.dtype), block, me)
+    for off in (1, 2, 3):
+        got = lax.ppermute(block, ("zl", "yl"), [(i, i ^ off) for i in range(4)])
+        total = put(total, got, me ^ off)
+    return total.reshape((4 * block.shape[0],) + block.shape[1:])
+
+
+RIGHT = [(i, (i + 1) % 4) for i in range(4)]
+LEFT = [(i, (i + 3) % 4) for i in range(4)]
+
+
+def spread_ring(block):
+    me = lax.axis_index("x")
+    half = block.shape[0] // 2
+    from_left = lax.ppermute(block, "x", RIGHT)
+    from_right = lax.ppermute(block, "x", LEFT)
+    far_top = lax.ppermute(from_left[:half], "x", RIGHT)
+    far_low = lax.ppermute(from_right[half:], "x", LEFT)
+    total = put(jnp.zeros((4,) + block.shape, block.dtype), block, me)
+    total = put(total, from_left, (me + 3) % 4)
+    total = put(total, from_right, (me + 1) % 4)
+    far = (me + 2) % 4
+    total = lax.dynamic_update_slice(total, far_top[None], (far, 0, 0))
+    total = lax.dynamic_update_slice(total, far_low[None], (far, half, 0))
+    return total.reshape((4 * block.shape[0],) + block.shape[1:])
 
 
 def dot(eq, a, b):
@@ -65,9 +99,10 @@
     cot_rows = dot("kc,cd->kd", keep, rows[:, wide:]).astype(BF)
 
     tok_half = spread(tok_rows, "x")
-    cot_half = spread(cot_rows, ("zl", "yl"))
+    cot_half = spread_square(cot_rows)
+    tok_half, cot_half, gathered = lax.optimization_barrier((tok_half, cot_half, gathered))
     slot_all = spread(tok_half, ("zl", "yl"))
-    slot_cotan = spread(cot_half, "x")
+    slot_cotan = spread_ring(cot_half)
     slot_tokens = slot_all[:, :features]
     slot_gates = slot_all[:, features : features + 1].astype(F32)
 

time: 240 us -> 206 us (0.86)
  waiting for transfers between devices: 119 us -> 75.1 us
  starting transfers between devices: 39.2 us -> 59.7 us
  blocking collectives: 16.1 us -> 0 us
  local copies, waits for them, and re-layouts: 12.2 us -> 20.7 us
  matrix products: 24.4 us -> 21.7 us
    all_to_all x3 -> x2, waiting for transfers between devices: 53.1 us -> 12.4 us  [spread(): got = lax.all_to_all(copies, axes, split_axis=0, concat_axis=0, tiled=True)]
    ppermute x0 -> x7, starting transfers between devices: none -> 25.4 us  [the longest x3 12.4 us: spread_square(): got = lax.ppermute(block, ('zl', 'yl'), [(i, i ^ off) for i in range(4)])]
    all_gather x1, waiting for transfers between devices: 17.7 us -> 0.63 us  [shards(): gathered = lax.all_gather(mine, DP, axis=0, tiled=True)]
    all_to_all x1 -> x0, blocking collectives: 16.1 us -> none  [spread(): got = lax.all_to_all(copies, axes, split_axis=0, concat_axis=0, tiled=True)]
    ppermute x0 -> x7, waiting for transfers between devices: none -> 13.7 us  [the longest x3 8.46 us: spread_square(): got = lax.ppermute(block, ('zl', 'yl'), [(i, i ^ off) for i in range(4)])]
    dynamic_update_slice x0 -> x8, local copies, waits for them, and re-layouts: none -> 5.54 us  [the longest x6 5.49 us: put(): return lax.dynamic_update_slice_in_dim(total, block[None], at, axis=0)]
    all_to_all x3 -> x2, starting transfers between devices: 13.4 us -> 8.61 us  [spread(): got = lax.all_to_all(copies, axes, split_axis=0, concat_axis=0, tiled=True)]
    dot_general x15, matrix products: 24.4 us -> 21.7 us  [dot(): return jnp.einsum(eq, a, b, preferred_element_type=F32)]
  transfers between devices with their start and end apart: 8 -> 14, of which waited for: 7 -> 10; matrix products, arithmetic and copies ran while one was open for 11% -> 19% of each run, Pallas kernels for 0% -> 0%
where the time goes in v2:
time: 206 us; the launch traced here: 203 us
  waiting for transfers between devices  75.1 us (36%)
  starting transfers between devices  59.7 us (29%)
  matrix products  21.7 us (11%)
  local copies, waits for them, and re-layouts  20.7 us (10%)
  between operations  14.4 us (7%)
  other arithmetic  11.6 us (6%)
    all_to_all x1, waiting for transfers between devices, shards(): lax.all_to_all(back, COLOR_A, split_axis=0, concat_axis=0, tiled=True)  30.3 us
    dot_general x15, matrix products, dot(): return jnp.einsum(eq, a, b, preferred_element_type=F32)  21.7 us
    all_to_all x2, waiting for transfers between devices, spread(): got = lax.all_to_all(copies, axes, split_axis=0, concat_axis=0, tiled=True)  12.4 us
    ppermute x3, starting transfers between devices, spread_square(): got = lax.ppermute(block, ('zl', 'yl'), [(i, i ^ off) for i in range(4)])  12.4 us
    all_to_all x1, starting transfers between devices, shards(): rows = lax.all_to_all(rows, 'ex', split_axis=0, concat_axis=0, tiled=True)  10.8 us
    all_to_all x1, waiting for transfers between devices, shards(): rows = lax.all_to_all(rows, 'ex', split_axis=0, concat_axis=0, tiled=True)  10.8 us
    all_to_all x1, starting transfers between devices, shards(): lax.all_to_all(home.reshape(EXPERTS, PAD, -1), 'ex', split_axis=0, concat...  10.3 us
    all_to_all x2, starting transfers between devices, spread(): got = lax.all_to_all(copies, axes, split_axis=0, concat_axis=0, tiled=True)  8.61 us
  transfers between devices with their start and end apart: 14, of which 10 were waited for; matrix products, arithmetic and copies ran while one was open for 19% of the time, Pallas kernels for 0%

profile of v2, /device:TPU:1, one launch (start us, length us, event | category | flops | bytes accessed | tf_op | source)
XLA Modules:
  0.0 203.1 jit_solution(14008031448016485435)
XLA Ops:
  7.2 1.9 pad_maximum_fusion.2
  11.0 1.5 convolution_convert_fusion.5
  13.6 10.8 %all-to-all-start = ((bf16[4,8,7296]{2,1,0:T(8,128)(2,1)}), bf16[4,8,7296]{2,1,0:T(8,128)(2,1)S(1)}, u32[]{:S(2)}, u32[]{:S(2)}) async-start(bf16[4,8,7296]{2,1,0:T(8,128)(2,1)} %maximum_bitcast_fusion), calls=%async_computation | async-start | bytes 933888 | tf_op jit(solution)/shard_map/all_to_all | solution.py:91
  24.5 10.8 %all-to-all-done = bf16[4,8,7296]{2,1,0:T(8,128)(2,1)S(1)} async-done(((bf16[4,8,7296]{2,1,0:T(8,128)(2,1)}), bf16[4,8,7296]{2,1,0:T(8,128)(2,1)S(1)}, u32[]{:S(2)}, u32[]{:S(2)}) %all-to-all-start) | async-done | bytes 466976 | tf_op jit(solution)/shard_map/all_to_all | solution.py:91
  37.1 3.2 %collective-permute-start = (bf16[24,3584]{1,0:T(8,128)(2,1)S(1)}, bf16[24,3584]{1,0:T(8,128)(2,1)S(1)}, u32[]{:S(2)}, u32[]{:S(2)}) collective-permute-start(bf16[24,3584]{1,0:T(8,128)(2,1)S(1)} %get-tuple-element.57), channel_id=1, source_target_pairs={{0,1},{1,0},{8,9},{9,8},{2,3},{3,2},{10,11},{11,10},{4,5},{5,4},{1... | collective-permute-start | bytes 516104 | tf_op jit(solution)/shard_map/ppermute | solution.py:34
  40.3 7.3 %collective-permute-start.1 = (bf16[24,3584]{1,0:T(8,128)(2,1)S(1)}, bf16[24,3584]{1,0:T(8,128)(2,1)S(1)}, u32[]{:S(2)}, u32[]{:S(2)}) collective-permute-start(bf16[24,3584]{1,0:T(8,128)(2,1)S(1)} %get-tuple-element.57), channel_id=1, source_target_pairs={{0,8},{1,9},{8,0},{9,1},{2,10},{3,11},{10,2},{11,3},{4,12},{5,13},... | collective-permute-start | bytes 516104 | tf_op jit(solution)/shard_map/ppermute | solution.py:34
  47.6 1.9 collective-permute-start.2
  50.7 4.0 %all-to-all-start.1 = ((bf16[4,24,3712]{2,1,0:T(8,128)(2,1)}), bf16[4,24,3712]{2,1,0:T(8,128)(2,1)S(1)}, u32[]{:S(2)}, u32[]{:S(2)}) async-start(bf16[4,24,3712]{2,1,0:T(8,128)(2,1)} %broadcast_in_dim.130), calls=%async_computation.1 | async-start | bytes 1425408 | tf_op jit(solution)/shard_map/all_to_all | solution.py:21
  56.6 7.9 %collective-permute-done.2 = bf16[24,3584]{1,0:T(8,128)(2,1)S(1)} collective-permute-done((bf16[24,3584]{1,0:T(8,128)(2,1)S(1)}, bf16[24,3584]{1,0:T(8,128)(2,1)S(1)}, u32[]{:S(2)}, u32[]{:S(2)}) %collective-permute-start.2) | collective-permute-done | bytes 172064 | tf_op jit(solution)/shard_map/ppermute | solution.py:34
  65.8 2.8 %collective-permute-start.3 = (bf16[96,3584]{1,0:T(8,128)(2,1)}, bf16[96,3584]{1,0:T(8,128)(2,1)}, u32[]{:S(2)}, u32[]{:S(2)}) collective-permute-start(bf16[96,3584]{1,0:T(8,128)(2,1)} %bitcast.11), channel_id=1, source_target_pairs={{0,2},{2,4},{4,6},{6,0},{1,3},{3,5},{5,7},{7,1},{8,10},{10,12},{12... | collective-permute-start | bytes 2064392 | tf_op jit(solution)/shard_map/ppermute | solution.py:46
  68.6 3.7 %collective-permute-start.4 = (bf16[96,3584]{1,0:T(8,128)(2,1)}, bf16[96,3584]{1,0:T(8,128)(2,1)}, u32[]{:S(2)}, u32[]{:S(2)}) collective-permute-start(bf16[96,3584]{1,0:T(8,128)(2,1)} %bitcast.11), channel_id=1, source_target_pairs={{0,6},{2,0},{4,2},{6,4},{1,7},{3,1},{5,3},{7,5},{8,14},{10,8},{12,... | collective-permute-start | bytes 2064392 | tf_op jit(solution)/shard_map/ppermute | solution.py:47
  72.3 2.9 %fusion.54 = (bf16[8,1,16,3584]{3,2,1,0:T(8,128)(2,1)S(1)}, bf16[8,1,16,3584]{3,2,1,0:T(8,128)(2,1)S(1)}, bf16[8,1,16,3584]{3,2,1,0:T(8,128)(2,1)}) fusion(bf16[8,3,16,3584]{3,2,1,0:T(8,128)(2,1)} %bitcast.136), kind=kLoop, calls=%fused_computation.109 | loop fusion | bytes 5505024 | tf_op jit(solution)/shard_map/slice | solution.py:115
  75.2 1.8 broadcast_in_dim.139
  77.0 4.6 %all-to-all-start.2 = ((bf16[4,96,3712]{2,1,0:T(8,128)(2,1)}), bf16[4,96,3712]{2,1,0:T(8,128)(2,1)}, u32[]{:S(2)}, u32[]{:S(2)}) async-start(bf16[4,96,3712]{2,1,0:T(8,128)(2,1)} %broadcast_in_dim.139), calls=%async_computation.2 | async-start | bytes 5701632 | tf_op jit(solution)/shard_map/all_to_all | solution.py:21
  83.0 1.8 collective-permute-done.3
  85.8 2.2 %collective-permute-start.5 = (bf16[48,3584]{1,0:T(8,128)(2,1)S(1)}, bf16[48,3584]{1,0:T(8,128)(2,1)S(1)}, u32[]{:S(2)}, u32[]{:S(2)}) collective-permute-start(bf16[48,3584]{1,0:T(8,128)(2,1)S(1)} %slice.89), channel_id=1, source_target_pairs={{0,2},{2,4},{4,6},{6,0},{1,3},{3,5},{5,7},{7,1},{8,10},{10,12},{12... | collective-permute-start | bytes 1032200 | tf_op jit(solution)/shard_map/ppermute | solution.py:48
  89.1 4.3 %collective-permute-start.6 = (bf16[48,3584]{1,0:T(8,128)(2,1)S(1)}, bf16[48,3584]{1,0:T(8,128)(2,1)S(1)}, u32[]{:S(2)}, u32[]{:S(2)}) collective-permute-start(bf16[48,3584]{1,0:T(8,128)(2,1)S(1)} %slice.90), channel_id=1, source_target_pairs={{0,6},{2,0},{4,2},{6,4},{1,7},{3,1},{5,3},{7,5},{8,14},{10,8},{12,... | collective-permute-start | bytes 1032200 | tf_op jit(solution)/shard_map/ppermute | solution.py:49
  96.3 2.8 %collective-permute-done.6 = bf16[48,3584]{1,0:T(8,128)(2,1)S(1)} collective-permute-done((bf16[48,3584]{1,0:T(8,128)(2,1)S(1)}, bf16[48,3584]{1,0:T(8,128)(2,1)S(1)}, u32[]{:S(2)}, u32[]{:S(2)}) %collective-permute-start.6) | collective-permute-done | bytes 344096 | tf_op jit(solution)/shard_map/ppermute | solution.py:49
  99.1 1.6 copy-done.1
  101.6 12.4 %all-to-all-done.2 = bf16[4,96,3712]{2,1,0:T(8,128)(2,1)} async-done(((bf16[4,96,3712]{2,1,0:T(8,128)(2,1)}), bf16[4,96,3712]{2,1,0:T(8,128)(2,1)}, u32[]{:S(2)}, u32[]{:S(2)}) %all-to-all-start.2) | async-done | bytes 2850848 | tf_op jit(solution)/shard_map/all_to_all | solution.py:21
  115.1 2.9 %fusion.5 = f32[384,128]{1,0:T(8,128)S(1)} fusion(bf16[128,3584]{1,0:T(8,128)(2,1)} %bitcast.132, bf16[384,3712]{1,0:T(8,128)(2,1)} %bitcast.28), kind=kOutput, calls=%fused_computation.17 | convolution fusion | flops 352321536 | bytes 3866624 | tf_op jit(solution)/shard_map/rd,hd->rh/dot_general | solution.py:60
  118.0 2.8 %fusion.16 = (bf16[384]{0:T(512)(128)(2,1)S(1)}, bf16[384,128]{1,0:T(8,128)(2,1)S(1)}, bf16[384,128]{1,0:T(8,128)(2,1)S(1)}, bf16[384,128]{1,0:T(8,128)(2,1)S(1)}) fusion(f32[4,4,24,128]{3,2,1,0:T(8,128)S(1)} %copy.40, f32[384,128]{1,0:T(8,128)S(1)} %fusion.5, f32[384]{0:T(512)S(1)} %convert_reduce_fusion, bf16[128,3584]{1,0:T(8,128)(2,1)S(1)} %bitcast.127, ...), kind=kOutput, calls=%fused_computation.44 | convolution fusion | flops 353255040 | bytes 4360448 | tf_op jit(solution)/shard_map/rd,hd->rh/dot_general | solution.py:60
  122.6 1.8 pad_maximum_fusion
  124.4 4.5 %all-to-all-start.3 = ((bf16[16,24,3712]{2,1,0:T(8,128)(2,1)}), bf16[16,24,3712]{2,1,0:T(8,128)(2,1)}, u32[]{:S(2)}, u32[]{:S(2)}) async-start(bf16[16,24,3712]{2,1,0:T(8,128)(2,1)} %bitcast.125), calls=%async_computation.4 | async-start | bytes 5701632 | tf_op jit(solution)/shard_map/all_to_all | solution.py:144
  129.1 2.7 %convolution_convert_fusion.2 = bf16[3584,128]{1,0:T(8,128)(2,1)S(1)} fusion(bf16[384,128]{1,0:T(8,128)(2,1)S(1)} %get-tuple-element.55, bf16[384,3712]{1,0:T(8,128)(2,1)} %bitcast.28), kind=kOutput, calls=%fused_computation.6 | convolution fusion | flops 352780288 | bytes 3768320 | tf_op jit(solution)/shard_map/rd,rh->dh/dot_general | solution.py:60
  131.8 2.8 %convolution_convert_fusion.3 = bf16[3584,128]{1,0:T(8,128)(2,1)S(1)} fusion(bf16[384,128]{1,0:T(8,128)(2,1)S(1)} %get-tuple-element.54, bf16[384,3712]{1,0:T(8,128)(2,1)} %bitcast.28), kind=kOutput, calls=%fused_computation.7 | convolution fusion | flops 352780288 | bytes 3768320 | tf_op jit(solution)/shard_map/rd,rh->dh/dot_general | solution.py:60
  135.6 1.8 pad_maximum_fusion.1
  139.3 30.3 %all-to-all-done.3 = bf16[16,24,3712]{2,1,0:T(8,128)(2,1)} async-done(((bf16[16,24,3712]{2,1,0:T(8,128)(2,1)}), bf16[16,24,3712]{2,1,0:T(8,128)(2,1)}, u32[]{:S(2)}, u32[]{:S(2)}) %all-to-all-start.3) | async-done | bytes 2850848 | tf_op jit(solution)/shard_map/all_to_all | solution.py:144
  169.7 2.4 %convolution_bitcast_fusion = f32[32,3712]{1,0:T(8,128)S(1)} fusion(bf16[16,24,3712]{2,1,0:T(8,128)(2,1)} %all-to-all-done.3, bf16[32,24]{0,1:T(8,128)(2,1)S(1)} %fusion.30), kind=kOutput, calls=%fused_computation.8 | convolution fusion | flops 91226112 | bytes 3327488 | tf_op jit(solution)/shard_map/ck,kd->cd/dot_general | solution.py:60
  172.8 10.3 %all-to-all-start.4 = ((bf16[4,8,3712]{2,1,0:T(8,128)(2,1)}), bf16[4,8,3712]{2,1,0:T(8,128)(2,1)S(1)}, u32[]{:S(2)}, u32[]{:S(2)}) async-start(bf16[4,8,3712]{2,1,0:T(8,128)(2,1)} %pad_maximum_fusion.3), calls=%async_computation.5 | async-start | bytes 475136 | tf_op jit(solution)/shard_map/all_to_all | solution.py:153
  184.9 7.2 %reduce-scatter.2.cloned.1.call-done = bf16[1,3,448,128]{3,2,1,0:T(8,128)(2,1)} async-done(((bf16[8,3,448,128]{3,2,1,0:T(8,128)(2,1)}), bf16[1,3,448,128]{3,2,1,0:T(8,128)(2,1)}) %reduce-scatter.2.cloned.1.call-update) | async-done | bytes 344080 | tf_op jit(solution)/shard_map/reduce_scatter | solution.py:137
  193.9 1.4 convolution_convert_fusion
  (71 shorter events, 27.5 us)
Async XLA Ops:
  7.2 3.6 %copy-start = (bf16[128,3584]{1,0:T(8,128)(2,1)S(1)}, bf16[128,3584]{1,0:T(8,128)(2,1)}, u32[]{:S(2)}) copy-start(bf16[128,3584]{1,0:T(8,128)(2,1)} %param.8) | copy-start | bytes 2752516
  7.2 5.4 %copy-start.4 = (s32[128,8]{0,1:T(8,128)S(1)}, s32[128,8]{0,1:T(8,128)}, u32[]{:S(2)}) copy-start(s32[128,8]{0,1:T(8,128)} %param.9) | copy-start | bytes 12292
  7.2 58.6 %all-gather.2.cloned.1.call-start = ((), (), s32[]{:S(2)}) async-start(), calls=%async_computation.6 | async-start | bytes 3096576 | tf_op jit(solution)/shard_map/all_gather | solution.py:68
  13.6 21.7 %all-to-all-start = ((bf16[4,8,7296]{2,1,0:T(8,128)(2,1)}), bf16[4,8,7296]{2,1,0:T(8,128)(2,1)S(1)}, u32[]{:S(2)}, u32[]{:S(2)}) async-start(bf16[4,8,7296]{2,1,0:T(8,128)(2,1)} %maximum_bitcast_fusion), calls=%async_computation | async-start | bytes 933888 | tf_op jit(solution)/shard_map/all_to_all | solution.py:91
  37.1 18.1 %collective-permute-start = (bf16[24,3584]{1,0:T(8,128)(2,1)S(1)}, bf16[24,3584]{1,0:T(8,128)(2,1)S(1)}, u32[]{:S(2)}, u32[]{:S(2)}) collective-permute-start(bf16[24,3584]{1,0:T(8,128)(2,1)S(1)} %get-tuple-element.57), channel_id=1, source_target_pairs={{0,1},{1,0},{8,9},{9,8},{2,3},{3,2},{10,11},{11,10},{4,5},{5,4},{1... | collective-permute-start | bytes 516104 | tf_op jit(solution)/shard_map/ppermute | solution.py:34
  40.3 15.6 %collective-permute-start.1 = (bf16[24,3584]{1,0:T(8,128)(2,1)S(1)}, bf16[24,3584]{1,0:T(8,128)(2,1)S(1)}, u32[]{:S(2)}, u32[]{:S(2)}) collective-permute-start(bf16[24,3584]{1,0:T(8,128)(2,1)S(1)} %get-tuple-element.57), channel_id=1, source_target_pairs={{0,8},{1,9},{8,0},{9,1},{2,10},{3,11},{10,2},{11,3},{4,12},{5,13},... | collective-permute-start | bytes 516104 | tf_op jit(solution)/shard_map/ppermute | solution.py:34
  47.6 16.9 %collective-permute-start.2 = (bf16[24,3584]{1,0:T(8,128)(2,1)S(1)}, bf16[24,3584]{1,0:T(8,128)(2,1)S(1)}, u32[]{:S(2)}, u32[]{:S(2)}) collective-permute-start(bf16[24,3584]{1,0:T(8,128)(2,1)S(1)} %get-tuple-element.57), channel_id=1, source_target_pairs={{0,9},{1,8},{8,1},{9,0},{2,11},{3,10},{10,3},{11,2},{4,13},{5,12},... | collective-permute-start | bytes 516104 | tf_op jit(solution)/shard_map/ppermute | solution.py:34
  50.7 14.5 %all-to-all-start.1 = ((bf16[4,24,3712]{2,1,0:T(8,128)(2,1)}), bf16[4,24,3712]{2,1,0:T(8,128)(2,1)S(1)}, u32[]{:S(2)}, u32[]{:S(2)}) async-start(bf16[4,24,3712]{2,1,0:T(8,128)(2,1)} %broadcast_in_dim.130), calls=%async_computation.1 | async-start | bytes 1425408 | tf_op jit(solution)/shard_map/all_to_all | solution.py:21
  65.8 19.0 %collective-permute-start.3 = (bf16[96,3584]{1,0:T(8,128)(2,1)}, bf16[96,3584]{1,0:T(8,128)(2,1)}, u32[]{:S(2)}, u32[]{:S(2)}) collective-permute-start(bf16[96,3584]{1,0:T(8,128)(2,1)} %bitcast.11), channel_id=1, source_target_pairs={{0,2},{2,4},{4,6},{6,0},{1,3},{3,5},{5,7},{7,1},{8,10},{10,12},{12... | collective-permute-start | bytes 2064392 | tf_op jit(solution)/shard_map/ppermute | solution.py:46
  68.6 19.4 %collective-permute-start.4 = (bf16[96,3584]{1,0:T(8,128)(2,1)}, bf16[96,3584]{1,0:T(8,128)(2,1)}, u32[]{:S(2)}, u32[]{:S(2)}) collective-permute-start(bf16[96,3584]{1,0:T(8,128)(2,1)} %bitcast.11), channel_id=1, source_target_pairs={{0,6},{2,0},{4,2},{6,4},{1,7},{3,1},{5,3},{7,5},{8,14},{10,8},{12,... | collective-permute-start | bytes 2064392 | tf_op jit(solution)/shard_map/ppermute | solution.py:47
  77.0 37.1 %all-to-all-start.2 = ((bf16[4,96,3712]{2,1,0:T(8,128)(2,1)}), bf16[4,96,3712]{2,1,0:T(8,128)(2,1)}, u32[]{:S(2)}, u32[]{:S(2)}) async-start(bf16[4,96,3712]{2,1,0:T(8,128)(2,1)} %broadcast_in_dim.139), calls=%async_computation.2 | async-start | bytes 5701632 | tf_op jit(solution)/shard_map/all_to_all | solution.py:21
  85.8 10.4 %collective-permute-start.5 = (bf16[48,3584]{1,0:T(8,128)(2,1)S(1)}, bf16[48,3584]{1,0:T(8,128)(2,1)S(1)}, u32[]{:S(2)}, u32[]{:S(2)}) collective-permute-start(bf16[48,3584]{1,0:T(8,128)(2,1)S(1)} %slice.89), channel_id=1, source_target_pairs={{0,2},{2,4},{4,6},{6,0},{1,3},{3,5},{5,7},{7,1},{8,10},{10,12},{12... | collective-permute-start | bytes 1032200 | tf_op jit(solution)/shard_map/ppermute | solution.py:48
  89.1 10.0 %collective-permute-start.6 = (bf16[48,3584]{1,0:T(8,128)(2,1)S(1)}, bf16[48,3584]{1,0:T(8,128)(2,1)S(1)}, u32[]{:S(2)}, u32[]{:S(2)}) collective-permute-start(bf16[48,3584]{1,0:T(8,128)(2,1)S(1)} %slice.90), channel_id=1, source_target_pairs={{0,6},{2,0},{4,2},{6,4},{1,7},{3,1},{5,3},{7,5},{8,14},{10,8},{12,... | collective-permute-start | bytes 1032200 | tf_op jit(solution)/shard_map/ppermute | solution.py:49
  99.1 1.6 copy-start.1
  117.9 2.8 %copy-start.3 = (bf16[8,1,16,3584]{3,2,1,0:T(8,128)(2,1)S(1)}, bf16[8,1,16,3584]{3,2,1,0:T(8,128)(2,1)}, u32[]{:S(2)}) copy-start(bf16[8,1,16,3584]{3,2,1,0:T(8,128)(2,1)} %get-tuple-element.50) | copy-start | bytes 2752516
  124.4 45.3 %all-to-all-start.3 = ((bf16[16,24,3712]{2,1,0:T(8,128)(2,1)}), bf16[16,24,3712]{2,1,0:T(8,128)(2,1)}, u32[]{:S(2)}, u32[]{:S(2)}) async-start(bf16[16,24,3712]{2,1,0:T(8,128)(2,1)} %bitcast.125), calls=%async_computation.4 | async-start | bytes 5701632 | tf_op jit(solution)/shard_map/all_to_all | solution.py:144
  128.9 63.1 %reduce-scatter.2.cloned.1.call-start = ((), (), s32[]{:S(2)}) async-start(), calls=%async_computation.7 | async-start | bytes 3096576 | tf_op jit(solution)/shard_map/reduce_scatter | solution.py:137
  131.8 2.9 %copy-start.2 = (bf16[4,96,3584]{2,1,0:T(8,128)(2,1)S(1)}, bf16[4,96,3584]{2,1,0:T(8,128)(2,1)}, u32[]{:S(2)}) copy-start(bf16[4,96,3584]{2,1,0:T(8,128)(2,1)} %copy-done.1) | copy-start | bytes 8257540
  172.8 21.1 %all-to-all-start.4 = ((bf16[4,8,3712]{2,1,0:T(8,128)(2,1)}), bf16[4,8,3712]{2,1,0:T(8,128)(2,1)S(1)}, u32[]{:S(2)}, u32[]{:S(2)}) async-start(bf16[4,8,3712]{2,1,0:T(8,128)(2,1)} %pad_maximum_fusion.3), calls=%async_computation.5 | async-start | bytes 475136 | tf_op jit(solution)/shard_map/all_to_all | solution.py:153
Sparse Core Ops, SparseCore 0:
  10.2 55.6 all-gather.1
  137.6 54.4 reduce-scatter.1

commit v3 on v2

--- a/solution.py
+++ b/solution.py
@@ -10,7 +10,6 @@
 EXPERTS = 4
 LANES = 128
 DP = ("yh", "core")
-COLOR_A = ("zl", "yl", "x")
 BF = jnp.bfloat16
 F32 = jnp.float32
 
@@ -22,22 +21,49 @@
     return got.reshape((count * block.shape[0],) + block.shape[1:])
 
 
-def put(total, block, at):
-    return lax.dynamic_update_slice_in_dim(total, block[None], at, axis=0)
-
-
-def spread_square(block):
-    z, y = lax.axis_index("zl"), lax.axis_index("yl")
-    me = 2 * z + y
+RIGHT = [(i, (i + 1) % 4) for i in range(4)]
+LEFT = [(i, (i + 3) % 4) for i in range(4)]
+SWAP = [(0, 1), (1, 0)]
+
+
+def put(total, block, at, row=0):
+    return lax.dynamic_update_slice(total, block[None], (at, row, 0))
+
+
+def square_index():
+    return 2 * lax.axis_index("zl") + lax.axis_index("yl")
+
+
+def spread_direct(block):
+    me = square_index()
     total = put(jnp.zeros((4,) + block.shape, block.dtype), block, me)
     for off in (1, 2, 3):
         got = lax.ppermute(block, ("zl", "yl"), [(i, i ^ off) for i in range(4)])
         total = put(total, got, me ^ off)
-    return total.reshape((4 * block.shape[0],) + block.shape[1:])
-
-
-RIGHT = [(i, (i + 1) % 4) for i in range(4)]
-LEFT = [(i, (i + 3) % 4) for i in range(4)]
+    return total
+
+
+def spread_square(block, held):
+    me = square_index()
+    top, low = block[:2], block[2:]
+    top_z = lax.ppermute(top, "zl", SWAP)
+    low_y = lax.ppermute(low, "yl", SWAP)
+    top_z, low_y, held = lax.optimization_barrier((top_z, low_y, held))
+    top_two = lax.ppermute(jnp.stack([top, top_z]), "yl", SWAP)
+    low_two = lax.ppermute(jnp.stack([low, low_y]), "zl", SWAP)
+    total = jnp.zeros((block.shape[0], 4) + block.shape[1:], block.dtype)
+
+    def place(total, piece, first, at):
+        return lax.dynamic_update_slice(total, piece[:, None], (first, at, 0, 0))
+
+    total = place(total, block, 0, me)
+    total = place(total, top_z, 0, me ^ 2)
+    total = place(total, low_y, 2, me ^ 1)
+    total = place(total, top_two[0], 0, me ^ 1)
+    total = place(total, top_two[1], 0, me ^ 3)
+    total = place(total, low_two[0], 2, me ^ 2)
+    total = place(total, low_two[1], 2, me ^ 3)
+    return total, held
 
 
 def spread_ring(block):
@@ -50,10 +76,28 @@
     total = put(jnp.zeros((4,) + block.shape, block.dtype), block, me)
     total = put(total, from_left, (me + 3) % 4)
     total = put(total, from_right, (me + 1) % 4)
-    far = (me + 2) % 4
-    total = lax.dynamic_update_slice(total, far_top[None], (far, 0, 0))
-    total = lax.dynamic_update_slice(total, far_low[None], (far, half, 0))
-    return total.reshape((4 * block.shape[0],) + block.shape[1:])
+    total = put(total, far_top, (me + 2) % 4)
+    return put(total, far_low, (me + 2) % 4, half)
+
+
+def sum_ring(parts):
+    me = lax.axis_index("x")
+    half = parts.shape[1] // 2
+
+    def part(off):
+        return lax.dynamic_index_in_dim(parts, (me + off) % 4, 0, keepdims=False)
+
+    far = part(2)
+    top = lax.ppermute(far[:half], "x", RIGHT)
+    low = lax.ppermute(far[half:], "x", LEFT)
+    right, left = part(1), part(3)
+    right = jnp.concatenate([add(right[:half], top), right[half:]], axis=0)
+    left = jnp.concatenate([left[:half], add(left[half:], low)], axis=0)
+    return part(0), lax.ppermute(right, "x", RIGHT), lax.ppermute(left, "x", LEFT)
+
+
+def add(a, b):
+    return (a.astype(F32) + b.astype(F32)).astype(BF)
 
 
 def dot(eq, a, b):
@@ -67,7 +111,6 @@
     mine = jnp.concatenate([w_gate[0].T, w_up[0].T, w_down[0].T], axis=0)
     gathered = lax.all_gather(mine, DP, axis=0, tiled=True)
     n_dp = lax.axis_size(DP)
-    gathered = gathered.reshape(n_dp, 3, hidden_dev, features)
 
     ids = route_ids.T
     gates_t = gates.T.astype(F32)
@@ -98,19 +141,15 @@
     tok_rows = dot("kc,cd->kd", keep, rows[:, :wide]).astype(BF)
     cot_rows = dot("kc,cd->kd", keep, rows[:, wide:]).astype(BF)
 
-    tok_half = spread(tok_rows, "x")
-    cot_half = spread_square(cot_rows)
-    tok_half, cot_half, gathered = lax.optimization_barrier((tok_half, cot_half, gathered))
-    slot_all = spread(tok_half, ("zl", "yl"))
-    slot_cotan = spread_ring(cot_half)
+    block = EXPERTS * CAP
+    tok_half = spread(tok_rows, "x").reshape(4, block, wide)
+    cot_half = spread_direct(cot_rows).reshape(4 * block, features)
+    slot_all, gathered = spread_square(tok_half, gathered)
+    slot_all = slot_all.reshape(-1, wide)
+    slot_cotan = spread_ring(cot_half).reshape(-1, features)
     slot_tokens = slot_all[:, :features]
     slot_gates = slot_all[:, features : features + 1].astype(F32)
-
-    block = EXPERTS * CAP
-
-    def to_tok_order(values):
-        v = values.reshape(4, 4, block, values.shape[-1])
-        return jnp.swapaxes(v, 0, 1).reshape(values.shape)
+    gathered = gathered.reshape(n_dp, 3, hidden_dev, features)
 
     slab = [gathered[:, j].reshape(n_dp * hidden_dev, features) for j in range(3)]
     gate_slab, up_slab, down_slab = slab
@@ -119,12 +158,12 @@
     sigmoid_gate = jax.nn.sigmoid(pre_gate)
     activation = pre_gate * sigmoid_gate
     hidden = (activation * pre_up).astype(BF)
-    back_proj = to_tok_order(dot("rd,hd->rh", slot_cotan, down_slab))
+    back_proj = dot("rd,hd->rh", slot_cotan, down_slab)
     score = jnp.sum(hidden.astype(F32) * back_proj, axis=1, keepdims=True).astype(BF)
     scaled = slot_gates * back_proj
     d_gate = (scaled * pre_up * sigmoid_gate * (1.0 + pre_gate * (1.0 - sigmoid_gate))).astype(BF)
     d_up = (scaled * activation).astype(BF)
-    hidden_gated = to_tok_order((slot_gates * hidden.astype(F32)).astype(BF))
+    hidden_gated = (slot_gates * hidden.astype(F32)).astype(BF)
 
     grads = jnp.stack(
         [
@@ -140,22 +179,20 @@
         dot("rh,hd->rd", d_gate, gate_slab) + dot("rh,hd->rd", d_up, up_slab)
     ).astype(BF)
     back = jnp.concatenate([partial, jnp.broadcast_to(score, (score.shape[0], LANES))], axis=1)
-    back = back.reshape(HSPLIT, block, -1)
-    back = lax.all_to_all(back, COLOR_A, split_axis=0, concat_axis=0, tiled=True)
-    back = back.reshape(HSPLIT * block, -1)
-    fold = jnp.tile(keep.T, (1, HSPLIT))
-    summed = dot("ck,kd->cd", fold, back)
-    score_sum = summed[:, features:]
-    high = lax.reduce_precision(score_sum, 8, 7)
-    lane = jnp.arange(LANES)[None, :]
-    score_cols = jnp.where(lane < LANES // 2, high, score_sum - high)
-    home = jnp.concatenate([summed[:, :features], score_cols], axis=1).astype(BF)
+    trio = jnp.concatenate(sum_ring(back.reshape(4, 4 * block, wide)), axis=0)
+    row = jnp.arange(4 * block)
+    target = (row // CAP % EXPERTS * 4 + row // block) * PAD + row % CAP
+    fold = (jnp.arange(HSPLIT * PAD)[:, None] == target[None, :]).astype(BF)
+    home = dot("ck,kd->cd", jnp.tile(fold, (1, 3)), trio).astype(BF)
     home = lax.all_to_all(
-        home.reshape(EXPERTS, PAD, -1), "ex", split_axis=0, concat_axis=0, tiled=True
-    ).reshape(EXPERTS * PAD, -1)
-    token_grad = dot("ct,cd->td", pick_rows, home[:, :features]).astype(BF)
-    pair = home[:, features:].astype(F32)
-    score_slots = (pair[:, :1] + pair[:, LANES // 2 : LANES // 2 + 1]).reshape(EXPERTS, PAD, 1)
+        home.reshape(HSPLIT, PAD, wide), ("ex", "zl", "yl"), split_axis=0, concat_axis=0, tiled=True
+    ).reshape(HSPLIT * PAD, wide)
+    pick_home = jnp.broadcast_to(pick[:, None], (EXPERTS, 4, PAD, tok_count))
+    pick_home = pick_home.reshape(HSPLIT * PAD, tok_count).astype(BF)
+    token_grad = dot("ct,cd->td", pick_home, home[:, :features]).astype(BF)
+    score_slots = jnp.sum(
+        home[:, features : features + 1].astype(F32).reshape(EXPERTS, 4, PAD, 1), axis=1
+    )
     score_token = jnp.sum(jnp.where(pick, score_slots, 0.0), axis=1)
     gate_grad = jnp.sum(jnp.where(hits, score_token[:, None, :], 0.0), axis=0).T
 

time: 206 us -> 217 us (1.053)
  the two profiles are of different devices: /device:TPU:1 before, /device:TPU:32 now
where the time goes in v3:
time: 217 us; the launch traced here: 216 us
  starting transfers between devices  77.4 us (36%)
  waiting for transfers between devices  70 us (32%)
  local copies, waits for them, and re-layouts  22.7 us (10%)
  matrix products  19 us (9%)
  between operations  14.6 us (7%)
  other arithmetic  12.2 us (6%)
    dot_general x15, matrix products, dot(): return jnp.einsum(eq, a, b, preferred_element_type=F32)  19 us
    all_to_all x1, waiting for transfers between devices, shards(): lax.all_to_all(home.reshape(HSPLIT, PAD, wide), ('ex', 'zl', 'yl'), split...  17.7 us
    all_to_all x1, waiting for transfers between devices, shards(): rows = lax.all_to_all(rows, 'ex', split_axis=0, concat_axis=0, tiled=True)  13.2 us
    all_to_all x1, starting transfers between devices, shards(): lax.all_to_all(home.reshape(HSPLIT, PAD, wide), ('ex', 'zl', 'yl'), split...  12.5 us
    ppermute x3, waiting for transfers between devices, spread_direct(): got = lax.ppermute(block, ('zl', 'yl'), [(i, i ^ off) for i in range(4)])  12.1 us
    all_to_all x1, starting transfers between devices, shards(): rows = lax.all_to_all(rows, 'ex', split_axis=0, concat_axis=0, tiled=True)  10.3 us
    ppermute x3, starting transfers between devices, spread_direct(): got = lax.ppermute(block, ('zl', 'yl'), [(i, i ^ off) for i in range(4)])  9.96 us
    ppermute x1, waiting for transfers between devices, spread_square(): top_two = lax.ppermute(jnp.stack([top, top_z]), 'yl', SWAP)  7.49 us
  transfers between devices with their start and end apart: 20, of which 10 were waited for; matrix products, arithmetic and copies ran while one was open for 13% of the time, Pallas kernels for 0%

profile of v3, /device:TPU:32, one launch (start us, length us, event | category | flops | bytes accessed | tf_op | source)
XLA Modules:
  0.0 215.8 jit_solution(9880957551360038477)
XLA Ops:
  12.5 10.3 %all-to-all-start = ((bf16[4,8,7296]{2,1,0:T(8,128)(2,1)}), bf16[4,8,7296]{2,1,0:T(8,128)(2,1)S(1)}, u32[]{:S(2)}, u32[]{:S(2)}) async-start(bf16[4,8,7296]{2,1,0:T(8,128)(2,1)} %maximum_bitcast_fusion), calls=%async_computation | async-start | bytes 933888 | tf_op jit(solution)/shard_map/all_to_all | solution.py:134
  23.6 13.2 %all-to-all-done = bf16[4,8,7296]{2,1,0:T(8,128)(2,1)S(1)} async-done(((bf16[4,8,7296]{2,1,0:T(8,128)(2,1)}), bf16[4,8,7296]{2,1,0:T(8,128)(2,1)S(1)}, u32[]{:S(2)}, u32[]{:S(2)}) %all-to-all-start) | async-done | bytes 466976 | tf_op jit(solution)/shard_map/all_to_all | solution.py:134
  37.1 2.6 %collective-permute-start.4 = (bf16[24,3584]{1,0:T(8,128)(2,1)S(1)}, bf16[24,3584]{1,0:T(8,128)(2,1)S(1)}, u32[]{:S(2)}, u32[]{:S(2)}) collective-permute-start(bf16[24,3584]{1,0:T(8,128)(2,1)S(1)} %get-tuple-element.59), channel_id=1, source_target_pairs={{0,1},{1,0},{8,9},{9,8},{2,3},{3,2},{10,11},{11,10},{4,5},{5,4},{1... | collective-permute-start | bytes 516104 | tf_op jit(solution)/shard_map/ppermute | solution.py:41
  39.7 4.7 %collective-permute-start.5 = (bf16[24,3584]{1,0:T(8,128)(2,1)S(1)}, bf16[24,3584]{1,0:T(8,128)(2,1)S(1)}, u32[]{:S(2)}, u32[]{:S(2)}) collective-permute-start(bf16[24,3584]{1,0:T(8,128)(2,1)S(1)} %get-tuple-element.59), channel_id=1, source_target_pairs={{0,8},{1,9},{8,0},{9,1},{2,10},{3,11},{10,2},{11,3},{4,12},{5,13},... | collective-permute-start | bytes 516104 | tf_op jit(solution)/shard_map/ppermute | solution.py:41
  44.4 2.7 %collective-permute-start.6 = (bf16[24,3584]{1,0:T(8,128)(2,1)S(1)}, bf16[24,3584]{1,0:T(8,128)(2,1)S(1)}, u32[]{:S(2)}, u32[]{:S(2)}) collective-permute-start(bf16[24,3584]{1,0:T(8,128)(2,1)S(1)} %get-tuple-element.59), channel_id=1, source_target_pairs={{0,9},{1,8},{8,1},{9,0},{2,11},{3,10},{10,3},{11,2},{4,13},{5,12},... | collective-permute-start | bytes 516104 | tf_op jit(solution)/shard_map/ppermute | solution.py:41
  48.3 4.3 %all-to-all-start.1 = ((bf16[4,24,3712]{2,1,0:T(8,128)(2,1)}), bf16[4,24,3712]{2,1,0:T(8,128)(2,1)S(1)}, u32[]{:S(2)}, u32[]{:S(2)}) async-start(bf16[4,24,3712]{2,1,0:T(8,128)(2,1)} %broadcast_in_dim.127), calls=%async_computation.1 | async-start | bytes 1425408 | tf_op jit(solution)/shard_map/all_to_all | solution.py:20
  52.6 12.1 %collective-permute-done.6 = bf16[24,3584]{1,0:T(8,128)(2,1)S(1)} collective-permute-done((bf16[24,3584]{1,0:T(8,128)(2,1)S(1)}, bf16[24,3584]{1,0:T(8,128)(2,1)S(1)}, u32[]{:S(2)}, u32[]{:S(2)}) %collective-permute-start.6) | collective-permute-done | bytes 172064 | tf_op jit(solution)/shard_map/ppermute | solution.py:41
  64.7 3.4 %collective-permute-start.7 = (bf16[96,3584]{1,0:T(8,128)(2,1)S(1)}, bf16[96,3584]{1,0:T(8,128)(2,1)S(1)}, u32[]{:S(2)}, u32[]{:S(2)}) collective-permute-start(bf16[96,3584]{1,0:T(8,128)(2,1)S(1)} %bitcast.177), channel_id=1, source_target_pairs={{0,2},{2,4},{4,6},{6,0},{1,3},{3,5},{5,7},{7,1},{8,10},{10,12},{12... | collective-permute-start | bytes 2064392 | tf_op jit(solution)/shard_map/ppermute | solution.py:72
  68.2 3.7 %collective-permute-start.8 = (bf16[96,3584]{1,0:T(8,128)(2,1)S(1)}, bf16[96,3584]{1,0:T(8,128)(2,1)}, u32[]{:S(2)}, u32[]{:S(2)}) collective-permute-start(bf16[96,3584]{1,0:T(8,128)(2,1)S(1)} %bitcast.178), channel_id=1, source_target_pairs={{0,6},{2,0},{4,2},{6,4},{1,7},{3,1},{5,3},{7,5},{8,14},{10,8},{12,... | collective-permute-start | bytes 2064392 | tf_op jit(solution)/shard_map/ppermute | solution.py:73
  75.5 1.9 collective-permute-start
  77.4 2.6 %collective-permute-start.1 = (bf16[2,24,3712]{2,1,0:T(8,128)(2,1)S(1)}, bf16[2,24,3712]{2,1,0:T(8,128)(2,1)S(1)}, u32[]{:S(2)}, u32[]{:S(2)}) collective-permute-start(bf16[2,24,3712]{2,1,0:T(8,128)(2,1)S(1)} %get-tuple-element.51), channel_id=1, source_target_pairs={{0,1},{1,0},{2,3},{3,2},{4,5},{5,4},{6,7},{7,6},{8,9},{9,8},{10,11... | collective-permute-start | bytes 1069064 | tf_op jit(solution)/shard_map/ppermute | solution.py:50
  80.3 2.2 %collective-permute-start.9 = (bf16[48,3584]{1,0:T(8,128)(2,1)S(1)}, bf16[48,3584]{1,0:T(8,128)(2,1)S(1)}, u32[]{:S(2)}, u32[]{:S(2)}) collective-permute-start(bf16[48,3584]{1,0:T(8,128)(2,1)S(1)} %slice.147), channel_id=1, source_target_pairs={{0,2},{2,4},{4,6},{6,0},{1,3},{3,5},{5,7},{7,1},{8,10},{10,12},{12... | collective-permute-start | bytes 1032200 | tf_op jit(solution)/shard_map/ppermute | solution.py:74
  83.6 4.8 %collective-permute-start.10 = (bf16[48,3584]{1,0:T(8,128)(2,1)S(1)}, bf16[48,3584]{1,0:T(8,128)(2,1)S(1)}, u32[]{:S(2)}, u32[]{:S(2)}) collective-permute-start(bf16[48,3584]{1,0:T(8,128)(2,1)S(1)} %slice.148), channel_id=1, source_target_pairs={{0,6},{2,0},{4,2},{6,4},{1,7},{3,1},{5,3},{7,5},{8,14},{10,8},{12,... | collective-permute-start | bytes 1032200 | tf_op jit(solution)/shard_map/ppermute | solution.py:75
  89.4 2.0 bitcast_dynamic-update-slice_fusion.1
  94.7 2.1 fusion.63
  97.5 4.1 %collective-permute-start.2 = (bf16[2,2,24,3712]{3,2,1,0:T(8,128)(2,1)S(1)}, bf16[2,2,24,3712]{3,2,1,0:T(8,128)(2,1)S(1)}, u32[]{:S(2)}, u32[]{:S(2)}) collective-permute-start(bf16[2,2,24,3712]{3,2,1,0:T(8,128)(2,1)S(1)} %pad_maximum_fusion.2), channel_id=1, source_target_pairs={{0,1},{1,0},{2,3},{3,2},{4,5},{5,4},{6,7},{7,6},{8,9},{9,8},{10,11... | collective-permute-start | bytes 2138120 | tf_op jit(solution)/shard_map/ppermute | solution.py:52
  101.8 3.0 %collective-permute-start.3 = (bf16[2,2,24,3712]{3,2,1,0:T(8,128)(2,1)S(1)}, bf16[2,2,24,3712]{3,2,1,0:T(8,128)(2,1)S(1)}, u32[]{:S(2)}, u32[]{:S(2)}) collective-permute-start(bf16[2,2,24,3712]{3,2,1,0:T(8,128)(2,1)S(1)} %pad_maximum_fusion.3), channel_id=1, source_target_pairs={{0,8},{8,0},{1,9},{9,1},{2,10},{10,2},{3,11},{11,3},{4,12},{12,4},... | collective-permute-start | bytes 2138120 | tf_op jit(solution)/shard_map/ppermute | solution.py:53
  104.8 7.5 %collective-permute-done.2 = bf16[2,2,24,3712]{3,2,1,0:T(8,128)(2,1)S(1)} collective-permute-done((bf16[2,2,24,3712]{3,2,1,0:T(8,128)(2,1)S(1)}, bf16[2,2,24,3712]{3,2,1,0:T(8,128)(2,1)S(1)}, u32[]{:S(2)}, u32[]{:S(2)}) %collective-permute-start.2) | collective-permute-done | bytes 712736 | tf_op jit(solution)/shard_map/ppermute | solution.py:52
  112.4 3.5 %collective-permute-done.3 = bf16[2,2,24,3712]{3,2,1,0:T(8,128)(2,1)S(1)} collective-permute-done((bf16[2,2,24,3712]{3,2,1,0:T(8,128)(2,1)S(1)}, bf16[2,2,24,3712]{3,2,1,0:T(8,128)(2,1)S(1)}, u32[]{:S(2)}, u32[]{:S(2)}) %collective-permute-start.3) | collective-permute-done | bytes 712736 | tf_op jit(solution)/shard_map/ppermute | solution.py:53
  118.1 2.8 %fusion.27 = (bf16[384]{0:T(512)(128)(2,1)S(1)}, bf16[384,128]{0,1:T(8,128)(2,1)S(1)}, bf16[384,128]{0,1:T(8,128)(2,1)S(1)}, bf16[384,128]{0,1:T(8,128)(2,1)S(1)}) fusion(f32[384,128]{0,1:T(8,128)S(1)} %fusion.13, f32[384,128]{0,1:T(8,128)S(1)} %fusion.11, f32[384]{0:T(512)S(1)} %convert_reduce_fusion, bf16[384,3584]{1,0:T(8,128)(2,1)} %bitcast.50, ...), kind=kOutput, calls=%fused_computation.72 | convolution fusion | flops 353255040 | bytes 4360448 | tf_op jit(solution)/shard_map/rd,hd->rh/dot_general | solution.py:104
  122.6 2.7 %convolution_convert_fusion.2 = bf16[3584,128]{1,0:T(8,128)(2,1)S(1)} fusion(bf16[384,3584]{1,0:T(8,128)(2,1)} %bitcast.50, bf16[384,128]{0,1:T(8,128)(2,1)S(1)} %get-tuple-element.39, f32[384]{0:T(512)S(1)} %convert_reduce_fusion), kind=kOutput, calls=%fused_computation.6 | convolution fusion | flops 352927744 | bytes 3769856 | tf_op jit(solution)/shard_map/rd,rh->dh/dot_general | solution.py:104
  130.1 2.7 %collective-permute-start.11 = (bf16[48,3712]{1,0:T(8,128)(2,1)}, bf16[48,3712]{1,0:T(8,128)(2,1)}, u32[]{:S(2)}, u32[]{:S(2)}) collective-permute-start(bf16[48,3712]{1,0:T(8,128)(2,1)} %get-tuple-element.42), channel_id=1, source_target_pairs={{0,2},{2,4},{4,6},{6,0},{1,3},{3,5},{5,7},{7,1},{8,10},{10,12},{12... | collective-permute-start | bytes 1069064 | tf_op jit(solution)/shard_map/ppermute | solution.py:91
  132.8 4.5 %collective-permute-start.13 = (bf16[48,3712]{1,0:T(8,128)(2,1)}, bf16[48,3712]{1,0:T(8,128)(2,1)}, u32[]{:S(2)}, u32[]{:S(2)}) collective-permute-start(bf16[48,3712]{1,0:T(8,128)(2,1)} %get-tuple-element.44), channel_id=1, source_target_pairs={{0,6},{2,0},{4,2},{6,4},{1,7},{3,1},{5,3},{7,5},{8,14},{10,8},{12,... | collective-permute-start | bytes 1069064 | tf_op jit(solution)/shard_map/ppermute | solution.py:92
  137.3 1.9 pad_maximum_fusion.1
  145.1 5.4 %collective-permute-start.14 = (bf16[96,3712]{1,0:T(8,128)(2,1)}, bf16[96,3712]{1,0:T(8,128)(2,1)}, u32[]{:S(2)}, u32[]{:S(2)}) collective-permute-start(bf16[96,3712]{1,0:T(8,128)(2,1)} %pad_maximum_fusion.5), channel_id=1, source_target_pairs={{0,6},{2,0},{4,2},{6,4},{1,7},{3,1},{5,3},{7,5},{8,14},{10,8},{12,... | collective-permute-start | bytes 2138120 | tf_op jit(solution)/shard_map/ppermute | solution.py:96
  151.5 1.9 collective-permute-start.12
  154.7 4.8 %collective-permute-done.14 = bf16[96,3712]{1,0:T(8,128)(2,1)} collective-permute-done((bf16[96,3712]{1,0:T(8,128)(2,1)}, bf16[96,3712]{1,0:T(8,128)(2,1)}, u32[]{:S(2)}, u32[]{:S(2)}) %collective-permute-start.14) | collective-permute-done | bytes 712736 | tf_op jit(solution)/shard_map/ppermute | solution.py:96
  159.5 6.6 %collective-permute-done.12 = bf16[96,3712]{1,0:T(8,128)(2,1)} collective-permute-done((bf16[96,3712]{1,0:T(8,128)(2,1)}, bf16[96,3712]{1,0:T(8,128)(2,1)}, u32[]{:S(2)}, u32[]{:S(2)}) %collective-permute-start.12) | collective-permute-done | bytes 712736 | tf_op jit(solution)/shard_map/ppermute | solution.py:96
  166.1 3.0 %fusion.3 = bf16[16,8,3712]{2,1,0:T(8,128)(2,1)} fusion(bf16[128,288]{0,1:T(8,128)(2,1)S(1)} %bitcast.191, bf16[96,3712]{1,0:T(8,128)(2,1)} %collective-permute-done.14, bf16[96,3712]{1,0:T(8,128)(2,1)} %collective-permute-done.12, bf16[96,3712]{1,0:T(8,128)(2,1)S(1)} %dynamic-slice_bitcast_fusion), kind=kOutput, calls=%fused_computation.9 | convolution fusion | flops 280567808 | bytes 3162112 | tf_op jit(solution)/shard_map/ck,kd->cd/dot_general | solution.py:104
  169.1 12.5 %all-to-all-start.2 = ((bf16[16,8,3712]{2,1,0:T(8,128)(2,1)}), bf16[16,8,3712]{2,1,0:T(8,128)(2,1)}, u32[]{:S(2)}, u32[]{:S(2)}) async-start(bf16[16,8,3712]{2,1,0:T(8,128)(2,1)} %fusion.3), calls=%async_computation.3 | async-start | bytes 1900544 | tf_op jit(solution)/shard_map/all_to_all | solution.py:187
  185.1 17.7 %all-to-all-done.2 = bf16[16,8,3712]{2,1,0:T(8,128)(2,1)} async-done(((bf16[16,8,3712]{2,1,0:T(8,128)(2,1)}), bf16[16,8,3712]{2,1,0:T(8,128)(2,1)}, u32[]{:S(2)}, u32[]{:S(2)}) %all-to-all-start.2) | async-done | bytes 950304 | tf_op jit(solution)/shard_map/all_to_all | solution.py:187
  204.6 2.5 %convolution_convert_fusion = bf16[128,3584]{1,0:T(8,128)(2,1)} fusion(pred[128,128]{1,0:T(8,128)(4,1)S(1)} %bitcast.192, bf16[128,3712]{1,0:T(8,128)(2,1)} %bitcast.71), kind=kOutput, calls=%fused_computation.4 | convolution fusion | flops 117899264 | bytes 1851392 | tf_op jit(solution)/shard_map/ct,cd->td/dot_general | solution.py:104
  (111 shorter events, 41.4 us)
Async XLA Ops:
  7.2 2.6 %copy-start = (bf16[128,3584]{1,0:T(8,128)(2,1)S(1)}, bf16[128,3584]{1,0:T(8,128)(2,1)}, u32[]{:S(2)}) copy-start(bf16[128,3584]{1,0:T(8,128)(2,1)} %param.8) | copy-start | bytes 2752516
  7.2 15.6 %copy-start.9 = (bf16[1,3584,16]{1,2,0:T(8,128)(2,1)S(1)}, bf16[1,3584,16]{1,2,0:T(8,128)(2,1)}, u32[]{:S(2)}) copy-start(bf16[1,3584,16]{1,2,0:T(8,128)(2,1)} %param.13) | copy-start | bytes 344068
  7.2 15.6 %copy-start.10 = (bf16[1,3584,16]{1,2,0:T(8,128)(2,1)S(1)}, bf16[1,3584,16]{1,2,0:T(8,128)(2,1)}, u32[]{:S(2)}) copy-start(bf16[1,3584,16]{1,2,0:T(8,128)(2,1)} %param.12) | copy-start | bytes 344068
  7.2 15.6 %copy-start.11 = (bf16[1,3584,16]{1,2,0:T(8,128)(2,1)S(1)}, bf16[1,3584,16]{1,2,0:T(8,128)(2,1)}, u32[]{:S(2)}) copy-start(bf16[1,3584,16]{1,2,0:T(8,128)(2,1)} %param.11) | copy-start | bytes 344068
  12.5 24.4 %all-to-all-start = ((bf16[4,8,7296]{2,1,0:T(8,128)(2,1)}), bf16[4,8,7296]{2,1,0:T(8,128)(2,1)S(1)}, u32[]{:S(2)}, u32[]{:S(2)}) async-start(bf16[4,8,7296]{2,1,0:T(8,128)(2,1)} %maximum_bitcast_fusion), calls=%async_computation | async-start | bytes 933888 | tf_op jit(solution)/shard_map/all_to_all | solution.py:134
  22.8 71.9 %all-gather.2.cloned.1.call-start = ((), (), s32[]{:S(2)}) async-start(), calls=%async_computation.4 | async-start | bytes 3096576 | tf_op jit(solution)/shard_map/all_gather | solution.py:112
  37.1 15.4 %collective-permute-start.4 = (bf16[24,3584]{1,0:T(8,128)(2,1)S(1)}, bf16[24,3584]{1,0:T(8,128)(2,1)S(1)}, u32[]{:S(2)}, u32[]{:S(2)}) collective-permute-start(bf16[24,3584]{1,0:T(8,128)(2,1)S(1)} %get-tuple-element.59), channel_id=1, source_target_pairs={{0,1},{1,0},{8,9},{9,8},{2,3},{3,2},{10,11},{11,10},{4,5},{5,4},{1... | collective-permute-start | bytes 516104 | tf_op jit(solution)/shard_map/ppermute | solution.py:41
  39.7 12.9 %collective-permute-start.5 = (bf16[24,3584]{1,0:T(8,128)(2,1)S(1)}, bf16[24,3584]{1,0:T(8,128)(2,1)S(1)}, u32[]{:S(2)}, u32[]{:S(2)}) collective-permute-start(bf16[24,3584]{1,0:T(8,128)(2,1)S(1)} %get-tuple-element.59), channel_id=1, source_target_pairs={{0,8},{1,9},{8,0},{9,1},{2,10},{3,11},{10,2},{11,3},{4,12},{5,13},... | collective-permute-start | bytes 516104 | tf_op jit(solution)/shard_map/ppermute | solution.py:41
  44.4 20.3 %collective-permute-start.6 = (bf16[24,3584]{1,0:T(8,128)(2,1)S(1)}, bf16[24,3584]{1,0:T(8,128)(2,1)S(1)}, u32[]{:S(2)}, u32[]{:S(2)}) collective-permute-start(bf16[24,3584]{1,0:T(8,128)(2,1)S(1)} %get-tuple-element.59), channel_id=1, source_target_pairs={{0,9},{1,8},{8,1},{9,0},{2,11},{3,10},{10,3},{11,2},{4,13},{5,12},... | collective-permute-start | bytes 516104 | tf_op jit(solution)/shard_map/ppermute | solution.py:41
  48.3 26.3 %all-to-all-start.1 = ((bf16[4,24,3712]{2,1,0:T(8,128)(2,1)}), bf16[4,24,3712]{2,1,0:T(8,128)(2,1)S(1)}, u32[]{:S(2)}, u32[]{:S(2)}) async-start(bf16[4,24,3712]{2,1,0:T(8,128)(2,1)} %broadcast_in_dim.127), calls=%async_computation.1 | async-start | bytes 1425408 | tf_op jit(solution)/shard_map/all_to_all | solution.py:20
  52.6 154.5 %reduce-scatter.2.cloned.1.call-start = ((), (), s32[]{:S(2)}) async-start(), calls=%async_computation.5 | async-start | bytes 3096576 | tf_op jit(solution)/shard_map/reduce_scatter | solution.py:176
  64.7 15.6 %collective-permute-start.7 = (bf16[96,3584]{1,0:T(8,128)(2,1)S(1)}, bf16[96,3584]{1,0:T(8,128)(2,1)S(1)}, u32[]{:S(2)}, u32[]{:S(2)}) collective-permute-start(bf16[96,3584]{1,0:T(8,128)(2,1)S(1)} %bitcast.177), channel_id=1, source_target_pairs={{0,2},{2,4},{4,6},{6,0},{1,3},{3,5},{5,7},{7,1},{8,10},{10,12},{12... | collective-permute-start | bytes 2064392 | tf_op jit(solution)/shard_map/ppermute | solution.py:72
  68.2 14.4 %collective-permute-start.8 = (bf16[96,3584]{1,0:T(8,128)(2,1)S(1)}, bf16[96,3584]{1,0:T(8,128)(2,1)}, u32[]{:S(2)}, u32[]{:S(2)}) collective-permute-start(bf16[96,3584]{1,0:T(8,128)(2,1)S(1)} %bitcast.178), channel_id=1, source_target_pairs={{0,6},{2,0},{4,2},{6,4},{1,7},{3,1},{5,3},{7,5},{8,14},{10,8},{12,... | collective-permute-start | bytes 2064392 | tf_op jit(solution)/shard_map/ppermute | solution.py:73
  75.5 18.5 %collective-permute-start = (bf16[2,24,3712]{2,1,0:T(8,128)(2,1)S(1)}, bf16[2,24,3712]{2,1,0:T(8,128)(2,1)S(1)}, u32[]{:S(2)}, u32[]{:S(2)}) collective-permute-start(bf16[2,24,3712]{2,1,0:T(8,128)(2,1)S(1)} %get-tuple-element.52), channel_id=1, source_target_pairs={{0,8},{8,0},{1,9},{9,1},{2,10},{10,2},{3,11},{11,3},{4,12},{12,4},... | collective-permute-start | bytes 1069064 | tf_op jit(solution)/shard_map/ppermute | solution.py:49
  77.4 17.3 %collective-permute-start.1 = (bf16[2,24,3712]{2,1,0:T(8,128)(2,1)S(1)}, bf16[2,24,3712]{2,1,0:T(8,128)(2,1)S(1)}, u32[]{:S(2)}, u32[]{:S(2)}) collective-permute-start(bf16[2,24,3712]{2,1,0:T(8,128)(2,1)S(1)} %get-tuple-element.51), channel_id=1, source_target_pairs={{0,1},{1,0},{2,3},{3,2},{4,5},{5,4},{6,7},{7,6},{8,9},{9,8},{10,11... | collective-permute-start | bytes 1069064 | tf_op jit(solution)/shard_map/ppermute | solution.py:50
  80.3 13.6 %copy-start.2 = (bf16[4,4,24,3712]{3,2,1,0:T(8,128)(2,1)}, bf16[4,4,24,3712]{3,2,1,0:T(8,128)(2,1)S(1)}, u32[]{:S(2)}) copy-start(bf16[4,4,24,3712]{3,2,1,0:T(8,128)(2,1)S(1)} %bitcast_dynamic-update-slice_fusion) | copy-start | bytes 8552452
  80.3 11.1 %collective-permute-start.9 = (bf16[48,3584]{1,0:T(8,128)(2,1)S(1)}, bf16[48,3584]{1,0:T(8,128)(2,1)S(1)}, u32[]{:S(2)}, u32[]{:S(2)}) collective-permute-start(bf16[48,3584]{1,0:T(8,128)(2,1)S(1)} %slice.147), channel_id=1, source_target_pairs={{0,2},{2,4},{4,6},{6,0},{1,3},{3,5},{5,7},{7,1},{8,10},{10,12},{12... | collective-permute-start | bytes 1032200 | tf_op jit(solution)/shard_map/ppermute | solution.py:74
  83.6 9.6 %collective-permute-start.10 = (bf16[48,3584]{1,0:T(8,128)(2,1)S(1)}, bf16[48,3584]{1,0:T(8,128)(2,1)S(1)}, u32[]{:S(2)}, u32[]{:S(2)}) collective-permute-start(bf16[48,3584]{1,0:T(8,128)(2,1)S(1)} %slice.148), channel_id=1, source_target_pairs={{0,6},{2,0},{4,2},{6,4},{1,7},{3,1},{5,3},{7,5},{8,14},{10,8},{12,... | collective-permute-start | bytes 1032200 | tf_op jit(solution)/shard_map/ppermute | solution.py:75
  94.7 2.6 %copy-start.3 = (bf16[4,4,24,3712]{3,2,1,0:T(8,128)(2,1)S(1)}, bf16[4,4,24,3712]{3,2,1,0:T(8,128)(2,1)}, u32[]{:S(2)}) copy-start(bf16[4,4,24,3712]{3,2,1,0:T(8,128)(2,1)} %copy-done.2) | copy-start | bytes 8552452
  94.7 2.7 %copy-start.5 = (bf16[2,24,3712]{2,1,0:T(8,128)(2,1)S(1)}, bf16[2,24,3712]{2,1,0:T(8,128)(2,1)}, u32[]{:S(2)}) copy-start(bf16[2,24,3712]{2,1,0:T(8,128)(2,1)} %copy-done.4) | copy-start | bytes 1069060
  94.7 2.8 %copy-start.7 = (bf16[1,2,24,3712]{3,2,1,0:T(8,128)(2,1)S(1)}, bf16[1,2,24,3712]{3,2,1,0:T(8,128)(2,1)}, u32[]{:S(2)}) copy-start(bf16[1,2,24,3712]{3,2,1,0:T(8,128)(2,1)} %get-tuple-element.50) | copy-start | bytes 1069060
  94.7 7.0 %copy-start.6 = (bf16[1,2,24,3712]{3,2,1,0:T(8,128)(2,1)S(1)}, bf16[1,2,24,3712]{3,2,1,0:T(8,128)(2,1)}, u32[]{:S(2)}) copy-start(bf16[1,2,24,3712]{3,2,1,0:T(8,128)(2,1)} %get-tuple-element.49) | copy-start | bytes 1069060
  97.3 20.7 %copy-start.8 = (bf16[8,1,16,3584]{3,2,1,0:T(8,128)(2,1)}, bf16[8,1,16,3584]{3,2,1,0:T(8,128)(2,1)S(1)}, u32[]{:S(2)}) copy-start(bf16[8,1,16,3584]{3,2,1,0:T(8,128)(2,1)S(1)} %get-tuple-element.46) | copy-start | bytes 2752516
  97.5 14.8 %collective-permute-start.2 = (bf16[2,2,24,3712]{3,2,1,0:T(8,128)(2,1)S(1)}, bf16[2,2,24,3712]{3,2,1,0:T(8,128)(2,1)S(1)}, u32[]{:S(2)}, u32[]{:S(2)}) collective-permute-start(bf16[2,2,24,3712]{3,2,1,0:T(8,128)(2,1)S(1)} %pad_maximum_fusion.2), channel_id=1, source_target_pairs={{0,1},{1,0},{2,3},{3,2},{4,5},{5,4},{6,7},{7,6},{8,9},{9,8},{10,11... | collective-permute-start | bytes 2138120 | tf_op jit(solution)/shard_map/ppermute | solution.py:52
  101.8 14.2 %collective-permute-start.3 = (bf16[2,2,24,3712]{3,2,1,0:T(8,128)(2,1)S(1)}, bf16[2,2,24,3712]{3,2,1,0:T(8,128)(2,1)S(1)}, u32[]{:S(2)}, u32[]{:S(2)}) collective-permute-start(bf16[2,2,24,3712]{3,2,1,0:T(8,128)(2,1)S(1)} %pad_maximum_fusion.3), channel_id=1, source_target_pairs={{0,8},{8,0},{1,9},{9,1},{2,10},{10,2},{3,11},{11,3},{4,12},{12,4},... | collective-permute-start | bytes 2138120 | tf_op jit(solution)/shard_map/ppermute | solution.py:53
  127.5 1.6 copy-start.1
  130.1 11.0 %collective-permute-start.11 = (bf16[48,3712]{1,0:T(8,128)(2,1)}, bf16[48,3712]{1,0:T(8,128)(2,1)}, u32[]{:S(2)}, u32[]{:S(2)}) collective-permute-start(bf16[48,3712]{1,0:T(8,128)(2,1)} %get-tuple-element.42), channel_id=1, source_target_pairs={{0,2},{2,4},{4,6},{6,0},{1,3},{3,5},{5,7},{7,1},{8,10},{10,12},{12... | collective-permute-start | bytes 1069064 | tf_op jit(solution)/shard_map/ppermute | solution.py:91
  132.8 9.9 %collective-permute-start.13 = (bf16[48,3712]{1,0:T(8,128)(2,1)}, bf16[48,3712]{1,0:T(8,128)(2,1)}, u32[]{:S(2)}, u32[]{:S(2)}) collective-permute-start(bf16[48,3712]{1,0:T(8,128)(2,1)} %get-tuple-element.44), channel_id=1, source_target_pairs={{0,6},{2,0},{4,2},{6,4},{1,7},{3,1},{5,3},{7,5},{8,14},{10,8},{12,... | collective-permute-start | bytes 1069064 | tf_op jit(solution)/shard_map/ppermute | solution.py:92
  145.1 14.4 %collective-permute-start.14 = (bf16[96,3712]{1,0:T(8,128)(2,1)}, bf16[96,3712]{1,0:T(8,128)(2,1)}, u32[]{:S(2)}, u32[]{:S(2)}) collective-permute-start(bf16[96,3712]{1,0:T(8,128)(2,1)} %pad_maximum_fusion.5), channel_id=1, source_target_pairs={{0,6},{2,0},{4,2},{6,4},{1,7},{3,1},{5,3},{7,5},{8,14},{10,8},{12,... | collective-permute-start | bytes 2138120 | tf_op jit(solution)/shard_map/ppermute | solution.py:96
  151.5 14.6 %collective-permute-start.12 = (bf16[96,3712]{1,0:T(8,128)(2,1)}, bf16[96,3712]{1,0:T(8,128)(2,1)}, u32[]{:S(2)}, u32[]{:S(2)}) collective-permute-start(bf16[96,3712]{1,0:T(8,128)(2,1)} %pad_maximum_fusion.4), channel_id=1, source_target_pairs={{0,2},{2,4},{4,6},{6,0},{1,3},{3,5},{5,7},{7,1},{8,10},{10,12},{12... | collective-permute-start | bytes 2138120 | tf_op jit(solution)/shard_map/ppermute | solution.py:96
  169.1 34.7 %copy-start.12 = (s32[128,8]{0,1:T(8,128)S(1)}, s32[128,8]{0,1:T(8,128)}, u32[]{:S(2)}) copy-start(s32[128,8]{0,1:T(8,128)} %param.9) | copy-start | bytes 12292
  169.1 33.7 %all-to-all-start.2 = ((bf16[16,8,3712]{2,1,0:T(8,128)(2,1)}), bf16[16,8,3712]{2,1,0:T(8,128)(2,1)}, u32[]{:S(2)}, u32[]{:S(2)}) async-start(bf16[16,8,3712]{2,1,0:T(8,128)(2,1)} %fusion.3), calls=%async_computation.3 | async-start | bytes 1900544 | tf_op jit(solution)/shard_map/all_to_all | solution.py:187
  (1 other events, 0.7 us)
Sparse Core Ops, SparseCore 0:
  25.7 45.9 all-gather.1
  139.4 56.0 reduce-scatter.1

commit v4 on v1

--- a/solution.py
+++ b/solution.py
@@ -10,7 +10,6 @@
 EXPERTS = 4
 LANES = 128
 DP = ("yh", "core")
-COLOR_A = ("zl", "yl", "x")
 BF = jnp.bfloat16
 F32 = jnp.float32
 
@@ -33,7 +32,6 @@
     mine = jnp.concatenate([w_gate[0].T, w_up[0].T, w_down[0].T], axis=0)
     gathered = lax.all_gather(mine, DP, axis=0, tiled=True)
     n_dp = lax.axis_size(DP)
-    gathered = gathered.reshape(n_dp, 3, hidden_dev, features)
 
     ids = route_ids.T
     gates_t = gates.T.astype(F32)
@@ -64,37 +62,38 @@
     tok_rows = dot("kc,cd->kd", keep, rows[:, :wide]).astype(BF)
     cot_rows = dot("kc,cd->kd", keep, rows[:, wide:]).astype(BF)
 
-    tok_half = spread(tok_rows, "x")
-    cot_half = spread(cot_rows, ("zl", "yl"))
+    block = EXPERTS * CAP
+    tok_half = lax.all_gather(tok_rows, "x", axis=0, tiled=True)
+    cot_half = lax.all_gather(cot_rows, ("zl", "yl"), axis=0, tiled=True)
+    cot_half, gathered = lax.optimization_barrier((cot_half, gathered))
     slot_all = spread(tok_half, ("zl", "yl"))
-    slot_cotan = spread(cot_half, "x")
+    slot_cotan = lax.all_gather(cot_half, "x", axis=0, tiled=True)
     slot_tokens = slot_all[:, :features]
-    slot_gates = slot_all[:, features : features + 1].astype(F32)
+    gathered = gathered.reshape(n_dp, 3, hidden_dev, features)
 
-    block = EXPERTS * CAP
-
-    def to_tok_order(values):
+    def reorder(values):
         v = values.reshape(4, 4, block, values.shape[-1])
         return jnp.swapaxes(v, 0, 1).reshape(values.shape)
 
     slab = [gathered[:, j].reshape(n_dp * hidden_dev, features) for j in range(3)]
     gate_slab, up_slab, down_slab = slab
-    pre_gate = dot("rd,hd->rh", slot_tokens, gate_slab)
-    pre_up = dot("rd,hd->rh", slot_tokens, up_slab)
+    pre_gate = reorder(dot("rd,hd->rh", slot_tokens, gate_slab))
+    pre_up = reorder(dot("rd,hd->rh", slot_tokens, up_slab))
+    slot_gates = reorder(slot_all[:, features : features + 1]).astype(F32)
     sigmoid_gate = jax.nn.sigmoid(pre_gate)
     activation = pre_gate * sigmoid_gate
     hidden = (activation * pre_up).astype(BF)
-    back_proj = to_tok_order(dot("rd,hd->rh", slot_cotan, down_slab))
+    back_proj = dot("rd,hd->rh", slot_cotan, down_slab)
     score = jnp.sum(hidden.astype(F32) * back_proj, axis=1, keepdims=True).astype(BF)
     scaled = slot_gates * back_proj
     d_gate = (scaled * pre_up * sigmoid_gate * (1.0 + pre_gate * (1.0 - sigmoid_gate))).astype(BF)
     d_up = (scaled * activation).astype(BF)
-    hidden_gated = to_tok_order((slot_gates * hidden.astype(F32)).astype(BF))
+    hidden_gated = (slot_gates * hidden.astype(F32)).astype(BF)
 
     grads = jnp.stack(
         [
-            dot("rd,rh->dh", slot_tokens, d_gate).astype(BF).reshape(n_dp, -1, LANES),
-            dot("rd,rh->dh", slot_tokens, d_up).astype(BF).reshape(n_dp, -1, LANES),
+            dot("rd,rh->dh", slot_tokens, reorder(d_gate)).astype(BF).reshape(n_dp, -1, LANES),
+            dot("rd,rh->dh", slot_tokens, reorder(d_up)).astype(BF).reshape(n_dp, -1, LANES),
             dot("rd,rh->dh", slot_cotan, hidden_gated).astype(BF).reshape(n_dp, -1, LANES),
         ],
         axis=1,
@@ -105,22 +104,22 @@
         dot("rh,hd->rd", d_gate, gate_slab) + dot("rh,hd->rd", d_up, up_slab)
     ).astype(BF)
     back = jnp.concatenate([partial, jnp.broadcast_to(score, (score.shape[0], LANES))], axis=1)
-    back = back.reshape(HSPLIT, block, -1)
-    back = lax.all_to_all(back, COLOR_A, split_axis=0, concat_axis=0, tiled=True)
-    back = back.reshape(HSPLIT * block, -1)
-    fold = jnp.tile(keep.T, (1, HSPLIT))
-    summed = dot("ck,kd->cd", fold, back)
-    score_sum = summed[:, features:]
-    high = lax.reduce_precision(score_sum, 8, 7)
-    lane = jnp.arange(LANES)[None, :]
-    score_cols = jnp.where(lane < LANES // 2, high, score_sum - high)
-    home = jnp.concatenate([summed[:, :features], score_cols], axis=1).astype(BF)
+    back = back.reshape(8, 2 * block, wide)
+    back = lax.all_to_all(back, ("x", "zl"), split_axis=0, concat_axis=0, tiled=True)
+    back = back.reshape(HSPLIT * block, wide)
+    row = jnp.arange(2 * block)
+    target = (row // CAP % EXPERTS * 2 + row // block) * PAD + row % CAP
+    fold = (jnp.arange(2 * EXPERTS * PAD)[:, None] == target[None, :]).astype(BF)
+    home = dot("ck,kd->cd", jnp.tile(fold, (1, 8)), back).astype(BF)
     home = lax.all_to_all(
-        home.reshape(EXPERTS, PAD, -1), "ex", split_axis=0, concat_axis=0, tiled=True
-    ).reshape(EXPERTS * PAD, -1)
-    token_grad = dot("ct,cd->td", pick_rows, home[:, :features]).astype(BF)
-    pair = home[:, features:].astype(F32)
-    score_slots = (pair[:, :1] + pair[:, LANES // 2 : LANES // 2 + 1]).reshape(EXPERTS, PAD, 1)
+        home.reshape(2 * EXPERTS, PAD, wide), ("ex", "yl"), split_axis=0, concat_axis=0, tiled=True
+    ).reshape(2 * EXPERTS * PAD, wide)
+    pick_home = jnp.broadcast_to(pick[:, None], (EXPERTS, 2, PAD, tok_count))
+    pick_home = pick_home.reshape(2 * EXPERTS * PAD, tok_count).astype(BF)
+    token_grad = dot("ct,cd->td", pick_home, home[:, :features]).astype(BF)
+    score_slots = jnp.sum(
+        home[:, features : features + 1].astype(F32).reshape(EXPERTS, 2, PAD, 1), axis=1
+    )
     score_token = jnp.sum(jnp.where(pick, score_slots, 0.0), axis=1)
     gate_grad = jnp.sum(jnp.where(hits, score_token[:, None, :], 0.0), axis=0).T
 

time: 240 us -> 235 us (0.979)
  blocking collectives: 16.1 us -> 55.2 us
  waiting for transfers between devices: 119 us -> 86.9 us
  starting transfers between devices: 39.2 us -> 32.1 us
    all_gather x0 -> x2, blocking collectives: none -> 55.2 us  [the longest x1 43.4 us: shards(): cot_half = lax.all_gather(cot_rows, ('zl', 'yl'), axis=0, tiled=True)]
    all_to_all x3 -> x1, waiting for transfers between devices: 53.1 us -> 0.01 us  [spread(): got = lax.all_to_all(copies, axes, split_axis=0, concat_axis=0, tiled=True)]
    all_gather x0 -> x1, waiting for transfers between devices: none -> 34.9 us  [shards(): slot_cotan = lax.all_gather(cot_half, 'x', axis=0, tiled=True)]
    all_gather x1, waiting for transfers between devices: 17.7 us -> 0.01 us  [shards(): gathered = lax.all_gather(mine, DP, axis=0, tiled=True)]
    all_to_all x1 -> x0, blocking collectives: 16.1 us -> none  [spread(): got = lax.all_to_all(copies, axes, split_axis=0, concat_axis=0, tiled=True)]
    all_to_all x3 -> x1, starting transfers between devices: 13.4 us -> 8.7 us  [spread(): got = lax.all_to_all(copies, axes, split_axis=0, concat_axis=0, tiled=True)]
    reduce_scatter x1, waiting for transfers between devices: 9.74 us -> 14.2 us  [shards(): lax.psum_scatter(grads, DP, scatter_dimension=0, tiled=True)[0].astype(F32)]
    broadcast_in_dim x4 -> x1, local copies, waits for them, and re-layouts: 4.46 us -> 1.82 us  [spread(): copies = jnp.broadcast_to(block[None], (count,) + block.shape)]
  transfers between devices with their start and end apart: 8 -> 7, of which waited for: 7 -> 4; matrix products, arithmetic and copies ran while one was open for 11% -> 13% of each run, Pallas kernels for 0% -> 0%
where the time goes in v4:
time: 235 us; the launch traced here: 234 us
  waiting for transfers between devices  86.9 us (37%)
  blocking collectives  55.2 us (23%)
  starting transfers between devices  32.1 us (14%)
  matrix products  22.6 us (10%)
  between operations  14 us (6%)
  local copies, waits for them, and re-layouts  11.6 us (5%)
  other arithmetic  11.4 us (5%)
    all_gather x1, blocking collectives, shards(): cot_half = lax.all_gather(cot_rows, ('zl', 'yl'), axis=0, tiled=True)  43.4 us
    all_gather x1, waiting for transfers between devices, shards(): slot_cotan = lax.all_gather(cot_half, 'x', axis=0, tiled=True)  34.9 us
    all_to_all x1, waiting for transfers between devices, shards(): lax.all_to_all(back, ('x', 'zl'), split_axis=0, concat_axis=0, tiled=True)  26.9 us
    dot_general x15, matrix products, dot(): return jnp.einsum(eq, a, b, preferred_element_type=F32)  22.6 us
    reduce_scatter x1, waiting for transfers between devices, shards(): lax.psum_scatter(grads, DP, scatter_dimension=0, tiled=True)[0].astype(F32)  14.2 us
    all_gather x1, blocking collectives, shards(): tok_half = lax.all_gather(tok_rows, 'x', axis=0, tiled=True)  11.8 us
    all_to_all x1, starting transfers between devices, shards(): rows = lax.all_to_all(rows, 'ex', split_axis=0, concat_axis=0, tiled=True)  10.8 us
    all_to_all x1, waiting for transfers between devices, shards(): rows = lax.all_to_all(rows, 'ex', split_axis=0, concat_axis=0, tiled=True)  10.8 us
  transfers between devices with their start and end apart: 7, of which 4 were waited for; matrix products, arithmetic and copies ran while one was open for 13% of the time, Pallas kernels for 0%

profile of v4, /device:TPU:1, one launch (start us, length us, event | category | flops | bytes accessed | tf_op | source)
XLA Modules:
  0.0 233.8 jit_solution(6626532098649604289)
XLA Ops:
  7.2 1.9 pad_maximum_fusion.2
  11.9 1.5 convolution_convert_fusion.5
  13.5 0.8 maximum_bitcast_fusion
  14.3 10.8 %all-to-all-start = ((bf16[4,8,7296]{2,1,0:T(8,128)(2,1)}), bf16[4,8,7296]{2,1,0:T(8,128)(2,1)S(1)}, u32[]{:S(2)}, u32[]{:S(2)}) async-start(bf16[4,8,7296]{2,1,0:T(8,128)(2,1)} %maximum_bitcast_fusion), calls=%async_computation | async-start | bytes 933888 | tf_op jit(solution)/shard_map/all_to_all | solution.py:55
  25.1 10.8 %all-to-all-done = bf16[4,8,7296]{2,1,0:T(8,128)(2,1)S(1)} async-done(((bf16[4,8,7296]{2,1,0:T(8,128)(2,1)}), bf16[4,8,7296]{2,1,0:T(8,128)(2,1)S(1)}, u32[]{:S(2)}, u32[]{:S(2)}) %all-to-all-start) | async-done | bytes 466976 | tf_op jit(solution)/shard_map/all_to_all | solution.py:55
  36.2 11.8 %all_gather.14 = bf16[96,3712]{1,0:T(8,128)(2,1)S(1)} all-gather(bf16[24,3712]{1,0:T(8,128)(2,1)S(1)} %convolution_convert_fusion.6), channel_id=1, replica_groups=mesh['yh'=4,'core'=2,'ex'=4,'zl'=2,'x'=4,'yl'=2] {'x'}, dimensions={0}, use_global_device_ids=true | all-gather | bytes 890880 | tf_op jit(solution)/shard_map/all_gather | solution.py:66
  48.1 1.8 broadcast_in_dim.91
  49.9 8.7 %all-to-all-start.1 = ((bf16[4,96,3712]{2,1,0:T(8,128)(2,1)}), bf16[4,96,3712]{2,1,0:T(8,128)(2,1)}, u32[]{:S(2)}, u32[]{:S(2)}) async-start(bf16[4,96,3712]{2,1,0:T(8,128)(2,1)} %broadcast_in_dim.91), calls=%async_computation.1 | async-start | bytes 5701632 | tf_op jit(solution)/shard_map/all_to_all | solution.py:20
  58.8 43.4 %all_gather.12 = bf16[96,3584]{1,0:T(8,128)(2,1)} all-gather(bf16[24,3584]{1,0:T(8,128)(2,1)S(1)} %convolution_convert_fusion.7), channel_id=1, replica_groups=mesh['yh'=4,'core'=2,'ex'=4,'zl'=2,'x'=4,'yl'=2] {'zl','yl'}, dimensions={0}, use_global_device_ids=true | all-gather | bytes 860160 | tf_op jit(solution)/shard_map/all_gather | solution.py:67
  102.2 2.8 %fusion.57 = (bf16[8,1,16,3584]{3,2,1,0:T(8,128)(2,1)}, bf16[8,1,16,3584]{3,2,1,0:T(8,128)(2,1)S(1)}, bf16[8,1,16,3584]{3,2,1,0:T(8,128)(2,1)S(1)}) fusion(bf16[8,3,16,3584]{3,2,1,0:T(8,128)(2,1)} %bitcast.156), kind=kLoop, calls=%fused_computation.110 | loop fusion | bytes 5505024 | tf_op jit(solution)/shard_map/slice | solution.py:78
  105.1 2.0 slice.65
  107.0 0.9 convolution_bitcast_fusion.2
  107.9 0.9 convolution_bitcast_fusion.1
  108.8 1.0 convert_reduce_fusion
  110.1 34.9 %all-gather.5.cloned.1.call-done = bf16[384,3584]{1,0:T(8,128)(2,1)} async-done(((bf16[96,3584]{1,0:T(8,128)(2,1)}), bf16[384,3584]{1,0:T(8,128)(2,1)}) %all-gather.5.cloned.1.call-update) | async-done | bytes 2752528 | tf_op jit(solution)/shard_map/all_gather | solution.py:70
  145.0 3.0 %fusion.11 = (bf16[384]{0:T(512)(128)(2,1)S(1)}, bf16[384,128]{1,0:T(8,128)(2,1)S(1)}, bf16[384,128]{1,0:T(8,128)(2,1)S(1)}, bf16[384,128]{1,0:T(8,128)(2,1)S(1)}) fusion(f32[4,4,24,128]{3,2,1,0:T(8,128)S(1)} %copy.51, f32[4,4,24,128]{3,2,1,0:T(8,128)S(1)} %copy.52, f32[384]{0:T(512)S(1)} %reshape.213, bf16[384,3584]{1,0:T(8,128)(2,1)} %all-gather.5.cloned.1.call-done, ...), kind=kOutput, calls=%fused_computation.33 | convolution fusion | flops 353255040 | bytes 4360448 | tf_op jit(solution)/shard_map/rd,hd->rh/dot_general | solution.py:25
  148.0 3.6 %convolution_convert_fusion.2 = bf16[3584,128]{1,0:T(8,128)(2,1)} fusion(bf16[384,128]{1,0:T(8,128)(2,1)S(1)} %bitcast.171, bf16[384,3712]{1,0:T(8,128)(2,1)} %bitcast.22), kind=kOutput, calls=%fused_computation.6 | convolution fusion | flops 352780288 | bytes 3768320 | tf_op jit(solution)/shard_map/rd,rh->dh/dot_general | solution.py:25
  151.6 0.9 fusion.60
  152.5 0.9 fusion.2
  153.5 1.8 pad_maximum_fusion
  155.2 4.4 %all-to-all-start.2 = ((bf16[8,48,3712]{2,1,0:T(8,128)(2,1)}), bf16[8,48,3712]{2,1,0:T(8,128)(2,1)}, u32[]{:S(2)}, u32[]{:S(2)}) async-start(bf16[8,48,3712]{2,1,0:T(8,128)(2,1)} %bitcast.148), calls=%async_computation.3 | async-start | bytes 5701632 | tf_op jit(solution)/shard_map/all_to_all | solution.py:108
  159.7 2.8 %convolution_convert_fusion.1 = bf16[3584,128]{1,0:T(8,128)(2,1)S(1)} fusion(bf16[384,3584]{1,0:T(8,128)(2,1)} %all-gather.5.cloned.1.call-done, bf16[384,128]{1,0:T(8,128)(2,1)S(1)} %get-tuple-element.45, f32[384]{0:T(512)S(1)} %reshape.213), kind=kOutput, calls=%fused_computation.5 | convolution fusion | flops 352927744 | bytes 3769856 | tf_op jit(solution)/shard_map/rd,rh->dh/dot_general | solution.py:25
  162.5 2.8 %convolution_convert_fusion.3 = bf16[3584,128]{1,0:T(8,128)(2,1)S(1)} fusion(bf16[384,128]{1,0:T(8,128)(2,1)S(1)} %bitcast.170, bf16[384,3712]{1,0:T(8,128)(2,1)} %bitcast.22), kind=kOutput, calls=%fused_computation.7 | convolution fusion | flops 352780288 | bytes 3768320 | tf_op jit(solution)/shard_map/rd,rh->dh/dot_general | solution.py:25
  165.3 1.9 pad_maximum_fusion.1
  167.3 26.9 %all-to-all-done.2 = bf16[8,48,3712]{2,1,0:T(8,128)(2,1)} async-done(((bf16[8,48,3712]{2,1,0:T(8,128)(2,1)}), bf16[8,48,3712]{2,1,0:T(8,128)(2,1)}, u32[]{:S(2)}, u32[]{:S(2)}) %all-to-all-start.2) | async-done | bytes 2850848 | tf_op jit(solution)/shard_map/all_to_all | solution.py:108
  194.2 3.2 %fusion.4 = bf16[8,8,3712]{2,1,0:T(8,128)(2,1)} fusion(bf16[8,48,3712]{2,1,0:T(8,128)(2,1)} %all-to-all-done.2, bf16[64,48]{0,1:T(8,128)(2,1)S(1)} %fusion.23), kind=kOutput, calls=%fused_computation.10 | convolution fusion | flops 182689792 | bytes 3332096 | tf_op jit(solution)/shard_map/ck,kd->cd/dot_general | solution.py:25
  197.4 8.0 %all-to-all-start.3 = ((bf16[8,8,3712]{2,1,0:T(8,128)(2,1)}), bf16[8,8,3712]{2,1,0:T(8,128)(2,1)S(1)}, u32[]{:S(2)}, u32[]{:S(2)}) async-start(bf16[8,8,3712]{2,1,0:T(8,128)(2,1)} %fusion.4), calls=%async_computation.4 | async-start | bytes 950272 | tf_op jit(solution)/shard_map/all_to_all | solution.py:114
  206.3 1.1 dynamic-slice_bitcast_fusion
  208.9 14.2 %reduce-scatter.2.cloned.1.call-done = bf16[1,3,448,128]{3,2,1,0:T(8,128)(2,1)} async-done(((bf16[8,3,448,128]{3,2,1,0:T(8,128)(2,1)}), bf16[1,3,448,128]{3,2,1,0:T(8,128)(2,1)}) %reduce-scatter.2.cloned.1.call-update) | async-done | bytes 344080 | tf_op jit(solution)/shard_map/reduce_scatter | solution.py:101
  223.1 1.0 convert_element_type.128
  224.2 0.9 slice_bitcast_fusion
  225.1 1.4 convolution_convert_fusion
  (47 shorter events, 7.3 us)
Async XLA Ops:
  7.2 4.4 %copy-start = (bf16[128,3584]{1,0:T(8,128)(2,1)S(1)}, bf16[128,3584]{1,0:T(8,128)(2,1)}, u32[]{:S(2)}) copy-start(bf16[128,3584]{1,0:T(8,128)(2,1)} %param.8) | copy-start | bytes 2752516
  7.2 95.0 %all-gather.3.cloned.1.call-start = ((), (), s32[]{:S(2)}) async-start(), calls=%async_computation.5 | async-start | bytes 3096576 | tf_op jit(solution)/shard_map/all_gather | solution.py:33
  14.3 21.7 %all-to-all-start = ((bf16[4,8,7296]{2,1,0:T(8,128)(2,1)}), bf16[4,8,7296]{2,1,0:T(8,128)(2,1)S(1)}, u32[]{:S(2)}, u32[]{:S(2)}) async-start(bf16[4,8,7296]{2,1,0:T(8,128)(2,1)} %maximum_bitcast_fusion), calls=%async_computation | async-start | bytes 933888 | tf_op jit(solution)/shard_map/all_to_all | solution.py:55
  49.9 55.2 %all-to-all-start.1 = ((bf16[4,96,3712]{2,1,0:T(8,128)(2,1)}), bf16[4,96,3712]{2,1,0:T(8,128)(2,1)}, u32[]{:S(2)}, u32[]{:S(2)}) async-start(bf16[4,96,3712]{2,1,0:T(8,128)(2,1)} %broadcast_in_dim.91), calls=%async_computation.1 | async-start | bytes 5701632 | tf_op jit(solution)/shard_map/all_to_all | solution.py:20
  58.6 86.4 %all-gather.5.cloned.1.call-start = ((), (), s32[]{:S(2)}) async-start(), calls=%async_computation.6 | async-start | bytes 3440640 | tf_op jit(solution)/shard_map/all_gather | solution.py:70
  155.2 38.9 %all-to-all-start.2 = ((bf16[8,48,3712]{2,1,0:T(8,128)(2,1)}), bf16[8,48,3712]{2,1,0:T(8,128)(2,1)}, u32[]{:S(2)}, u32[]{:S(2)}) async-start(bf16[8,48,3712]{2,1,0:T(8,128)(2,1)} %bitcast.148), calls=%async_computation.3 | async-start | bytes 5701632 | tf_op jit(solution)/shard_map/all_to_all | solution.py:108
  159.7 63.5 %reduce-scatter.2.cloned.1.call-start = ((), (), s32[]{:S(2)}) async-start(), calls=%async_computation.7 | async-start | bytes 3096576 | tf_op jit(solution)/shard_map/reduce_scatter | solution.py:101
  162.5 2.8 %copy-start.1 = (bf16[3584,128]{1,0:T(8,128)(2,1)S(1)}, bf16[3584,128]{1,0:T(8,128)(2,1)}, u32[]{:S(2)}) copy-start(bf16[3584,128]{1,0:T(8,128)(2,1)} %convolution_convert_fusion.2) | copy-start | bytes 2752516
  197.4 27.7 %all-to-all-start.3 = ((bf16[8,8,3712]{2,1,0:T(8,128)(2,1)}), bf16[8,8,3712]{2,1,0:T(8,128)(2,1)S(1)}, u32[]{:S(2)}, u32[]{:S(2)}) async-start(bf16[8,8,3712]{2,1,0:T(8,128)(2,1)} %fusion.4), calls=%async_computation.4 | async-start | bytes 950272 | tf_op jit(solution)/shard_map/all_to_all | solution.py:114
  205.4 21.2 %copy-start.2 = (s32[128,8]{0,1:T(8,128)S(1)}, s32[128,8]{0,1:T(8,128)}, u32[]{:S(2)}) copy-start(s32[128,8]{0,1:T(8,128)} %param.9) | copy-start | bytes 12292
Sparse Core Ops, SparseCore 0:
  10.1 49.4 all-gather.2
  102.4 42.5 all-gather.4
  167.3 55.7 reduce-scatter.1

commit v5 on v4

--- a/solution.py
+++ b/solution.py
@@ -64,7 +64,7 @@
 
     block = EXPERTS * CAP
     tok_half = lax.all_gather(tok_rows, "x", axis=0, tiled=True)
-    cot_half = lax.all_gather(cot_rows, ("zl", "yl"), axis=0, tiled=True)
+    cot_half = spread(cot_rows, ("zl", "yl"))
     cot_half, gathered = lax.optimization_barrier((cot_half, gathered))
     slot_all = spread(tok_half, ("zl", "yl"))
     slot_cotan = lax.all_gather(cot_half, "x", axis=0, tiled=True)
@@ -100,10 +100,20 @@
     )
     grads = lax.psum_scatter(grads, DP, scatter_dimension=0, tiled=True)[0].astype(F32)
 
-    partial = (
-        dot("rh,hd->rd", d_gate, gate_slab) + dot("rh,hd->rd", d_up, up_slab)
-    ).astype(BF)
-    back = jnp.concatenate([partial, jnp.broadcast_to(score, (score.shape[0], LANES))], axis=1)
+    left = jnp.concatenate([d_gate, d_up, jnp.broadcast_to(score, d_up.shape)], axis=1)
+    first = (jnp.arange(LANES) == 0).astype(BF)[:, None]
+    right = jnp.concatenate(
+        [
+            jnp.concatenate([gate_slab, jnp.zeros((LANES, LANES), BF)], axis=1),
+            jnp.concatenate([up_slab, jnp.zeros((LANES, LANES), BF)], axis=1),
+            jnp.concatenate(
+                [jnp.zeros((LANES, features), BF), jnp.broadcast_to(first, (LANES, LANES))], axis=1
+            ),
+        ],
+        axis=0,
+    )
+    right = lax.optimization_barrier(right)
+    back = dot("rh,hd->rd", left, right).astype(BF)
     back = back.reshape(8, 2 * block, wide)
     back = lax.all_to_all(back, ("x", "zl"), split_axis=0, concat_axis=0, tiled=True)
     back = back.reshape(HSPLIT * block, wide)

time: 235 us -> 204 us (0.87)
  blocking collectives: 55.2 us -> 12.8 us
  other arithmetic: 11.4 us -> 15.8 us
  starting transfers between devices: 32.1 us -> 35.9 us
    all_gather x1 -> x0, blocking collectives: 43.4 us -> none  [shards(): cot_half = lax.all_gather(cot_rows, ('zl', 'yl'), axis=0, tiled=True)]
    all_to_all x1 -> x2, waiting for transfers between devices: 0.01 us -> 28.9 us  [spread(): got = lax.all_to_all(copies, axes, split_axis=0, concat_axis=0, tiled=True)]
    all_gather x1, waiting for transfers between devices: 34.9 us -> 6.88 us  [shards(): slot_cotan = lax.all_gather(cot_half, 'x', axis=0, tiled=True)]
    concatenate x1, other arithmetic: 1.77 us -> 6.13 us  [shards(): jnp.concatenate([jnp.concatenate([gate_slab, jnp.zeros((LANES, LANES), BF...]
    all_to_all x1 -> x2, starting transfers between devices: 8.7 us -> 12.2 us  [spread(): got = lax.all_to_all(copies, axes, split_axis=0, concat_axis=0, tiled=True)]
    dot_general x15 -> x14, matrix products: 22.6 us -> 24.2 us  [dot(): return jnp.einsum(eq, a, b, preferred_element_type=F32)]
  transfers between devices with their start and end apart: 7 -> 8, of which waited for: 4 -> 6; matrix products, arithmetic and copies ran while one was open for 13% -> 19% of each run, Pallas kernels for 0% -> 0%
where the time goes in v5:
time: 204 us; the launch traced here: 203 us
  waiting for transfers between devices  87.6 us (43%)
  starting transfers between devices  35.9 us (18%)
  matrix products  24.2 us (12%)
  other arithmetic  15.8 us (8%)
  between operations  14 us (7%)
  blocking collectives  12.8 us (6%)
  local copies, waits for them, and re-layouts  12.6 us (6%)
    all_to_all x2, waiting for transfers between devices, spread(): got = lax.all_to_all(copies, axes, split_axis=0, concat_axis=0, tiled=True)  28.9 us
    all_to_all x1, waiting for transfers between devices, shards(): lax.all_to_all(back, ('x', 'zl'), split_axis=0, concat_axis=0, tiled=True)  26.7 us
    dot_general x14, matrix products, dot(): return jnp.einsum(eq, a, b, preferred_element_type=F32)  24.2 us
    reduce_scatter x1, waiting for transfers between devices, shards(): lax.psum_scatter(grads, DP, scatter_dimension=0, tiled=True)[0].astype(F32)  13.7 us
    all_gather x1, blocking collectives, shards(): tok_half = lax.all_gather(tok_rows, 'x', axis=0, tiled=True)  12.8 us
    all_to_all x2, starting transfers between devices, spread(): got = lax.all_to_all(copies, axes, split_axis=0, concat_axis=0, tiled=True)  12.2 us
    all_to_all x1, starting transfers between devices, shards(): rows = lax.all_to_all(rows, 'ex', split_axis=0, concat_axis=0, tiled=True)  10.8 us
    all_to_all x1, waiting for transfers between devices, shards(): rows = lax.all_to_all(rows, 'ex', split_axis=0, concat_axis=0, tiled=True)  10.8 us
  transfers between devices with their start and end apart: 8, of which 6 were waited for; matrix products, arithmetic and copies ran while one was open for 19% of the time, Pallas kernels for 0%

profile of v5, /device:TPU:1, one launch (start us, length us, event | category | flops | bytes accessed | tf_op | source)
XLA Modules:
  0.0 203.0 jit_solution(5433098685010183178)
XLA Ops:
  7.2 1.9 pad_maximum_fusion.1
  11.9 1.5 convolution_convert_fusion.6
  14.3 10.8 %all-to-all-start = ((bf16[4,8,7296]{2,1,0:T(8,128)(2,1)}), bf16[4,8,7296]{2,1,0:T(8,128)(2,1)S(1)}, u32[]{:S(2)}, u32[]{:S(2)}) async-start(bf16[4,8,7296]{2,1,0:T(8,128)(2,1)} %maximum_bitcast_fusion), calls=%async_computation | async-start | bytes 933888 | tf_op jit(solution)/shard_map/all_to_all | solution.py:55
  25.1 10.8 %all-to-all-done = bf16[4,8,7296]{2,1,0:T(8,128)(2,1)S(1)} async-done(((bf16[4,8,7296]{2,1,0:T(8,128)(2,1)}), bf16[4,8,7296]{2,1,0:T(8,128)(2,1)S(1)}, u32[]{:S(2)}, u32[]{:S(2)}) %all-to-all-start) | async-done | bytes 466976 | tf_op jit(solution)/shard_map/all_to_all | solution.py:55
  36.2 0.9 broadcast_in_dim.56
  37.1 7.7 %all-to-all-start.1 = ((bf16[4,24,3584]{2,1,0:T(8,128)(2,1)}), bf16[4,24,3584]{2,1,0:T(8,128)(2,1)S(1)}, u32[]{:S(2)}, u32[]{:S(2)}) async-start(bf16[4,24,3584]{2,1,0:T(8,128)(2,1)} %broadcast_in_dim.56), calls=%async_computation.1 | async-start | bytes 1376256 | tf_op jit(solution)/shard_map/all_to_all | solution.py:20
  45.0 12.8 %all_gather.10 = bf16[96,3712]{1,0:T(8,128)(2,1)S(1)} all-gather(bf16[24,3712]{1,0:T(8,128)(2,1)S(1)} %convolution_convert_fusion.7), channel_id=1, replica_groups=mesh['yh'=4,'core'=2,'ex'=4,'zl'=2,'x'=4,'yl'=2] {'x'}, dimensions={0}, use_global_device_ids=true | all-gather | bytes 890880 | tf_op jit(solution)/shard_map/all_gather | solution.py:66
  57.9 5.4 %all-to-all-done.1 = bf16[4,24,3584]{2,1,0:T(8,128)(2,1)S(1)} async-done(((bf16[4,24,3584]{2,1,0:T(8,128)(2,1)}), bf16[4,24,3584]{2,1,0:T(8,128)(2,1)S(1)}, u32[]{:S(2)}, u32[]{:S(2)}) %all-to-all-start.1) | async-done | bytes 688160 | tf_op jit(solution)/shard_map/all_to_all | solution.py:20
  63.3 1.8 broadcast_in_dim.64
  65.1 4.6 %all-to-all-start.2 = ((bf16[4,96,3712]{2,1,0:T(8,128)(2,1)}), bf16[4,96,3712]{2,1,0:T(8,128)(2,1)}, u32[]{:S(2)}, u32[]{:S(2)}) async-start(bf16[4,96,3712]{2,1,0:T(8,128)(2,1)} %broadcast_in_dim.64), calls=%async_computation.2 | async-start | bytes 5701632 | tf_op jit(solution)/shard_map/all_to_all | solution.py:20
  70.4 2.8 %fusion.68 = (bf16[8,1,16,3584]{3,2,1,0:T(8,128)(2,1)}, bf16[8,1,16,3584]{3,2,1,0:T(8,128)(2,1)S(1)}, bf16[8,1,16,3584]{3,2,1,0:T(8,128)(2,1)S(1)}) fusion(bf16[8,3,16,3584]{3,2,1,0:T(8,128)(2,1)} %bitcast.154), kind=kLoop, calls=%fused_computation.125 | loop fusion | bytes 5505024 | tf_op jit(solution)/shard_map/slice | solution.py:78
  73.4 6.1 %fusion.9 = bf16[384,3712]{1,0:T(8,128)(2,1)} fusion(bf16[128,128]{1,0:T(8,128)(2,1)S(1)} %broadcast_in_dim.108, bf16[128,3584]{1,0:T(8,128)(2,1)S(1)} %bitcast.147, bf16[128,3584]{1,0:T(8,128)(2,1)S(1)} %bitcast.150), kind=kLoop, calls=%fused_computation.23 | loop fusion | flops 19955712 | bytes 4718592 | tf_op jit(solution)/shard_map/concatenate | solution.py:105
  79.5 23.5 %all-to-all-done.2 = bf16[4,96,3712]{2,1,0:T(8,128)(2,1)} async-done(((bf16[4,96,3712]{2,1,0:T(8,128)(2,1)}), bf16[4,96,3712]{2,1,0:T(8,128)(2,1)}, u32[]{:S(2)}, u32[]{:S(2)}) %all-to-all-start.2) | async-done | bytes 2850848 | tf_op jit(solution)/shard_map/all_to_all | solution.py:20
  103.0 2.0 slice.65
  104.9 0.9 convolution_bitcast_fusion.2
  105.8 0.9 convolution_bitcast_fusion.1
  106.7 1.0 convert_reduce_fusion
  108.0 6.9 %all-gather.5.cloned.1.call-done = bf16[384,3584]{1,0:T(8,128)(2,1)} async-done(((bf16[96,3584]{1,0:T(8,128)(2,1)}), bf16[384,3584]{1,0:T(8,128)(2,1)}) %all-gather.5.cloned.1.call-update) | async-done | bytes 2752528 | tf_op jit(solution)/shard_map/all_gather | solution.py:70
  114.8 3.0 %fusion.21 = (bf16[384]{0:T(512)(128)(2,1)S(1)}, bf16[384,128]{1,0:T(8,128)(2,1)S(1)}, bf16[384,128]{1,0:T(8,128)(2,1)S(1)}, bf16[384,128]{1,0:T(8,128)(2,1)S(1)}) fusion(f32[4,4,24,128]{3,2,1,0:T(8,128)S(1)} %copy.51, f32[4,4,24,128]{3,2,1,0:T(8,128)S(1)} %copy.52, f32[384]{0:T(512)S(1)} %reshape.223, bf16[384,3584]{1,0:T(8,128)(2,1)} %all-gather.5.cloned.1.call-done, ...), kind=kOutput, calls=%fused_computation.46 | convolution fusion | flops 353255040 | bytes 4360448 | tf_op jit(solution)/shard_map/rd,hd->rh/dot_general | solution.py:25
  117.8 3.8 %convolution_convert_fusion.3 = bf16[3584,128]{1,0:T(8,128)(2,1)} fusion(bf16[384,128]{1,0:T(8,128)(2,1)S(1)} %bitcast.170, bf16[384,3712]{1,0:T(8,128)(2,1)} %bitcast.23), kind=kOutput, calls=%fused_computation.13 | convolution fusion | flops 352780288 | bytes 3768320 | tf_op jit(solution)/shard_map/rd,rh->dh/dot_general | solution.py:25
  121.7 3.2 %convolution_convert_fusion = bf16[384,3712]{1,0:T(8,128)(2,1)} fusion(bf16[384,3712]{1,0:T(8,128)(2,1)S(1)} %copy-done.1, bf16[384,128]{1,0:T(8,128)(2,1)S(1)} %broadcast_in_dim.107, bf16[384,128]{1,0:T(8,128)(2,1)S(1)} %get-tuple-element.53, bf16[384,128]{1,0:T(8,128)(2,1)S(1)} %get-tuple-element.52), kind=kOutput, calls=%fused_computation.10 | convolution fusion | flops 1097023488 | bytes 5996544 | tf_op jit(solution)/shard_map/rh,hd->rd/dot_general | solution.py:25
  125.0 4.4 %all-to-all-start.3 = ((bf16[8,48,3712]{2,1,0:T(8,128)(2,1)}), bf16[8,48,3712]{2,1,0:T(8,128)(2,1)}, u32[]{:S(2)}, u32[]{:S(2)}) async-start(bf16[8,48,3712]{2,1,0:T(8,128)(2,1)} %bitcast.146), calls=%async_computation.4 | async-start | bytes 5701632 | tf_op jit(solution)/shard_map/all_to_all | solution.py:118
  129.7 2.8 %convolution_convert_fusion.2 = bf16[3584,128]{1,0:T(8,128)(2,1)S(1)} fusion(bf16[384,3584]{1,0:T(8,128)(2,1)} %all-gather.5.cloned.1.call-done, bf16[384,128]{1,0:T(8,128)(2,1)S(1)} %get-tuple-element.45, f32[384]{0:T(512)S(1)} %reshape.223), kind=kOutput, calls=%fused_computation.12 | convolution fusion | flops 352927744 | bytes 3769856 | tf_op jit(solution)/shard_map/rd,rh->dh/dot_general | solution.py:25
  132.5 2.8 %convolution_convert_fusion.4 = bf16[3584,128]{1,0:T(8,128)(2,1)S(1)} fusion(bf16[384,128]{1,0:T(8,128)(2,1)S(1)} %bitcast.169, bf16[384,3712]{1,0:T(8,128)(2,1)} %bitcast.23), kind=kOutput, calls=%fused_computation.14 | convolution fusion | flops 352780288 | bytes 3768320 | tf_op jit(solution)/shard_map/rd,rh->dh/dot_general | solution.py:25
  135.2 1.9 pad_maximum_fusion
  137.2 26.7 %all-to-all-done.3 = bf16[8,48,3712]{2,1,0:T(8,128)(2,1)} async-done(((bf16[8,48,3712]{2,1,0:T(8,128)(2,1)}), bf16[8,48,3712]{2,1,0:T(8,128)(2,1)}, u32[]{:S(2)}, u32[]{:S(2)}) %all-to-all-start.3) | async-done | bytes 2850848 | tf_op jit(solution)/shard_map/all_to_all | solution.py:118
  163.9 3.2 %fusion.7 = bf16[8,8,3712]{2,1,0:T(8,128)(2,1)} fusion(bf16[8,48,3712]{2,1,0:T(8,128)(2,1)} %all-to-all-done.3, bf16[64,48]{0,1:T(8,128)(2,1)S(1)} %fusion.33), kind=kOutput, calls=%fused_computation.17 | convolution fusion | flops 182689792 | bytes 3332096 | tf_op jit(solution)/shard_map/ck,kd->cd/dot_general | solution.py:25
  167.1 8.0 %all-to-all-start.4 = ((bf16[8,8,3712]{2,1,0:T(8,128)(2,1)}), bf16[8,8,3712]{2,1,0:T(8,128)(2,1)S(1)}, u32[]{:S(2)}, u32[]{:S(2)}) async-start(bf16[8,8,3712]{2,1,0:T(8,128)(2,1)} %fusion.7), calls=%async_computation.5 | async-start | bytes 950272 | tf_op jit(solution)/shard_map/all_to_all | solution.py:124
  176.0 1.1 dynamic-slice_bitcast_fusion
  178.6 13.7 %reduce-scatter.2.cloned.1.call-done = bf16[1,3,448,128]{3,2,1,0:T(8,128)(2,1)} async-done(((bf16[8,3,448,128]{3,2,1,0:T(8,128)(2,1)}), bf16[1,3,448,128]{3,2,1,0:T(8,128)(2,1)}) %reduce-scatter.2.cloned.1.call-update) | async-done | bytes 344080 | tf_op jit(solution)/shard_map/reduce_scatter | solution.py:101
  192.3 1.0 convert_element_type.135
  194.3 1.4 convolution_convert_fusion.1
  (54 shorter events, 9.9 us)
Async XLA Ops:
  7.2 4.4 %copy-start = (bf16[128,3584]{1,0:T(8,128)(2,1)S(1)}, bf16[128,3584]{1,0:T(8,128)(2,1)}, u32[]{:S(2)}) copy-start(bf16[128,3584]{1,0:T(8,128)(2,1)} %param.8) | copy-start | bytes 2752516
  7.2 62.6 %all-gather.3.cloned.1.call-start = ((), (), s32[]{:S(2)}) async-start(), calls=%async_computation.6 | async-start | bytes 3096576 | tf_op jit(solution)/shard_map/all_gather | solution.py:33
  14.3 21.7 %all-to-all-start = ((bf16[4,8,7296]{2,1,0:T(8,128)(2,1)}), bf16[4,8,7296]{2,1,0:T(8,128)(2,1)S(1)}, u32[]{:S(2)}, u32[]{:S(2)}) async-start(bf16[4,8,7296]{2,1,0:T(8,128)(2,1)} %maximum_bitcast_fusion), calls=%async_computation | async-start | bytes 933888 | tf_op jit(solution)/shard_map/all_to_all | solution.py:55
  37.1 26.1 %all-to-all-start.1 = ((bf16[4,24,3584]{2,1,0:T(8,128)(2,1)}), bf16[4,24,3584]{2,1,0:T(8,128)(2,1)S(1)}, u32[]{:S(2)}, u32[]{:S(2)}) async-start(bf16[4,24,3584]{2,1,0:T(8,128)(2,1)} %broadcast_in_dim.56), calls=%async_computation.1 | async-start | bytes 1376256 | tf_op jit(solution)/shard_map/all_to_all | solution.py:20
  63.3 1.8 copy-start.2
  65.1 37.9 %all-to-all-start.2 = ((bf16[4,96,3712]{2,1,0:T(8,128)(2,1)}), bf16[4,96,3712]{2,1,0:T(8,128)(2,1)}, u32[]{:S(2)}, u32[]{:S(2)}) async-start(bf16[4,96,3712]{2,1,0:T(8,128)(2,1)} %broadcast_in_dim.64), calls=%async_computation.2 | async-start | bytes 5701632 | tf_op jit(solution)/shard_map/all_to_all | solution.py:20
  69.7 45.2 %all-gather.5.cloned.1.call-start = ((), (), s32[]{:S(2)}) async-start(), calls=%async_computation.7 | async-start | bytes 3440640 | tf_op jit(solution)/shard_map/all_gather | solution.py:70
  117.8 3.9 %copy-start.1 = (bf16[384,3712]{1,0:T(8,128)(2,1)S(1)}, bf16[384,3712]{1,0:T(8,128)(2,1)}, u32[]{:S(2)}) copy-start(bf16[384,3712]{1,0:T(8,128)(2,1)} %fusion.9) | copy-start | bytes 8552452
  125.0 38.9 %all-to-all-start.3 = ((bf16[8,48,3712]{2,1,0:T(8,128)(2,1)}), bf16[8,48,3712]{2,1,0:T(8,128)(2,1)}, u32[]{:S(2)}, u32[]{:S(2)}) async-start(bf16[8,48,3712]{2,1,0:T(8,128)(2,1)} %bitcast.146), calls=%async_computation.4 | async-start | bytes 5701632 | tf_op jit(solution)/shard_map/all_to_all | solution.py:118
  129.4 62.9 %reduce-scatter.2.cloned.1.call-start = ((), (), s32[]{:S(2)}) async-start(), calls=%async_computation.8 | async-start | bytes 3096576 | tf_op jit(solution)/shard_map/reduce_scatter | solution.py:101
  132.4 2.8 %copy-start.3 = (bf16[3584,128]{1,0:T(8,128)(2,1)S(1)}, bf16[3584,128]{1,0:T(8,128)(2,1)}, u32[]{:S(2)}) copy-start(bf16[3584,128]{1,0:T(8,128)(2,1)} %convolution_convert_fusion.3) | copy-start | bytes 2752516
  167.1 27.1 %all-to-all-start.4 = ((bf16[8,8,3712]{2,1,0:T(8,128)(2,1)}), bf16[8,8,3712]{2,1,0:T(8,128)(2,1)S(1)}, u32[]{:S(2)}, u32[]{:S(2)}) async-start(bf16[8,8,3712]{2,1,0:T(8,128)(2,1)} %fusion.7), calls=%async_computation.5 | async-start | bytes 950272 | tf_op jit(solution)/shard_map/all_to_all | solution.py:124
  175.1 20.7 %copy-start.4 = (s32[128,8]{0,1:T(8,128)S(1)}, s32[128,8]{0,1:T(8,128)}, u32[]{:S(2)}) copy-start(s32[128,8]{0,1:T(8,128)} %param.9) | copy-start | bytes 12292
Sparse Core Ops, SparseCore 0:
  10.1 54.1 all-gather.2
  72.6 42.1 all-gather.4
  137.2 55.0 reduce-scatter.1

commit v6 on v4

--- a/solution.py
+++ b/solution.py
@@ -1,6 +1,8 @@
 import jax
 import jax.numpy as jnp
 from jax import lax
+from jax.experimental import pallas as pl
+from jax.experimental.pallas import tpu as pltpu
 from jax.sharding import Mesh
 from jax.sharding import PartitionSpec as P
 
@@ -9,6 +11,8 @@
 PAD = 8
 EXPERTS = 4
 LANES = 128
+CHUNK = 512
+SPLIT = 2560
 DP = ("yh", "core")
 BF = jnp.bfloat16
 F32 = jnp.float32
@@ -19,6 +23,47 @@
     copies = jnp.broadcast_to(block[None], (count,) + block.shape)
     got = lax.all_to_all(copies, axes, split_axis=0, concat_axis=0, tiled=True)
     return got.reshape((count * block.shape[0],) + block.shape[1:])
+
+
+def weight_grads(x, dy_low, dy_high, d_gate_up, hidden_gated, features):
+    rows = x.shape[0]
+    low = dy_low.shape[1] // CHUNK
+    over_rows = (((0,), (0,)), ((), ()))
+
+    def kernel(x_ref, low_ref, high_ref, d_ref, h_ref, o_ref):
+        def product(a, b):
+            return lax.dot_general(a, b, over_rows, preferred_element_type=F32).astype(BF)
+
+        o_ref[:, : 2 * LANES] = product(x_ref[...], d_ref[...])
+
+        @pl.when(pl.program_id(0) < low)
+        def _():
+            o_ref[:, 2 * LANES :] = product(low_ref[...], h_ref[...])
+
+        @pl.when(pl.program_id(0) >= low)
+        def _():
+            o_ref[:, 2 * LANES :] = product(high_ref[...], h_ref[...])
+
+    return pl.pallas_call(
+        kernel,
+        grid=(features // CHUNK,),
+        in_specs=[
+            pl.BlockSpec((rows, CHUNK), lambda j: (0, j)),
+            pl.BlockSpec((rows, CHUNK), lambda j: (0, jnp.minimum(j, low - 1))),
+            pl.BlockSpec((rows, CHUNK), lambda j: (0, jnp.maximum(j - low, 0))),
+            pl.BlockSpec((rows, 2 * LANES), lambda j: (0, 0)),
+            pl.BlockSpec((rows, LANES), lambda j: (0, 0)),
+        ],
+        out_specs=pl.BlockSpec((CHUNK, 3 * LANES), lambda j: (j, 0)),
+        out_shape=jax.ShapeDtypeStruct((features, 3 * LANES), BF),
+        compiler_params=pltpu.CompilerParams(vmem_limit_bytes=32 << 20),
+        cost_estimate=pl.CostEstimate(
+            flops=2 * rows * features * 3 * LANES,
+            bytes_accessed=2 * features * (2 * rows + 3 * LANES),
+            transcendentals=0,
+        ),
+        name="weight_grads",
+    )(x, dy_low, dy_high, d_gate_up, hidden_gated)
 
 
 def dot(eq, a, b):
@@ -64,11 +109,11 @@
 
     block = EXPERTS * CAP
     tok_half = lax.all_gather(tok_rows, "x", axis=0, tiled=True)
-    cot_half = lax.all_gather(cot_rows, ("zl", "yl"), axis=0, tiled=True)
+    cot_half = spread(cot_rows, ("zl", "yl"))
     cot_half, gathered = lax.optimization_barrier((cot_half, gathered))
     slot_all = spread(tok_half, ("zl", "yl"))
-    slot_cotan = lax.all_gather(cot_half, "x", axis=0, tiled=True)
-    slot_tokens = slot_all[:, :features]
+    cot_low = lax.all_gather(cot_half[:, :SPLIT], "x", axis=0, tiled=True)
+    cot_high = lax.all_gather(cot_half[:, SPLIT:], "x", axis=0, tiled=True)
     gathered = gathered.reshape(n_dp, 3, hidden_dev, features)
 
     def reorder(values):
@@ -77,33 +122,40 @@
 
     slab = [gathered[:, j].reshape(n_dp * hidden_dev, features) for j in range(3)]
     gate_slab, up_slab, down_slab = slab
-    pre_gate = reorder(dot("rd,hd->rh", slot_tokens, gate_slab))
-    pre_up = reorder(dot("rd,hd->rh", slot_tokens, up_slab))
-    slot_gates = reorder(slot_all[:, features : features + 1]).astype(F32)
+    pad = jnp.zeros((LANES, LANES), BF)
+    wide_slab = jnp.concatenate(
+        [
+            jnp.concatenate([gate_slab, pad], axis=1),
+            jnp.concatenate([up_slab, pad], axis=1),
+            jnp.concatenate([jnp.zeros((LANES, features), BF), jnp.eye(LANES, dtype=BF)], axis=1),
+        ],
+        axis=0,
+    )
+    wide_slab = lax.optimization_barrier(wide_slab)
+    both = reorder(dot("rd,hd->rh", slot_all, wide_slab))
+    pre_gate = both[:, :LANES]
+    pre_up = both[:, LANES : 2 * LANES]
+    slot_gates = both[:, 2 * LANES :]
     sigmoid_gate = jax.nn.sigmoid(pre_gate)
     activation = pre_gate * sigmoid_gate
     hidden = (activation * pre_up).astype(BF)
-    back_proj = dot("rd,hd->rh", slot_cotan, down_slab)
+    back_proj = dot("rd,hd->rh", cot_low, down_slab[:, :SPLIT]) + dot(
+        "rd,hd->rh", cot_high, down_slab[:, SPLIT:]
+    )
     score = jnp.sum(hidden.astype(F32) * back_proj, axis=1, keepdims=True).astype(BF)
     scaled = slot_gates * back_proj
     d_gate = (scaled * pre_up * sigmoid_gate * (1.0 + pre_gate * (1.0 - sigmoid_gate))).astype(BF)
     d_up = (scaled * activation).astype(BF)
     hidden_gated = (slot_gates * hidden.astype(F32)).astype(BF)
 
-    grads = jnp.stack(
-        [
-            dot("rd,rh->dh", slot_tokens, reorder(d_gate)).astype(BF).reshape(n_dp, -1, LANES),
-            dot("rd,rh->dh", slot_tokens, reorder(d_up)).astype(BF).reshape(n_dp, -1, LANES),
-            dot("rd,rh->dh", slot_cotan, hidden_gated).astype(BF).reshape(n_dp, -1, LANES),
-        ],
-        axis=1,
+    left = jnp.concatenate([d_gate, d_up, jnp.broadcast_to(score, d_up.shape)], axis=1)
+    back = dot("rh,hd->rd", left, wide_slab).astype(BF)
+    grads = weight_grads(
+        slot_all, cot_low, cot_high, reorder(left[:, : 2 * LANES]), hidden_gated, features
     )
-    grads = lax.psum_scatter(grads, DP, scatter_dimension=0, tiled=True)[0].astype(F32)
+    grads = lax.psum_scatter(grads, DP, scatter_dimension=0, tiled=True).astype(F32)
+    grads = [grads[None, :, LANES * j : LANES * (j + 1)] for j in range(3)]
 
-    partial = (
-        dot("rh,hd->rd", d_gate, gate_slab) + dot("rh,hd->rd", d_up, up_slab)
-    ).astype(BF)
-    back = jnp.concatenate([partial, jnp.broadcast_to(score, (score.shape[0], LANES))], axis=1)
     back = back.reshape(8, 2 * block, wide)
     back = lax.all_to_all(back, ("x", "zl"), split_axis=0, concat_axis=0, tiled=True)
     back = back.reshape(HSPLIT * block, wide)
@@ -127,7 +179,7 @@
     relaid = [
         lax.dynamic_slice_in_dim(w, start, features // n_dp, axis=1).T[None] for w in slab
     ]
-    return (*relaid, grads[0:1], grads[1:2], grads[2:3], token_grad, gate_grad)
+    return (*relaid, *grads, token_grad, gate_grad)
 
 
 def solution(mesh):

time: 235 us -> 196 us (0.83)
  blocking collectives: 55.2 us -> 25 us
  waiting for transfers between devices: 86.9 us -> 68.2 us
  Pallas kernels: 0 us -> 6.64 us
  matrix products: 22.6 us -> 17.6 us
  starting transfers between devices: 32.1 us -> 36.5 us
  local copies, waits for them, and re-layouts: 11.6 us -> 14.3 us
    all_gather x1, waiting for transfers between devices: 34.9 us -> 0.85 us  [shards(): cot_low = lax.all_gather(cot_half[:, :SPLIT], 'x', axis=0, tiled=True)]
    all_gather x1, blocking collectives: 43.4 us -> 12.1 us  [shards(): cot_high = lax.all_gather(cot_half[:, SPLIT:], 'x', axis=0, tiled=True)]
    all_to_all x1 -> x2, waiting for transfers between devices: 0.01 us -> 17.5 us  [spread(): got = lax.all_to_all(copies, axes, split_axis=0, concat_axis=0, tiled=True)]
    pallas_call x0 -> x1, Pallas kernels: none -> 6.64 us  [weight_grads(): pl.pallas_call(kernel, grid=(features // CHUNK,), in_specs=[pl.BlockSpec(...]
    dot_general x15 -> x11, matrix products: 22.6 us -> 17.6 us  [dot(): return jnp.einsum(eq, a, b, preferred_element_type=F32)]
    concatenate x1 -> x3, other arithmetic: 1.77 us -> 5.76 us  [the longest x1 5.67 us: shards(): jnp.concatenate([jnp.concatenate([gate_slab, pad], axis=1), jnp.concatena...]
    all_to_all x1 -> x2, starting transfers between devices: 8.7 us -> 12.2 us  [spread(): got = lax.all_to_all(copies, axes, split_axis=0, concat_axis=0, tiled=True)]
    unnamed x9 -> x17, local copies, waits for them, and re-layouts: 2.31 us -> 5.41 us
  transfers between devices with their start and end apart: 7 -> 8, of which waited for: 4 -> 6; matrix products, arithmetic and copies ran while one was open for 13% -> 16% of each run, Pallas kernels for 0% -> 3%
where the time goes in v6:
time: 196 us; the launch traced here: 195 us
  waiting for transfers between devices  68.2 us (35%)
  starting transfers between devices  36.5 us (19%)
  blocking collectives  25 us (13%)
  matrix products  17.6 us (9%)
  local copies, waits for them, and re-layouts  14.3 us (7%)
  between operations  14 us (7%)
  other arithmetic  12.6 us (6%)
  Pallas kernels  6.64 us (3%)
    all_to_all x1, waiting for transfers between devices, shards(): lax.all_to_all(back, ('x', 'zl'), split_axis=0, concat_axis=0, tiled=True)  24.5 us
    dot_general x11, matrix products, dot(): return jnp.einsum(eq, a, b, preferred_element_type=F32)  17.6 us
    all_to_all x2, waiting for transfers between devices, spread(): got = lax.all_to_all(copies, axes, split_axis=0, concat_axis=0, tiled=True)  17.5 us
    reduce_scatter x1, waiting for transfers between devices, shards(): lax.psum_scatter(grads, DP, scatter_dimension=0, tiled=True).astype(F32)  14.4 us
    all_gather x1, blocking collectives, shards(): tok_half = lax.all_gather(tok_rows, 'x', axis=0, tiled=True)  12.8 us
    all_to_all x2, starting transfers between devices, spread(): got = lax.all_to_all(copies, axes, split_axis=0, concat_axis=0, tiled=True)  12.2 us
    all_gather x1, blocking collectives, shards(): cot_high = lax.all_gather(cot_half[:, SPLIT:], 'x', axis=0, tiled=True)  12.1 us
    all_to_all x1, starting transfers between devices, shards(): rows = lax.all_to_all(rows, 'ex', split_axis=0, concat_axis=0, tiled=True)  10.8 us
  transfers between devices with their start and end apart: 8, of which 6 were waited for; matrix products, arithmetic and copies ran while one was open for 16% of the time, Pallas kernels for 3%

profile of v6, /device:TPU:1, one launch (start us, length us, event | category | flops | bytes accessed | tf_op | source)
XLA Modules:
  0.0 194.8 jit_solution(13695761511998117547)
XLA Ops:
  7.2 1.9 pad_maximum_fusion
  11.9 1.5 convolution_convert_fusion.3
  14.3 10.8 %all-to-all-start = ((bf16[4,8,7296]{2,1,0:T(8,128)(2,1)}), bf16[4,8,7296]{2,1,0:T(8,128)(2,1)S(1)}, u32[]{:S(2)}, u32[]{:S(2)}) async-start(bf16[4,8,7296]{2,1,0:T(8,128)(2,1)} %maximum_bitcast_fusion), calls=%async_computation | async-start | bytes 933888 | tf_op jit(solution)/shard_map/all_to_all | solution.py:100
  25.2 10.8 %all-to-all-done = bf16[4,8,7296]{2,1,0:T(8,128)(2,1)S(1)} async-done(((bf16[4,8,7296]{2,1,0:T(8,128)(2,1)}), bf16[4,8,7296]{2,1,0:T(8,128)(2,1)S(1)}, u32[]{:S(2)}, u32[]{:S(2)}) %all-to-all-start) | async-done | bytes 466976 | tf_op jit(solution)/shard_map/all_to_all | solution.py:100
  36.2 0.9 broadcast_in_dim.64
  37.1 7.7 %all-to-all-start.1 = ((bf16[4,24,3584]{2,1,0:T(8,128)(2,1)}), bf16[4,24,3584]{2,1,0:T(8,128)(2,1)S(1)}, u32[]{:S(2)}, u32[]{:S(2)}) async-start(bf16[4,24,3584]{2,1,0:T(8,128)(2,1)} %broadcast_in_dim.64), calls=%async_computation.1 | async-start | bytes 1376256 | tf_op jit(solution)/shard_map/all_to_all | solution.py:24
  45.1 12.8 %all_gather.13 = bf16[96,3712]{1,0:T(8,128)(2,1)S(1)} all-gather(bf16[24,3712]{1,0:T(8,128)(2,1)S(1)} %convolution_convert_fusion.4), channel_id=1, replica_groups=mesh['yh'=4,'core'=2,'ex'=4,'zl'=2,'x'=4,'yl'=2] {'x'}, dimensions={0}, use_global_device_ids=true | all-gather | bytes 890880 | tf_op jit(solution)/shard_map/all_gather | solution.py:111
  57.9 5.4 %all-to-all-done.1 = bf16[4,24,3584]{2,1,0:T(8,128)(2,1)S(1)} async-done(((bf16[4,24,3584]{2,1,0:T(8,128)(2,1)}), bf16[4,24,3584]{2,1,0:T(8,128)(2,1)S(1)}, u32[]{:S(2)}, u32[]{:S(2)}) %all-to-all-start.1) | async-done | bytes 688160 | tf_op jit(solution)/shard_map/all_to_all | solution.py:24
  63.2 1.8 broadcast_in_dim.109
  65.0 4.6 %all-to-all-start.2 = ((bf16[4,96,3712]{2,1,0:T(8,128)(2,1)}), bf16[4,96,3712]{2,1,0:T(8,128)(2,1)}, u32[]{:S(2)}, u32[]{:S(2)}) async-start(bf16[4,96,3712]{2,1,0:T(8,128)(2,1)} %broadcast_in_dim.109), calls=%async_computation.2 | async-start | bytes 5701632 | tf_op jit(solution)/shard_map/all_to_all | solution.py:24
  69.7 0.8 slice.58
  70.7 1.9 fusion.63
  72.6 5.7 %fusion.8 = bf16[384,3712]{1,0:T(8,128)(2,1)} fusion(bf16[128,3584]{1,0:T(8,128)(2,1)S(1)} %bitcast.87, bf16[128,3584]{1,0:T(8,128)(2,1)S(1)} %bitcast.89, bf16[128,3712]{1,0:T(8,128)(2,1)S(1)} %pad_convert_fusion), kind=kLoop, calls=%fused_computation.18 | loop fusion | flops 17104896 | bytes 5636096 | tf_op jit(solution)/shard_map/concatenate | solution.py:126
  78.3 12.1 %all_gather.15.high_ref = bf16[384,1024]{1,0:T(8,128)(2,1)S(1)} all-gather(bf16[96,1024]{1,0:T(8,128)(2,1)S(1)} %slice.59), channel_id=1, replica_groups=mesh['yh'=4,'core'=2,'ex'=4,'zl'=2,'x'=4,'yl'=2] {'x'}, dimensions={0}, use_global_device_ids=true | all-gather | bytes 983040 | tf_op jit(solution)/shard_map/all_gather | solution.py:116
  90.8 12.1 %all-to-all-done.2 = bf16[4,96,3712]{2,1,0:T(8,128)(2,1)} async-done(((bf16[4,96,3712]{2,1,0:T(8,128)(2,1)}), bf16[4,96,3712]{2,1,0:T(8,128)(2,1)}, u32[]{:S(2)}, u32[]{:S(2)}) %all-to-all-start.2) | async-done | bytes 2850848 | tf_op jit(solution)/shard_map/all_to_all | solution.py:24
  103.0 4.4 %fusion.11 = f32[4,4,24,384]{3,2,0,1:T(8,128)S(1)} fusion(bf16[4,4,24,3712]{3,2,1,0:T(8,128)(2,1)} %bitcast.24, bf16[384,3712]{1,0:T(8,128)(2,1)} %fusion.8), kind=kOutput, calls=%fused_computation.22 | convolution fusion | flops 1094713344 | bytes 6291456 | tf_op jit(solution)/shard_map/rd,hd->rh/dot_general | solution.py:70
  107.4 0.8 all-gather.5.cloned.1.call-done.low_ref
  108.3 2.6 %fusion.28 = (bf16[384]{0:T(512)(128)(2,1)S(1)}, bf16[384,128]{1,0:T(8,128)(2,1)S(1)}, bf16[384,128]{1,0:T(8,128)(2,1)S(1)}, bf16[384,128]{1,0:T(8,128)(2,1)S(1)}) fusion(f32[384,384]{1,0:T(8,128)S(1)} %bitcast.101, f32[384,128]{1,0:T(8,128)S(1)} %fusion.23, bf16[384,2560]{1,0:T(8,128)(2,1)} %all-gather.5.cloned.1.call-done.low_ref, ...), kind=kOutput, calls=%fused_computation.46 | convolution fusion | flops 252640896 | bytes 3703552 | tf_op jit(solution)/shard_map/rd,hd->rh/dot_general | solution.py:70
  111.1 3.2 %convolution_convert_fusion = bf16[384,3712]{1,0:T(8,128)(2,1)} fusion(bf16[384,3712]{1,0:T(8,128)(2,1)S(1)} %copy-done.3, bf16[384,128]{1,0:T(8,128)(2,1)S(1)} %broadcast_in_dim.114, bf16[384,128]{1,0:T(8,128)(2,1)S(1)} %get-tuple-element.41, bf16[384,128]{1,0:T(8,128)(2,1)S(1)} %get-tuple-element.42), kind=kOutput, calls=%fused_computation.8 | convolution fusion | flops 1097023488 | bytes 5996544 | tf_op jit(solution)/shard_map/rh,hd->rd/dot_general | solution.py:70
  114.3 4.4 %all-to-all-start.3 = ((bf16[8,48,3712]{2,1,0:T(8,128)(2,1)}), bf16[8,48,3712]{2,1,0:T(8,128)(2,1)}, u32[]{:S(2)}, u32[]{:S(2)}) async-start(bf16[8,48,3712]{2,1,0:T(8,128)(2,1)} %bitcast.86), calls=%async_computation.4 | async-start | bytes 5701632 | tf_op jit(solution)/shard_map/all_to_all | solution.py:160
  118.8 1.5 copy-done.2
  120.4 6.6 %weight_grads.1 = bf16[3584,384]{1,0:T(8,128)(2,1)S(1)} custom-call(bf16[384,3712]{1,0:T(8,128)(2,1)} %bitcast.23.x_ref, bf16[384,2560]{1,0:T(8,128)(2,1)S(1)} %copy-done.2, bf16[384,1024]{1,0:T(8,128)(2,1)S(1)} %all_gather.15.high_ref, bf16[384,256]{1,0:T(8,128)(2,1)S(1)} %bitcast.85, bf16[384,128]{1,0:T(8,128)(2,1)S(1)} %fusion.27.h_ref), custom_call_target="tpu_custom_call" | custom-call | flops 1056964608 | bytes 8257536 | tf_op jit(solution)/shard_map/weight_grads/pallas_call | solution.py:47
  127.0 1.5 copy-done.1
  128.7 24.5 %all-to-all-done.3 = bf16[8,48,3712]{2,1,0:T(8,128)(2,1)} async-done(((bf16[8,48,3712]{2,1,0:T(8,128)(2,1)}), bf16[8,48,3712]{2,1,0:T(8,128)(2,1)}, u32[]{:S(2)}, u32[]{:S(2)}) %all-to-all-start.3) | async-done | bytes 2850848 | tf_op jit(solution)/shard_map/all_to_all | solution.py:160
  153.2 3.3 %fusion.6 = bf16[8,8,3712]{2,1,0:T(8,128)(2,1)} fusion(bf16[8,48,3712]{2,1,0:T(8,128)(2,1)} %all-to-all-done.3, bf16[64,48]{0,1:T(8,128)(2,1)S(1)} %fusion.31), kind=kOutput, calls=%fused_computation.12 | convolution fusion | flops 182689792 | bytes 3332096 | tf_op jit(solution)/shard_map/ck,kd->cd/dot_general | solution.py:70
  156.5 8.8 %all-to-all-start.4 = ((bf16[8,8,3712]{2,1,0:T(8,128)(2,1)}), bf16[8,8,3712]{2,1,0:T(8,128)(2,1)S(1)}, u32[]{:S(2)}, u32[]{:S(2)}) async-start(bf16[8,8,3712]{2,1,0:T(8,128)(2,1)} %fusion.6), calls=%async_computation.5 | async-start | bytes 950272 | tf_op jit(solution)/shard_map/all_to_all | solution.py:166
  165.3 1.0 dynamic-slice_bitcast_fusion.2
  167.1 1.1 dynamic-slice_bitcast_fusion
  169.7 14.4 %reduce-scatter.2.cloned.1.call-done = bf16[448,384]{1,0:T(8,128)(2,1)} async-done(((bf16[3584,384]{1,0:T(8,128)(2,1)}), bf16[448,384]{1,0:T(8,128)(2,1)}) %reduce-scatter.2.cloned.1.call-update) | async-done | bytes 344080 | tf_op jit(solution)/shard_map/reduce_scatter | solution.py:156
  184.1 1.0 convert_element_type.95
  185.1 0.9 slice_bitcast_fusion
  186.1 1.4 convolution_convert_fusion.1
  (53 shorter events, 8.4 us)
Async XLA Ops:
  7.2 4.5 %copy-start = (bf16[128,3584]{1,0:T(8,128)(2,1)S(1)}, bf16[128,3584]{1,0:T(8,128)(2,1)}, u32[]{:S(2)}) copy-start(bf16[128,3584]{1,0:T(8,128)(2,1)} %param.8) | copy-start | bytes 2752516
  7.2 62.5 %all-gather.3.cloned.1.call-start = ((), (), s32[]{:S(2)}) async-start(), calls=%async_computation.6 | async-start | bytes 3096576 | tf_op jit(solution)/shard_map/all_gather | solution.py:78
  14.3 21.7 %all-to-all-start = ((bf16[4,8,7296]{2,1,0:T(8,128)(2,1)}), bf16[4,8,7296]{2,1,0:T(8,128)(2,1)S(1)}, u32[]{:S(2)}, u32[]{:S(2)}) async-start(bf16[4,8,7296]{2,1,0:T(8,128)(2,1)} %maximum_bitcast_fusion), calls=%async_computation | async-start | bytes 933888 | tf_op jit(solution)/shard_map/all_to_all | solution.py:100
  37.1 26.1 %all-to-all-start.1 = ((bf16[4,24,3584]{2,1,0:T(8,128)(2,1)}), bf16[4,24,3584]{2,1,0:T(8,128)(2,1)S(1)}, u32[]{:S(2)}, u32[]{:S(2)}) async-start(bf16[4,24,3584]{2,1,0:T(8,128)(2,1)} %broadcast_in_dim.64), calls=%async_computation.1 | async-start | bytes 1376256 | tf_op jit(solution)/shard_map/all_to_all | solution.py:24
  65.0 37.9 %all-to-all-start.2 = ((bf16[4,96,3712]{2,1,0:T(8,128)(2,1)}), bf16[4,96,3712]{2,1,0:T(8,128)(2,1)}, u32[]{:S(2)}, u32[]{:S(2)}) async-start(bf16[4,96,3712]{2,1,0:T(8,128)(2,1)} %broadcast_in_dim.109), calls=%async_computation.2 | async-start | bytes 5701632 | tf_op jit(solution)/shard_map/all_to_all | solution.py:24
  69.6 38.6 %all-gather.5.cloned.1.call-start = ((), (), s32[]{:S(2)}) async-start(), calls=%async_computation.7 | async-start | bytes 2457600 | tf_op jit(solution)/shard_map/all_gather | solution.py:115
  72.6 17.8 %copy-start.4 = (bf16[8,1,16,3584]{3,2,1,0:T(8,128)(2,1)}, bf16[8,1,16,3584]{3,2,1,0:T(8,128)(2,1)S(1)}, u32[]{:S(2)}) copy-start(bf16[8,1,16,3584]{3,2,1,0:T(8,128)(2,1)S(1)} %get-tuple-element.40) | copy-start | bytes 2752516
  72.6 17.8 %copy-start.5 = (bf16[8,1,16,3584]{3,2,1,0:T(8,128)(2,1)}, bf16[8,1,16,3584]{3,2,1,0:T(8,128)(2,1)S(1)}, u32[]{:S(2)}) copy-start(bf16[8,1,16,3584]{3,2,1,0:T(8,128)(2,1)S(1)} %get-tuple-element.38) | copy-start | bytes 2752516
  108.3 2.8 %copy-start.3 = (bf16[384,3712]{1,0:T(8,128)(2,1)S(1)}, bf16[384,3712]{1,0:T(8,128)(2,1)}, u32[]{:S(2)}) copy-start(bf16[384,3712]{1,0:T(8,128)(2,1)} %fusion.8) | copy-start | bytes 8552452
  114.3 38.9 %all-to-all-start.3 = ((bf16[8,48,3712]{2,1,0:T(8,128)(2,1)}), bf16[8,48,3712]{2,1,0:T(8,128)(2,1)}, u32[]{:S(2)}, u32[]{:S(2)}) async-start(bf16[8,48,3712]{2,1,0:T(8,128)(2,1)} %bitcast.86), calls=%async_computation.4 | async-start | bytes 5701632 | tf_op jit(solution)/shard_map/all_to_all | solution.py:160
  118.7 65.4 %reduce-scatter.2.cloned.1.call-start = ((), (), s32[]{:S(2)}) async-start(), calls=%async_computation.8 | async-start | bytes 3096576 | tf_op jit(solution)/shard_map/reduce_scatter | solution.py:156
  118.8 1.5 copy-start.2
  127.0 1.6 copy-start.1
  156.5 29.5 %all-to-all-start.4 = ((bf16[8,8,3712]{2,1,0:T(8,128)(2,1)}), bf16[8,8,3712]{2,1,0:T(8,128)(2,1)S(1)}, u32[]{:S(2)}, u32[]{:S(2)}) async-start(bf16[8,8,3712]{2,1,0:T(8,128)(2,1)} %fusion.6), calls=%async_computation.5 | async-start | bytes 950272 | tf_op jit(solution)/shard_map/all_to_all | solution.py:166
  165.3 22.3 %copy-start.6 = (s32[128,8]{0,1:T(8,128)S(1)}, s32[128,8]{0,1:T(8,128)}, u32[]{:S(2)}) copy-start(s32[128,8]{0,1:T(8,128)} %param.9) | copy-start | bytes 12292
Sparse Core Ops, SparseCore 0:
  10.1 54.1 all-gather.2
  72.6 35.6 all-gather.4
  128.7 55.3 reduce-scatter.1

commit v7 on v4

--- a/solution.py
+++ b/solution.py
@@ -1,6 +1,8 @@
 import jax
 import jax.numpy as jnp
 from jax import lax
+from jax.experimental import pallas as pl
+from jax.experimental.pallas import tpu as pltpu
 from jax.sharding import Mesh
 from jax.sharding import PartitionSpec as P
 
@@ -9,6 +11,8 @@
 PAD = 8
 EXPERTS = 4
 LANES = 128
+CHUNK = 512
+SPLIT = 2560
 DP = ("yh", "core")
 BF = jnp.bfloat16
 F32 = jnp.float32
@@ -19,6 +23,137 @@
     copies = jnp.broadcast_to(block[None], (count,) + block.shape)
     got = lax.all_to_all(copies, axes, split_axis=0, concat_axis=0, tiled=True)
     return got.reshape((count * block.shape[0],) + block.shape[1:])
+
+
+def slab_math(x, dy_low, dy_high, weights, features):
+    rows, wide = x.shape
+    block = rows // HSPLIT
+    steps = features // CHUNK
+    low = dy_low.shape[1] // CHUNK
+    n_dp, _, hidden_dev, _ = weights.shape
+    by_columns = (((1,), (1,)), ((), ()))
+    by_rows = (((0,), (0,)), ((), ()))
+
+    def column(j):
+        return jnp.where(j < steps, j, jnp.minimum(j - steps, steps - 1))
+
+    def kernel(
+        x_ref, gate_ref, low_ref, high_ref, w_ref, back_ref, grad_ref, au, q, d_tok, d_cot, hg, score, d_tok_h, d_cot_h, hg_h
+    ):
+        j = pl.program_id(0)
+        at = column(j)
+
+        def slab(which):
+            return w_ref[:, which].reshape(n_dp * hidden_dev, CHUNK)
+
+        @pl.when(j == 0)
+        def _():
+            au[...] = jnp.zeros_like(au)
+            q[...] = jnp.zeros_like(q)
+
+        @pl.when(j < steps)
+        def _():
+            both = jnp.concatenate([slab(0), slab(1)], axis=0)
+            au[...] += lax.dot_general(x_ref[...], both, by_columns, preferred_element_type=F32)
+
+        @pl.when((j < steps) & (at < low))
+        def _():
+            q[...] += lax.dot_general(low_ref[...], slab(2), by_columns, preferred_element_type=F32)
+
+        @pl.when((j < steps) & (at >= low))
+        def _():
+            q[...] += lax.dot_general(high_ref[...], slab(2), by_columns, preferred_element_type=F32)
+
+        @pl.when(j == steps - 1)
+        def _():
+            for i in range(HSPLIT):
+                tok = slice(i * block, (i + 1) * block)
+                first = (i % 4 * 4 + i // 4) * block
+                cot = slice(first, first + block)
+                a = au[tok, :LANES]
+                u = au[tok, LANES:]
+                gate = gate_ref[tok, :].astype(F32)
+                back_proj = q[cot, :]
+                sigmoid = jax.nn.sigmoid(a)
+                act = a * sigmoid
+                hidden = (act * u).astype(BF).astype(F32)
+                scaled = gate * back_proj
+                d_gate = scaled * u * sigmoid * (1.0 + a * (1.0 - sigmoid))
+                d_up = scaled * act
+                d_tok[tok, :LANES] = d_gate
+                d_tok[tok, LANES:] = d_up
+                d_cot[cot, :LANES] = d_gate
+                d_cot[cot, LANES:] = d_up
+                hg[cot, :] = gate * hidden
+                part = jnp.sum(hidden * back_proj, axis=1, keepdims=True)
+                score[cot, :] = jnp.broadcast_to(part, (block, LANES))
+            d_tok_h[...] = d_tok[...].astype(BF)
+            d_cot_h[...] = d_cot[...].astype(BF)
+            hg_h[...] = hg[...].astype(BF)
+
+        @pl.when((j >= steps) & (j < 2 * steps))
+        def _():
+            both = jnp.concatenate([slab(0), slab(1)], axis=0)
+            back_ref[...] = jnp.dot(d_cot_h[...], both, preferred_element_type=F32).astype(BF)
+            grad_ref[:, : 2 * LANES] = lax.dot_general(
+                x_ref[...], d_tok_h[...], by_rows, preferred_element_type=F32
+            ).astype(BF)
+
+        @pl.when((j >= steps) & (j < 2 * steps) & (at < low))
+        def _():
+            grad_ref[:, 2 * LANES :] = lax.dot_general(
+                low_ref[...], hg_h[...], by_rows, preferred_element_type=F32
+            ).astype(BF)
+
+        @pl.when((j >= steps) & (j < 2 * steps) & (at >= low))
+        def _():
+            grad_ref[:, 2 * LANES :] = lax.dot_general(
+                high_ref[...], hg_h[...], by_rows, preferred_element_type=F32
+            ).astype(BF)
+
+        @pl.when(j == 2 * steps)
+        def _():
+            back_ref[:, :LANES] = score[...].astype(BF)
+
+    return pl.pallas_call(
+        kernel,
+        grid=(2 * steps + 1,),
+        in_specs=[
+            pl.BlockSpec((rows, CHUNK), lambda j: (0, column(j))),
+            pl.BlockSpec((rows, LANES), lambda j: (0, features // LANES)),
+            pl.BlockSpec((rows, CHUNK), lambda j: (0, jnp.minimum(column(j), low - 1))),
+            pl.BlockSpec((rows, CHUNK), lambda j: (0, jnp.maximum(column(j) - low, 0))),
+            pl.BlockSpec((n_dp, 3, hidden_dev, CHUNK), lambda j: (0, 0, 0, column(j))),
+        ],
+        out_specs=[
+            pl.BlockSpec((rows, CHUNK), lambda j: (0, jnp.maximum(j - steps, 0))),
+            pl.BlockSpec(
+                (CHUNK, 3 * LANES), lambda j: (jnp.clip(j - steps, 0, steps - 1), 0)
+            ),
+        ],
+        out_shape=[
+            jax.ShapeDtypeStruct((rows, wide), BF),
+            jax.ShapeDtypeStruct((features, 3 * LANES), BF),
+        ],
+        scratch_shapes=[
+            pltpu.VMEM((rows, 2 * LANES), F32),
+            pltpu.VMEM((rows, LANES), F32),
+            pltpu.VMEM((rows, 2 * LANES), F32),
+            pltpu.VMEM((rows, 2 * LANES), F32),
+            pltpu.VMEM((rows, LANES), F32),
+            pltpu.VMEM((rows, LANES), F32),
+            pltpu.VMEM((rows, 2 * LANES), BF),
+            pltpu.VMEM((rows, 2 * LANES), BF),
+            pltpu.VMEM((rows, LANES), BF),
+        ],
+        compiler_params=pltpu.CompilerParams(vmem_limit_bytes=56 << 20),
+        cost_estimate=pl.CostEstimate(
+            flops=2 * rows * features * 8 * LANES,
+            bytes_accessed=2 * features * (6 * rows + 9 * LANES),
+            transcendentals=rows * LANES,
+        ),
+        name="slab_math",
+    )(x, x, dy_low, dy_high, weights)
 
 
 def dot(eq, a, b):
@@ -64,46 +199,18 @@
 
     block = EXPERTS * CAP
     tok_half = lax.all_gather(tok_rows, "x", axis=0, tiled=True)
-    cot_half = lax.all_gather(cot_rows, ("zl", "yl"), axis=0, tiled=True)
+    cot_half = spread(cot_rows, ("zl", "yl"))
     cot_half, gathered = lax.optimization_barrier((cot_half, gathered))
     slot_all = spread(tok_half, ("zl", "yl"))
-    slot_cotan = lax.all_gather(cot_half, "x", axis=0, tiled=True)
-    slot_tokens = slot_all[:, :features]
+    cot_low = lax.all_gather(cot_half[:, :SPLIT], "x", axis=0, tiled=True)
+    cot_high = lax.all_gather(cot_half[:, SPLIT:], "x", axis=0, tiled=True)
     gathered = gathered.reshape(n_dp, 3, hidden_dev, features)
 
-    def reorder(values):
-        v = values.reshape(4, 4, block, values.shape[-1])
-        return jnp.swapaxes(v, 0, 1).reshape(values.shape)
-
     slab = [gathered[:, j].reshape(n_dp * hidden_dev, features) for j in range(3)]
-    gate_slab, up_slab, down_slab = slab
-    pre_gate = reorder(dot("rd,hd->rh", slot_tokens, gate_slab))
-    pre_up = reorder(dot("rd,hd->rh", slot_tokens, up_slab))
-    slot_gates = reorder(slot_all[:, features : features + 1]).astype(F32)
-    sigmoid_gate = jax.nn.sigmoid(pre_gate)
-    activation = pre_gate * sigmoid_gate
-    hidden = (activation * pre_up).astype(BF)
-    back_proj = dot("rd,hd->rh", slot_cotan, down_slab)
-    score = jnp.sum(hidden.astype(F32) * back_proj, axis=1, keepdims=True).astype(BF)
-    scaled = slot_gates * back_proj
-    d_gate = (scaled * pre_up * sigmoid_gate * (1.0 + pre_gate * (1.0 - sigmoid_gate))).astype(BF)
-    d_up = (scaled * activation).astype(BF)
-    hidden_gated = (slot_gates * hidden.astype(F32)).astype(BF)
-
-    grads = jnp.stack(
-        [
-            dot("rd,rh->dh", slot_tokens, reorder(d_gate)).astype(BF).reshape(n_dp, -1, LANES),
-            dot("rd,rh->dh", slot_tokens, reorder(d_up)).astype(BF).reshape(n_dp, -1, LANES),
-            dot("rd,rh->dh", slot_cotan, hidden_gated).astype(BF).reshape(n_dp, -1, LANES),
-        ],
-        axis=1,
-    )
-    grads = lax.psum_scatter(grads, DP, scatter_dimension=0, tiled=True)[0].astype(F32)
-
-    partial = (
-        dot("rh,hd->rd", d_gate, gate_slab) + dot("rh,hd->rd", d_up, up_slab)
-    ).astype(BF)
-    back = jnp.concatenate([partial, jnp.broadcast_to(score, (score.shape[0], LANES))], axis=1)
+    back, grads = slab_math(slot_all, cot_low, cot_high, gathered, features)
+    grads = lax.psum_scatter(grads, DP, scatter_dimension=0, tiled=True).astype(F32)
+    grads = [grads[None, :, LANES * j : LANES * (j + 1)] for j in range(3)]
+
     back = back.reshape(8, 2 * block, wide)
     back = lax.all_to_all(back, ("x", "zl"), split_axis=0, concat_axis=0, tiled=True)
     back = back.reshape(HSPLIT * block, wide)
@@ -127,7 +234,7 @@
     relaid = [
         lax.dynamic_slice_in_dim(w, start, features // n_dp, axis=1).T[None] for w in slab
     ]
-    return (*relaid, grads[0:1], grads[1:2], grads[2:3], token_grad, gate_grad)
+    return (*relaid, *grads, token_grad, gate_grad)
 
 
 def solution(mesh):

time: 235 us -> 201 us (0.86)
  blocking collectives: 55.2 us -> 25.5 us
  Pallas kernels: 0 us -> 16.8 us
  matrix products: 22.6 us -> 6.96 us
  other arithmetic: 11.4 us -> 6.81 us
  starting transfers between devices: 32.1 us -> 35.7 us
  waiting for transfers between devices: 86.9 us -> 84.4 us
    all_gather x1, blocking collectives: 43.4 us -> 12.7 us  [shards(): cot_high = lax.all_gather(cot_half[:, SPLIT:], 'x', axis=0, tiled=True)]
    all_gather x1, waiting for transfers between devices: 34.9 us -> 5.92 us  [shards(): cot_low = lax.all_gather(cot_half[:, :SPLIT], 'x', axis=0, tiled=True)]
    all_to_all x1 -> x2, waiting for transfers between devices: 0.01 us -> 25 us  [spread(): got = lax.all_to_all(copies, axes, split_axis=0, concat_axis=0, tiled=True)]
    pallas_call x0 -> x1, Pallas kernels: none -> 16.8 us  [slab_math(): pl.pallas_call(kernel, grid=(2 * steps + 1,), in_specs=[pl.BlockSpec((row...]
    dot_general x15 -> x7, matrix products: 22.6 us -> 6.96 us  [dot(): return jnp.einsum(eq, a, b, preferred_element_type=F32)]
    reduce_scatter x1, waiting for transfers between devices: 14.2 us -> 5.47 us  [shards(): lax.psum_scatter(grads, DP, scatter_dimension=0, tiled=True).astype(F32)]
    all_to_all x1, waiting for transfers between devices: 26.9 us -> 33.6 us  [shards(): lax.all_to_all(back, ('x', 'zl'), split_axis=0, concat_axis=0, tiled=True)]
    all_to_all x1 -> x2, starting transfers between devices: 8.7 us -> 12.2 us  [spread(): got = lax.all_to_all(copies, axes, split_axis=0, concat_axis=0, tiled=True)]
  transfers between devices with their start and end apart: 7 -> 8, of which waited for: 4 -> 7; matrix products, arithmetic and copies ran while one was open for 13% -> 9% of each run, Pallas kernels for 0% -> 0%
where the time goes in v7:
time: 201 us; the launch traced here: 199 us
  waiting for transfers between devices  84.4 us (42%)
  starting transfers between devices  35.7 us (18%)
  blocking collectives  25.5 us (13%)
  Pallas kernels  16.8 us (8%)
  between operations  13.9 us (7%)
  local copies, waits for them, and re-layouts  9.28 us (5%)
  matrix products  6.96 us (3%)
  other arithmetic  6.81 us (3%)
    all_to_all x1, waiting for transfers between devices, shards(): lax.all_to_all(back, ('x', 'zl'), split_axis=0, concat_axis=0, tiled=True)  33.6 us
    all_to_all x2, waiting for transfers between devices, spread(): got = lax.all_to_all(copies, axes, split_axis=0, concat_axis=0, tiled=True)  25 us
    pallas_call x1, Pallas kernels, slab_math(): pl.pallas_call(kernel, grid=(2 * steps + 1,), in_specs=[pl.BlockSpec((row...  16.8 us
    all_gather x1, blocking collectives, shards(): tok_half = lax.all_gather(tok_rows, 'x', axis=0, tiled=True)  12.8 us
    all_gather x1, blocking collectives, shards(): cot_high = lax.all_gather(cot_half[:, SPLIT:], 'x', axis=0, tiled=True)  12.7 us
    all_to_all x2, starting transfers between devices, spread(): got = lax.all_to_all(copies, axes, split_axis=0, concat_axis=0, tiled=True)  12.2 us
    all_to_all x1, starting transfers between devices, shards(): rows = lax.all_to_all(rows, 'ex', split_axis=0, concat_axis=0, tiled=True)  10.9 us
    all_to_all x1, waiting for transfers between devices, shards(): rows = lax.all_to_all(rows, 'ex', split_axis=0, concat_axis=0, tiled=True)  10.8 us
  transfers between devices with their start and end apart: 8, of which 7 were waited for; matrix products, arithmetic and copies ran while one was open for 9% of the time, Pallas kernels for 0%

profile of v7, /device:TPU:1, one launch (start us, length us, event | category | flops | bytes accessed | tf_op | source)
XLA Modules:
  0.0 199.4 jit_solution(3603487283011419617)
XLA Ops:
  7.2 1.9 pad_maximum_fusion
  9.1 0.7 fusion.13
  10.0 0.7 convert_bitcast_fusion
  10.7 0.8 fusion.42
  11.9 1.5 convolution_convert_fusion.1
  13.5 0.8 maximum_bitcast_fusion
  14.3 10.9 %all-to-all-start = ((bf16[4,8,7296]{2,1,0:T(8,128)(2,1)}), bf16[4,8,7296]{2,1,0:T(8,128)(2,1)S(1)}, u32[]{:S(2)}, u32[]{:S(2)}) async-start(bf16[4,8,7296]{2,1,0:T(8,128)(2,1)} %maximum_bitcast_fusion), calls=%async_computation | async-start | bytes 933888 | tf_op jit(solution)/shard_map/all_to_all | solution.py:190
  25.2 10.8 %all-to-all-done = bf16[4,8,7296]{2,1,0:T(8,128)(2,1)S(1)} async-done(((bf16[4,8,7296]{2,1,0:T(8,128)(2,1)}), bf16[4,8,7296]{2,1,0:T(8,128)(2,1)S(1)}, u32[]{:S(2)}, u32[]{:S(2)}) %all-to-all-start) | async-done | bytes 466976 | tf_op jit(solution)/shard_map/all_to_all | solution.py:190
  36.2 0.9 broadcast_in_dim.97
  37.1 7.7 %all-to-all-start.1 = ((bf16[4,24,3584]{2,1,0:T(8,128)(2,1)}), bf16[4,24,3584]{2,1,0:T(8,128)(2,1)S(1)}, u32[]{:S(2)}, u32[]{:S(2)}) async-start(bf16[4,24,3584]{2,1,0:T(8,128)(2,1)} %broadcast_in_dim.97), calls=%async_computation.1 | async-start | bytes 1376256 | tf_op jit(solution)/shard_map/all_to_all | solution.py:24
  45.0 12.8 %all_gather.13 = bf16[96,3712]{1,0:T(8,128)(2,1)S(1)} all-gather(bf16[24,3712]{1,0:T(8,128)(2,1)S(1)} %convolution_convert_fusion.3), channel_id=1, replica_groups=mesh['yh'=4,'core'=2,'ex'=4,'zl'=2,'x'=4,'yl'=2] {'x'}, dimensions={0}, use_global_device_ids=true | all-gather | bytes 890880 | tf_op jit(solution)/shard_map/all_gather | solution.py:201
  57.9 5.4 %all-to-all-done.1 = bf16[4,24,3584]{2,1,0:T(8,128)(2,1)S(1)} async-done(((bf16[4,24,3584]{2,1,0:T(8,128)(2,1)}), bf16[4,24,3584]{2,1,0:T(8,128)(2,1)S(1)}, u32[]{:S(2)}, u32[]{:S(2)}) %all-to-all-start.1) | async-done | bytes 688160 | tf_op jit(solution)/shard_map/all_to_all | solution.py:24
  63.2 1.8 broadcast_in_dim.101
  65.1 4.6 %all-to-all-start.2 = ((bf16[4,96,3712]{2,1,0:T(8,128)(2,1)}), bf16[4,96,3712]{2,1,0:T(8,128)(2,1)}, u32[]{:S(2)}, u32[]{:S(2)}) async-start(bf16[4,96,3712]{2,1,0:T(8,128)(2,1)} %broadcast_in_dim.101), calls=%async_computation.2 | async-start | bytes 5701632 | tf_op jit(solution)/shard_map/all_to_all | solution.py:24
  69.7 0.8 slice.41
  70.6 12.7 %all_gather.15.high_ref = bf16[384,1024]{1,0:T(8,128)(2,1)} all-gather(bf16[96,1024]{1,0:T(8,128)(2,1)S(1)} %slice.42), channel_id=1, replica_groups=mesh['yh'=4,'core'=2,'ex'=4,'zl'=2,'x'=4,'yl'=2] {'x'}, dimensions={0}, use_global_device_ids=true | all-gather | bytes 983040 | tf_op jit(solution)/shard_map/all_gather | solution.py:206
  83.3 19.7 %all-to-all-done.2 = bf16[4,96,3712]{2,1,0:T(8,128)(2,1)} async-done(((bf16[4,96,3712]{2,1,0:T(8,128)(2,1)}), bf16[4,96,3712]{2,1,0:T(8,128)(2,1)}, u32[]{:S(2)}, u32[]{:S(2)}) %all-to-all-start.2) | async-done | bytes 2850848 | tf_op jit(solution)/shard_map/all_to_all | solution.py:24
  102.9 5.9 %all-gather.5.cloned.1.call-done.low_ref = bf16[384,2560]{1,0:T(8,128)(2,1)} async-done(((bf16[96,2560]{1,0:T(8,128)(2,1)}), bf16[384,2560]{1,0:T(8,128)(2,1)}) %all-gather.5.cloned.1.call-update) | async-done | bytes 1966096 | tf_op jit(solution)/shard_map/all_gather | solution.py:205
  108.9 16.8 %slab_math.1 = (bf16[384,3712]{1,0:T(8,128)(2,1)}, bf16[3584,384]{1,0:T(8,128)(2,1)}) custom-call(bf16[384,3712]{1,0:T(8,128)(2,1)} %bitcast.23.x_ref.gate_ref, bf16[384,3712]{1,0:T(8,128)(2,1)} %bitcast.23.x_ref.gate_ref, bf16[384,2560]{1,0:T(8,128)(2,1)} %all-gather.5.cloned.1.call-done.low_ref, bf16[384,1024]{1,0:T(8,128)(2,1)} %all_gather.15.high_ref, ...), custom_call_target="tpu_custom_call" | custom-call | flops 2818572288 | bytes 24772608 | tf_op jit(solution)/shard_map/slab_math/pallas_call | solution.py:118
  125.7 4.4 %all-to-all-start.3 = ((bf16[8,48,3712]{2,1,0:T(8,128)(2,1)}), bf16[8,48,3712]{2,1,0:T(8,128)(2,1)}, u32[]{:S(2)}, u32[]{:S(2)}) async-start(bf16[8,48,3712]{2,1,0:T(8,128)(2,1)} %bitcast.65), calls=%async_computation.4 | async-start | bytes 5701632 | tf_op jit(solution)/shard_map/all_to_all | solution.py:215
  131.0 33.6 %all-to-all-done.3 = bf16[8,48,3712]{2,1,0:T(8,128)(2,1)} async-done(((bf16[8,48,3712]{2,1,0:T(8,128)(2,1)}), bf16[8,48,3712]{2,1,0:T(8,128)(2,1)}, u32[]{:S(2)}, u32[]{:S(2)}) %all-to-all-start.3) | async-done | bytes 2850848 | tf_op jit(solution)/shard_map/all_to_all | solution.py:215
  164.6 3.2 %fusion.3 = bf16[8,8,3712]{2,1,0:T(8,128)(2,1)} fusion(bf16[8,48,3712]{2,1,0:T(8,128)(2,1)} %all-to-all-done.3, bf16[64,48]{0,1:T(8,128)(2,1)S(1)} %fusion.10), kind=kOutput, calls=%fused_computation.5 | convolution fusion | flops 182689792 | bytes 3332096 | tf_op jit(solution)/shard_map/ck,kd->cd/dot_general | solution.py:160
  167.8 8.1 %all-to-all-start.4 = ((bf16[8,8,3712]{2,1,0:T(8,128)(2,1)}), bf16[8,8,3712]{2,1,0:T(8,128)(2,1)S(1)}, u32[]{:S(2)}, u32[]{:S(2)}) async-start(bf16[8,8,3712]{2,1,0:T(8,128)(2,1)} %fusion.3), calls=%async_computation.5 | async-start | bytes 950272 | tf_op jit(solution)/shard_map/all_to_all | solution.py:221
  175.9 2.0 fusion.41
  178.0 0.8 copy.29
  178.8 0.8 copy.30
  179.7 0.8 copy.28
  180.4 5.5 %reduce-scatter.2.cloned.1.call-done = bf16[448,384]{1,0:T(8,128)(2,1)} async-done(((bf16[3584,384]{1,0:T(8,128)(2,1)}), bf16[448,384]{1,0:T(8,128)(2,1)}) %reduce-scatter.2.cloned.1.call-update) | async-done | bytes 344080 | tf_op jit(solution)/shard_map/reduce_scatter | solution.py:211
  185.9 1.0 convert_element_type.62
  186.9 0.9 slice_bitcast_fusion
  187.8 2.8 %all-to-all-done.4 = bf16[8,8,3712]{2,1,0:T(8,128)(2,1)S(1)} async-done(((bf16[8,8,3712]{2,1,0:T(8,128)(2,1)}), bf16[8,8,3712]{2,1,0:T(8,128)(2,1)S(1)}, u32[]{:S(2)}, u32[]{:S(2)}) %all-to-all-start.4) | async-done | bytes 475168 | tf_op jit(solution)/shard_map/all_to_all | solution.py:221
  190.7 1.4 convolution_convert_fusion
  (31 shorter events, 3.3 us)
Async XLA Ops:
  7.2 4.5 %copy-start = (bf16[128,3584]{1,0:T(8,128)(2,1)S(1)}, bf16[128,3584]{1,0:T(8,128)(2,1)}, u32[]{:S(2)}) copy-start(bf16[128,3584]{1,0:T(8,128)(2,1)} %param.7) | copy-start | bytes 2752516
  7.2 62.5 %all-gather.3.cloned.1.call-start = ((), (), s32[]{:S(2)}) async-start(), calls=%async_computation.6 | async-start | bytes 3096576 | tf_op jit(solution)/shard_map/all_gather | solution.py:168
  14.3 21.7 %all-to-all-start = ((bf16[4,8,7296]{2,1,0:T(8,128)(2,1)}), bf16[4,8,7296]{2,1,0:T(8,128)(2,1)S(1)}, u32[]{:S(2)}, u32[]{:S(2)}) async-start(bf16[4,8,7296]{2,1,0:T(8,128)(2,1)} %maximum_bitcast_fusion), calls=%async_computation | async-start | bytes 933888 | tf_op jit(solution)/shard_map/all_to_all | solution.py:190
  37.1 26.1 %all-to-all-start.1 = ((bf16[4,24,3584]{2,1,0:T(8,128)(2,1)}), bf16[4,24,3584]{2,1,0:T(8,128)(2,1)S(1)}, u32[]{:S(2)}, u32[]{:S(2)}) async-start(bf16[4,24,3584]{2,1,0:T(8,128)(2,1)} %broadcast_in_dim.97), calls=%async_computation.1 | async-start | bytes 1376256 | tf_op jit(solution)/shard_map/all_to_all | solution.py:24
  65.1 37.9 %all-to-all-start.2 = ((bf16[4,96,3712]{2,1,0:T(8,128)(2,1)}), bf16[4,96,3712]{2,1,0:T(8,128)(2,1)}, u32[]{:S(2)}, u32[]{:S(2)}) async-start(bf16[4,96,3712]{2,1,0:T(8,128)(2,1)} %broadcast_in_dim.101), calls=%async_computation.2 | async-start | bytes 5701632 | tf_op jit(solution)/shard_map/all_to_all | solution.py:24
  69.7 39.2 %all-gather.5.cloned.1.call-start = ((), (), s32[]{:S(2)}) async-start(), calls=%async_computation.7 | async-start | bytes 2457600 | tf_op jit(solution)/shard_map/all_gather | solution.py:205
  125.7 38.9 %all-to-all-start.3 = ((bf16[8,48,3712]{2,1,0:T(8,128)(2,1)}), bf16[8,48,3712]{2,1,0:T(8,128)(2,1)}, u32[]{:S(2)}, u32[]{:S(2)}) async-start(bf16[8,48,3712]{2,1,0:T(8,128)(2,1)} %bitcast.65), calls=%async_computation.4 | async-start | bytes 5701632 | tf_op jit(solution)/shard_map/all_to_all | solution.py:215
  130.1 55.8 %reduce-scatter.2.cloned.1.call-start = ((), (), s32[]{:S(2)}) async-start(), calls=%async_computation.8 | async-start | bytes 3096576 | tf_op jit(solution)/shard_map/reduce_scatter | solution.py:211
  167.8 22.8 %all-to-all-start.4 = ((bf16[8,8,3712]{2,1,0:T(8,128)(2,1)}), bf16[8,8,3712]{2,1,0:T(8,128)(2,1)S(1)}, u32[]{:S(2)}, u32[]{:S(2)}) async-start(bf16[8,8,3712]{2,1,0:T(8,128)(2,1)} %fusion.3), calls=%async_computation.5 | async-start | bytes 950272 | tf_op jit(solution)/shard_map/all_to_all | solution.py:221
  177.8 14.3 %copy-start.1 = (s32[128,8]{0,1:T(8,128)S(1)}, s32[128,8]{0,1:T(8,128)}, u32[]{:S(2)}) copy-start(s32[128,8]{0,1:T(8,128)} %param.9) | copy-start | bytes 12292
Sparse Core Ops, SparseCore 0:
  10.1 54.1 all-gather.2
  73.2 35.6 all-gather.4
  133.8 52.0 reduce-scatter.1

commit v8 on v6

--- a/solution.py
+++ b/solution.py
@@ -28,21 +28,26 @@
 def weight_grads(x, dy_low, dy_high, d_gate_up, hidden_gated, features):
     rows = x.shape[0]
     low = dy_low.shape[1] // CHUNK
-    over_rows = (((0,), (0,)), ((), ()))
-
-    def kernel(x_ref, low_ref, high_ref, d_ref, h_ref, o_ref):
-        def product(a, b):
-            return lax.dot_general(a, b, over_rows, preferred_element_type=F32).astype(BF)
-
-        o_ref[:, : 2 * LANES] = product(x_ref[...], d_ref[...])
+
+    def kernel(x_ref, low_ref, high_ref, d_ref, h_ref, o_ref, d_turned, h_turned):
+        def product(turned, columns):
+            out = jnp.dot(turned[...], columns[...], preferred_element_type=F32)
+            return out.astype(BF).T
+
+        @pl.when(pl.program_id(0) == 0)
+        def _():
+            d_turned[...] = d_ref[...].T
+            h_turned[...] = h_ref[...].T
+
+        o_ref[:, : 2 * LANES] = product(d_turned, x_ref)
 
         @pl.when(pl.program_id(0) < low)
         def _():
-            o_ref[:, 2 * LANES :] = product(low_ref[...], h_ref[...])
+            o_ref[:, 2 * LANES :] = product(h_turned, low_ref)
 
         @pl.when(pl.program_id(0) >= low)
         def _():
-            o_ref[:, 2 * LANES :] = product(high_ref[...], h_ref[...])
+            o_ref[:, 2 * LANES :] = product(h_turned, high_ref)
 
     return pl.pallas_call(
         kernel,
@@ -56,7 +61,8 @@
         ],
         out_specs=pl.BlockSpec((CHUNK, 3 * LANES), lambda j: (j, 0)),
         out_shape=jax.ShapeDtypeStruct((features, 3 * LANES), BF),
-        compiler_params=pltpu.CompilerParams(vmem_limit_bytes=32 << 20),
+        scratch_shapes=[pltpu.VMEM((2 * LANES, rows), BF), pltpu.VMEM((LANES, rows), BF)],
+        compiler_params=pltpu.CompilerParams(vmem_limit_bytes=58 << 20),
         cost_estimate=pl.CostEstimate(
             flops=2 * rows * features * 3 * LANES,
             bytes_accessed=2 * features * (2 * rows + 3 * LANES),

time: 196 us -> 197 us (level)
  local copies, waits for them, and re-layouts: 14.3 us -> 11.9 us
  Pallas kernels: 6.64 us -> 8.76 us
    unnamed x17 -> x13, local copies, waits for them, and re-layouts: 5.41 us -> 2.32 us
    pallas_call x1, Pallas kernels: 6.64 us -> 8.76 us  [weight_grads(): pl.pallas_call(kernel, grid=(features // CHUNK,), in_specs=[pl.BlockSpec(...]
  transfers between devices with their start and end apart: 8 -> 8, of which waited for: 6 -> 5; matrix products, arithmetic and copies ran while one was open for 16% -> 17% of each run, Pallas kernels for 3% -> 4%
where the time goes in v8:
time: 197 us; the launch traced here: 196 us
  waiting for transfers between devices  66.5 us (34%)
  starting transfers between devices  37.2 us (19%)
  blocking collectives  25 us (13%)
  matrix products  18.6 us (9%)
  other arithmetic  14.2 us (7%)
  between operations  14 us (7%)
  local copies, waits for them, and re-layouts  11.9 us (6%)
  Pallas kernels  8.76 us (4%)
    all_to_all x1, waiting for transfers between devices, shards(): lax.all_to_all(back, ('x', 'zl'), split_axis=0, concat_axis=0, tiled=True)  23.2 us
    dot_general x11, matrix products, dot(): return jnp.einsum(eq, a, b, preferred_element_type=F32)  18.6 us
    all_to_all x2, waiting for transfers between devices, spread(): got = lax.all_to_all(copies, axes, split_axis=0, concat_axis=0, tiled=True)  16.8 us
    reduce_scatter x1, waiting for transfers between devices, shards(): lax.psum_scatter(grads, DP, scatter_dimension=0, tiled=True).astype(F32)  15.6 us
    all_gather x1, blocking collectives, shards(): tok_half = lax.all_gather(tok_rows, 'x', axis=0, tiled=True)  12.8 us
    all_to_all x2, starting transfers between devices, spread(): got = lax.all_to_all(copies, axes, split_axis=0, concat_axis=0, tiled=True)  12.3 us
    all_gather x1, blocking collectives, shards(): cot_high = lax.all_gather(cot_half[:, SPLIT:], 'x', axis=0, tiled=True)  12.1 us
    all_to_all x1, starting transfers between devices, shards(): rows = lax.all_to_all(rows, 'ex', split_axis=0, concat_axis=0, tiled=True)  10.8 us
  transfers between devices with their start and end apart: 8, of which 5 were waited for; matrix products, arithmetic and copies ran while one was open for 17% of the time, Pallas kernels for 4%

profile of v8, /device:TPU:1, one launch (start us, length us, event | category | flops | bytes accessed | tf_op | source)
XLA Modules:
  0.0 195.9 jit_solution(6802748879767602882)
XLA Ops:
  7.2 1.9 pad_maximum_fusion
  11.9 1.5 convolution_convert_fusion.3
  13.5 0.8 maximum_bitcast_fusion
  14.3 10.8 %all-to-all-start = ((bf16[4,8,7296]{2,1,0:T(8,128)(2,1)}), bf16[4,8,7296]{2,1,0:T(8,128)(2,1)S(1)}, u32[]{:S(2)}, u32[]{:S(2)}) async-start(bf16[4,8,7296]{2,1,0:T(8,128)(2,1)} %maximum_bitcast_fusion), calls=%async_computation | async-start | bytes 933888 | tf_op jit(solution)/shard_map/all_to_all | solution.py:106
  25.2 10.8 %all-to-all-done = bf16[4,8,7296]{2,1,0:T(8,128)(2,1)S(1)} async-done(((bf16[4,8,7296]{2,1,0:T(8,128)(2,1)}), bf16[4,8,7296]{2,1,0:T(8,128)(2,1)S(1)}, u32[]{:S(2)}, u32[]{:S(2)}) %all-to-all-start) | async-done | bytes 466976 | tf_op jit(solution)/shard_map/all_to_all | solution.py:106
  36.2 0.9 broadcast_in_dim.64
  37.1 7.7 %all-to-all-start.1 = ((bf16[4,24,3584]{2,1,0:T(8,128)(2,1)}), bf16[4,24,3584]{2,1,0:T(8,128)(2,1)S(1)}, u32[]{:S(2)}, u32[]{:S(2)}) async-start(bf16[4,24,3584]{2,1,0:T(8,128)(2,1)} %broadcast_in_dim.64), calls=%async_computation.1 | async-start | bytes 1376256 | tf_op jit(solution)/shard_map/all_to_all | solution.py:24
  45.1 12.8 %all_gather.13 = bf16[96,3712]{1,0:T(8,128)(2,1)S(1)} all-gather(bf16[24,3712]{1,0:T(8,128)(2,1)S(1)} %convolution_convert_fusion.4), channel_id=1, replica_groups=mesh['yh'=4,'core'=2,'ex'=4,'zl'=2,'x'=4,'yl'=2] {'x'}, dimensions={0}, use_global_device_ids=true | all-gather | bytes 890880 | tf_op jit(solution)/shard_map/all_gather | solution.py:117
  57.9 5.4 %all-to-all-done.1 = bf16[4,24,3584]{2,1,0:T(8,128)(2,1)S(1)} async-done(((bf16[4,24,3584]{2,1,0:T(8,128)(2,1)}), bf16[4,24,3584]{2,1,0:T(8,128)(2,1)S(1)}, u32[]{:S(2)}, u32[]{:S(2)}) %all-to-all-start.1) | async-done | bytes 688160 | tf_op jit(solution)/shard_map/all_to_all | solution.py:24
  63.2 1.8 broadcast_in_dim.109
  65.1 4.6 %all-to-all-start.2 = ((bf16[4,96,3712]{2,1,0:T(8,128)(2,1)}), bf16[4,96,3712]{2,1,0:T(8,128)(2,1)}, u32[]{:S(2)}, u32[]{:S(2)}) async-start(bf16[4,96,3712]{2,1,0:T(8,128)(2,1)} %broadcast_in_dim.109), calls=%async_computation.2 | async-start | bytes 5701632 | tf_op jit(solution)/shard_map/all_to_all | solution.py:24
  69.8 0.8 slice.58
  70.7 1.9 fusion.63
  72.7 5.7 %fusion.8 = bf16[384,3712]{1,0:T(8,128)(2,1)} fusion(bf16[128,3584]{1,0:T(8,128)(2,1)S(1)} %bitcast.86, bf16[128,3584]{1,0:T(8,128)(2,1)S(1)} %bitcast.88, bf16[128,3712]{1,0:T(8,128)(2,1)S(1)} %pad_convert_fusion), kind=kLoop, calls=%fused_computation.18 | loop fusion | flops 17104896 | bytes 5636096 | tf_op jit(solution)/shard_map/concatenate | solution.py:132
  78.3 12.1 %all_gather.15.high_ref = bf16[384,1024]{1,0:T(8,128)(2,1)S(1)} all-gather(bf16[96,1024]{1,0:T(8,128)(2,1)S(1)} %slice.59), channel_id=1, replica_groups=mesh['yh'=4,'core'=2,'ex'=4,'zl'=2,'x'=4,'yl'=2] {'x'}, dimensions={0}, use_global_device_ids=true | all-gather | bytes 983040 | tf_op jit(solution)/shard_map/all_gather | solution.py:122
  90.5 1.1 fusion.23
  91.5 11.4 %all-to-all-done.2 = bf16[4,96,3712]{2,1,0:T(8,128)(2,1)} async-done(((bf16[4,96,3712]{2,1,0:T(8,128)(2,1)}), bf16[4,96,3712]{2,1,0:T(8,128)(2,1)}, u32[]{:S(2)}, u32[]{:S(2)}) %all-to-all-start.2) | async-done | bytes 2850848 | tf_op jit(solution)/shard_map/all_to_all | solution.py:24
  102.9 4.4 %fusion.11 = f32[4,4,24,384]{3,2,0,1:T(8,128)S(1)} fusion(bf16[4,4,24,3712]{3,2,1,0:T(8,128)(2,1)} %bitcast.24, bf16[384,3712]{1,0:T(8,128)(2,1)} %fusion.8), kind=kOutput, calls=%fused_computation.22 | convolution fusion | flops 1094713344 | bytes 6291456 | tf_op jit(solution)/shard_map/rd,hd->rh/dot_general | solution.py:76
  107.4 0.9 copy.38
  108.3 2.8 %fusion.28 = (bf16[384]{0:T(512)(128)(2,1)S(1)}, bf16[384,128]{1,0:T(8,128)(2,1)S(1)}, bf16[384,128]{1,0:T(8,128)(2,1)S(1)}, bf16[384,128]{1,0:T(8,128)(2,1)S(1)}) fusion(f32[384,384]{1,0:T(8,128)} %bitcast.100, f32[384,128]{1,0:T(8,128)} %fusion.23, bf16[384,2560]{1,0:T(8,128)(2,1)} %all-gather.5.cloned.1.call-done.low_ref, bf16[128,3584]{1,0:T(8,128)(2,1)} %bitcast.96), kind=kOutput, calls=%fused_computation.46 | convolution fusion | flops 252640896 | bytes 3703552 | tf_op jit(solution)/shard_map/rd,hd->rh/dot_general | solution.py:76
  112.0 3.2 %convolution_convert_fusion = bf16[384,3712]{1,0:T(8,128)(2,1)} fusion(bf16[384,3712]{1,0:T(8,128)(2,1)S(1)} %copy-done.1, bf16[384,128]{1,0:T(8,128)(2,1)S(1)} %broadcast_in_dim.114, bf16[384,128]{1,0:T(8,128)(2,1)S(1)} %get-tuple-element.41, bf16[384,128]{1,0:T(8,128)(2,1)S(1)} %get-tuple-element.42), kind=kOutput, calls=%fused_computation.8 | convolution fusion | flops 1097023488 | bytes 5996544 | tf_op jit(solution)/shard_map/rh,hd->rd/dot_general | solution.py:76
  115.2 4.4 %all-to-all-start.3 = ((bf16[8,48,3712]{2,1,0:T(8,128)(2,1)}), bf16[8,48,3712]{2,1,0:T(8,128)(2,1)}, u32[]{:S(2)}, u32[]{:S(2)}) async-start(bf16[8,48,3712]{2,1,0:T(8,128)(2,1)} %bitcast.85), calls=%async_computation.4 | async-start | bytes 5701632 | tf_op jit(solution)/shard_map/all_to_all | solution.py:166
  119.7 1.6 fusion.27.h_ref
  121.3 8.8 %weight_grads.1 = bf16[3584,384]{1,0:T(8,128)(2,1)} custom-call(bf16[384,3712]{1,0:T(8,128)(2,1)} %bitcast.23.x_ref, bf16[384,2560]{1,0:T(8,128)(2,1)} %all-gather.5.cloned.1.call-done.low_ref, bf16[384,1024]{1,0:T(8,128)(2,1)} %copy-done.2, bf16[384,256]{1,0:T(8,128)(2,1)} %bitcast.103, bf16[384,128]{1,0:T(8,128)(2,1)} %fusion.27.h_ref), custom_call_target="tpu_custom_call" | custom-call | flops 1056964608 | bytes 8257536 | tf_op jit(solution)/shard_map/weight_grads/pallas_call | solution.py:52
  130.2 23.2 %all-to-all-done.3 = bf16[8,48,3712]{2,1,0:T(8,128)(2,1)} async-done(((bf16[8,48,3712]{2,1,0:T(8,128)(2,1)}), bf16[8,48,3712]{2,1,0:T(8,128)(2,1)}, u32[]{:S(2)}, u32[]{:S(2)}) %all-to-all-start.3) | async-done | bytes 2850848 | tf_op jit(solution)/shard_map/all_to_all | solution.py:166
  153.3 3.3 %fusion.6 = bf16[8,8,3712]{2,1,0:T(8,128)(2,1)} fusion(bf16[8,48,3712]{2,1,0:T(8,128)(2,1)} %all-to-all-done.3, bf16[64,48]{0,1:T(8,128)(2,1)S(1)} %fusion.31), kind=kOutput, calls=%fused_computation.12 | convolution fusion | flops 182689792 | bytes 3332096 | tf_op jit(solution)/shard_map/ck,kd->cd/dot_general | solution.py:76
  156.6 9.6 %all-to-all-start.4 = ((bf16[8,8,3712]{2,1,0:T(8,128)(2,1)}), bf16[8,8,3712]{2,1,0:T(8,128)(2,1)S(1)}, u32[]{:S(2)}, u32[]{:S(2)}) async-start(bf16[8,8,3712]{2,1,0:T(8,128)(2,1)} %fusion.6), calls=%async_computation.5 | async-start | bytes 950272 | tf_op jit(solution)/shard_map/all_to_all | solution.py:172
  167.1 1.1 dynamic-slice_bitcast_fusion
  169.7 15.6 %reduce-scatter.2.cloned.1.call-done = bf16[448,384]{1,0:T(8,128)(2,1)} async-done(((bf16[3584,384]{1,0:T(8,128)(2,1)}), bf16[448,384]{1,0:T(8,128)(2,1)}) %reduce-scatter.2.cloned.1.call-update) | async-done | bytes 344080 | tf_op jit(solution)/shard_map/reduce_scatter | solution.py:162
  185.2 1.0 convert_element_type.95
  186.3 0.9 slice_bitcast_fusion
  187.3 1.4 convolution_convert_fusion.1
  (49 shorter events, 7.9 us)
Async XLA Ops:
  7.2 4.5 %copy-start = (bf16[128,3584]{1,0:T(8,128)(2,1)S(1)}, bf16[128,3584]{1,0:T(8,128)(2,1)}, u32[]{:S(2)}) copy-start(bf16[128,3584]{1,0:T(8,128)(2,1)} %param.8) | copy-start | bytes 2752516
  7.2 62.6 %all-gather.3.cloned.1.call-start = ((), (), s32[]{:S(2)}) async-start(), calls=%async_computation.6 | async-start | bytes 3096576 | tf_op jit(solution)/shard_map/all_gather | solution.py:84
  14.3 21.7 %all-to-all-start = ((bf16[4,8,7296]{2,1,0:T(8,128)(2,1)}), bf16[4,8,7296]{2,1,0:T(8,128)(2,1)S(1)}, u32[]{:S(2)}, u32[]{:S(2)}) async-start(bf16[4,8,7296]{2,1,0:T(8,128)(2,1)} %maximum_bitcast_fusion), calls=%async_computation | async-start | bytes 933888 | tf_op jit(solution)/shard_map/all_to_all | solution.py:106
  37.1 26.1 %all-to-all-start.1 = ((bf16[4,24,3584]{2,1,0:T(8,128)(2,1)}), bf16[4,24,3584]{2,1,0:T(8,128)(2,1)S(1)}, u32[]{:S(2)}, u32[]{:S(2)}) async-start(bf16[4,24,3584]{2,1,0:T(8,128)(2,1)} %broadcast_in_dim.64), calls=%async_computation.1 | async-start | bytes 1376256 | tf_op jit(solution)/shard_map/all_to_all | solution.py:24
  65.1 37.9 %all-to-all-start.2 = ((bf16[4,96,3712]{2,1,0:T(8,128)(2,1)}), bf16[4,96,3712]{2,1,0:T(8,128)(2,1)}, u32[]{:S(2)}, u32[]{:S(2)}) async-start(bf16[4,96,3712]{2,1,0:T(8,128)(2,1)} %broadcast_in_dim.109), calls=%async_computation.2 | async-start | bytes 5701632 | tf_op jit(solution)/shard_map/all_to_all | solution.py:24
  69.7 38.6 %all-gather.5.cloned.1.call-start = ((), (), s32[]{:S(2)}) async-start(), calls=%async_computation.7 | async-start | bytes 2457600 | tf_op jit(solution)/shard_map/all_gather | solution.py:121
  72.6 17.8 %copy-start.3 = (bf16[8,1,16,3584]{3,2,1,0:T(8,128)(2,1)}, bf16[8,1,16,3584]{3,2,1,0:T(8,128)(2,1)S(1)}, u32[]{:S(2)}) copy-start(bf16[8,1,16,3584]{3,2,1,0:T(8,128)(2,1)S(1)} %get-tuple-element.38) | copy-start | bytes 2752516
  90.4 16.9 %copy-start.2 = (bf16[384,1024]{1,0:T(8,128)(2,1)}, bf16[384,1024]{1,0:T(8,128)(2,1)S(1)}, u32[]{:S(2)}) copy-start(bf16[384,1024]{1,0:T(8,128)(2,1)S(1)} %all_gather.15.high_ref) | copy-start | bytes 2359300
  108.3 3.7 %copy-start.1 = (bf16[384,3712]{1,0:T(8,128)(2,1)S(1)}, bf16[384,3712]{1,0:T(8,128)(2,1)}, u32[]{:S(2)}) copy-start(bf16[384,3712]{1,0:T(8,128)(2,1)} %fusion.8) | copy-start | bytes 8552452
  115.2 38.1 %all-to-all-start.3 = ((bf16[8,48,3712]{2,1,0:T(8,128)(2,1)}), bf16[8,48,3712]{2,1,0:T(8,128)(2,1)}, u32[]{:S(2)}, u32[]{:S(2)}) async-start(bf16[8,48,3712]{2,1,0:T(8,128)(2,1)} %bitcast.85), calls=%async_computation.4 | async-start | bytes 5701632 | tf_op jit(solution)/shard_map/all_to_all | solution.py:166
  119.6 65.6 %reduce-scatter.2.cloned.1.call-start = ((), (), s32[]{:S(2)}) async-start(), calls=%async_computation.8 | async-start | bytes 3096576 | tf_op jit(solution)/shard_map/reduce_scatter | solution.py:162
  156.6 30.5 %all-to-all-start.4 = ((bf16[8,8,3712]{2,1,0:T(8,128)(2,1)}), bf16[8,8,3712]{2,1,0:T(8,128)(2,1)S(1)}, u32[]{:S(2)}, u32[]{:S(2)}) async-start(bf16[8,8,3712]{2,1,0:T(8,128)(2,1)} %fusion.6), calls=%async_computation.5 | async-start | bytes 950272 | tf_op jit(solution)/shard_map/all_to_all | solution.py:172
  166.2 22.6 %copy-start.4 = (s32[128,8]{0,1:T(8,128)S(1)}, s32[128,8]{0,1:T(8,128)}, u32[]{:S(2)}) copy-start(s32[128,8]{0,1:T(8,128)} %param.9) | copy-start | bytes 12292
Sparse Core Ops, SparseCore 0:
  10.1 54.1 all-gather.2
  72.6 35.6 all-gather.4
  130.2 55.0 reduce-scatter.1

commit v9 on v6

--- a/solution.py
+++ b/solution.py
@@ -75,7 +75,7 @@
     hidden_dev = w_gate.shape[2]
 
     mine = jnp.concatenate([w_gate[0].T, w_up[0].T, w_down[0].T], axis=0)
-    gathered = lax.all_gather(mine, DP, axis=0, tiled=True)
+    gathered = lax.all_gather(mine, "yh", axis=0, tiled=True)
     n_dp = lax.axis_size(DP)
 
     ids = route_ids.T
@@ -110,11 +110,19 @@
     block = EXPERTS * CAP
     tok_half = lax.all_gather(tok_rows, "x", axis=0, tiled=True)
     cot_half = spread(cot_rows, ("zl", "yl"))
-    cot_half, gathered = lax.optimization_barrier((cot_half, gathered))
+    tok_half, cot_half, gathered = lax.optimization_barrier((tok_half, cot_half, gathered))
     slot_all = spread(tok_half, ("zl", "yl"))
     cot_low = lax.all_gather(cot_half[:, :SPLIT], "x", axis=0, tiled=True)
     cot_high = lax.all_gather(cot_half[:, SPLIT:], "x", axis=0, tiled=True)
-    gathered = gathered.reshape(n_dp, 3, hidden_dev, features)
+    other = lax.ppermute(gathered, "core", [(0, 1), (1, 0)])
+    even = lax.axis_index("core") == 0
+    gathered = jnp.stack(
+        [
+            jnp.where(even, mixed[0], mixed[1]).reshape(n_dp // 2, 3, hidden_dev, features)
+            for mixed in ((gathered, other), (other, gathered))
+        ],
+        axis=1,
+    ).reshape(n_dp, 3, hidden_dev, features)
 
     def reorder(values):
         v = values.reshape(4, 4, block, values.shape[-1])

time: 196 us -> 197 us (level)
  waiting for transfers between devices: 68.2 us -> 64.8 us
  other arithmetic: 12.6 us -> 15.7 us
    ppermute x0 -> x1, starting transfers between devices: none -> 2.7 us  [shards(): other = lax.ppermute(gathered, 'core', [(0, 1), (1, 0)])]
    all_to_all x2, waiting for transfers between devices: 17.5 us -> 15.3 us  [spread(): got = lax.all_to_all(copies, axes, split_axis=0, concat_axis=0, tiled=True)]
    unnamed x17 -> x19, local copies, waits for them, and re-layouts: 5.41 us -> 6.68 us
  transfers between devices with their start and end apart: 8 -> 9, of which waited for: 6 -> 5; matrix products, arithmetic and copies ran while one was open for 16% -> 17% of each run, Pallas kernels for 3% -> 3%
where the time goes in v9:
time: 197 us; the launch traced here: 196 us
  waiting for transfers between devices  64.8 us (33%)
  starting transfers between devices  38 us (19%)
  blocking collectives  25 us (13%)
  matrix products  17.6 us (9%)
  other arithmetic  15.7 us (8%)
  local copies, waits for them, and re-layouts  14.1 us (7%)
  between operations  14.1 us (7%)
  Pallas kernels  6.65 us (3%)
    all_to_all x1, waiting for transfers between devices, shards(): lax.all_to_all(back, ('x', 'zl'), split_axis=0, concat_axis=0, tiled=True)  24.5 us
    dot_general x11, matrix products, dot(): return jnp.einsum(eq, a, b, preferred_element_type=F32)  17.6 us
    all_to_all x2, waiting for transfers between devices, spread(): got = lax.all_to_all(copies, axes, split_axis=0, concat_axis=0, tiled=True)  15.3 us
    reduce_scatter x1, waiting for transfers between devices, shards(): lax.psum_scatter(grads, DP, scatter_dimension=0, tiled=True).astype(F32)  14.1 us
    all_gather x1, blocking collectives, shards(): tok_half = lax.all_gather(tok_rows, 'x', axis=0, tiled=True)  12.8 us
    all_to_all x2, starting transfers between devices, spread(): got = lax.all_to_all(copies, axes, split_axis=0, concat_axis=0, tiled=True)  12.3 us
    all_gather x1, blocking collectives, shards(): cot_high = lax.all_gather(cot_half[:, SPLIT:], 'x', axis=0, tiled=True)  12.2 us
    all_to_all x1, starting transfers between devices, shards(): rows = lax.all_to_all(rows, 'ex', split_axis=0, concat_axis=0, tiled=True)  10.8 us
  transfers between devices with their start and end apart: 9, of which 5 were waited for; matrix products, arithmetic and copies ran while one was open for 17% of the time, Pallas kernels for 3%

profile of v9, /device:TPU:1, one launch (start us, length us, event | category | flops | bytes accessed | tf_op | source)
XLA Modules:
  0.0 195.9 jit_solution(8725736353615292207)
XLA Ops:
  7.2 1.8 pad_maximum_fusion.1
  11.9 1.5 convolution_convert_fusion.3
  14.3 10.8 %all-to-all-start = ((bf16[4,8,7296]{2,1,0:T(8,128)(2,1)}), bf16[4,8,7296]{2,1,0:T(8,128)(2,1)S(1)}, u32[]{:S(2)}, u32[]{:S(2)}) async-start(bf16[4,8,7296]{2,1,0:T(8,128)(2,1)} %maximum_bitcast_fusion), calls=%async_computation | async-start | bytes 933888 | tf_op jit(solution)/shard_map/all_to_all | solution.py:100
  25.1 10.8 %all-to-all-done = bf16[4,8,7296]{2,1,0:T(8,128)(2,1)S(1)} async-done(((bf16[4,8,7296]{2,1,0:T(8,128)(2,1)}), bf16[4,8,7296]{2,1,0:T(8,128)(2,1)S(1)}, u32[]{:S(2)}, u32[]{:S(2)}) %all-to-all-start) | async-done | bytes 466976 | tf_op jit(solution)/shard_map/all_to_all | solution.py:100
  36.2 0.9 broadcast_in_dim.64
  37.1 7.7 %all-to-all-start.1 = ((bf16[4,24,3584]{2,1,0:T(8,128)(2,1)}), bf16[4,24,3584]{2,1,0:T(8,128)(2,1)S(1)}, u32[]{:S(2)}, u32[]{:S(2)}) async-start(bf16[4,24,3584]{2,1,0:T(8,128)(2,1)} %broadcast_in_dim.64), calls=%async_computation.1 | async-start | bytes 1376256 | tf_op jit(solution)/shard_map/all_to_all | solution.py:24
  45.0 12.8 %all_gather.12 = bf16[96,3712]{1,0:T(8,128)(2,1)S(1)} all-gather(bf16[24,3712]{1,0:T(8,128)(2,1)S(1)} %convolution_convert_fusion.5), channel_id=1, replica_groups=mesh['yh'=4,'core'=2,'ex'=4,'zl'=2,'x'=4,'yl'=2] {'x'}, dimensions={0}, use_global_device_ids=true | all-gather | bytes 890880 | tf_op jit(solution)/shard_map/all_gather | solution.py:111
  57.8 5.4 %all-to-all-done.1 = bf16[4,24,3584]{2,1,0:T(8,128)(2,1)S(1)} async-done(((bf16[4,24,3584]{2,1,0:T(8,128)(2,1)}), bf16[4,24,3584]{2,1,0:T(8,128)(2,1)S(1)}, u32[]{:S(2)}, u32[]{:S(2)}) %all-to-all-start.1) | async-done | bytes 688160 | tf_op jit(solution)/shard_map/all_to_all | solution.py:24
  63.2 2.7 %collective-permute-start = (bf16[192,3584]{1,0:T(8,128)(2,1)}, bf16[192,3584]{1,0:T(8,128)(2,1)}, u32[]{:S(2)}, u32[]{:S(2)}) collective-permute-start(bf16[192,3584]{1,0:T(8,128)(2,1)} %all-gather.3.cloned.1.call-done), channel_id=1, source_target_pairs={{0,64},{64,0},{1,65},{65,1},{2,66},{66,2},{3,67},{67,3},{4,68},{68... | collective-permute-start | bytes 4128776 | tf_op jit(solution)/shard_map/ppermute | solution.py:117
  65.9 1.8 broadcast_in_dim.109
  67.8 4.6 %all-to-all-start.2 = ((bf16[4,96,3712]{2,1,0:T(8,128)(2,1)}), bf16[4,96,3712]{2,1,0:T(8,128)(2,1)}, u32[]{:S(2)}, u32[]{:S(2)}) async-start(bf16[4,96,3712]{2,1,0:T(8,128)(2,1)} %broadcast_in_dim.109), calls=%async_computation.2 | async-start | bytes 5701632 | tf_op jit(solution)/shard_map/all_to_all | solution.py:24
  72.4 1.0 pad_convert_fusion
  74.3 12.2 %all_gather.15.high_ref = bf16[384,1024]{1,0:T(8,128)(2,1)S(1)} all-gather(bf16[96,1024]{1,0:T(8,128)(2,1)S(1)} %slice.59), channel_id=1, replica_groups=mesh['yh'=4,'core'=2,'ex'=4,'zl'=2,'x'=4,'yl'=2] {'x'}, dimensions={0}, use_global_device_ids=true | all-gather | bytes 983040 | tf_op jit(solution)/shard_map/all_gather | solution.py:116
  86.6 1.9 broadcast_select_fusion.1
  89.2 0.9 copy-done.4
  90.5 5.7 %fusion.8 = bf16[384,3712]{1,0:T(8,128)(2,1)} fusion(bf16[128,3584]{1,0:T(8,128)(2,1)S(1)} %bitcast.92, bf16[128,3584]{1,0:T(8,128)(2,1)S(1)} %bitcast.94, bf16[128,3712]{1,0:T(8,128)(2,1)S(1)} %copy-done.5), kind=kLoop, calls=%fused_computation.18 | loop fusion | flops 17104896 | bytes 5636096 | tf_op jit(solution)/shard_map/concatenate | solution.py:134
  96.5 9.9 %all-to-all-done.2 = bf16[4,96,3712]{2,1,0:T(8,128)(2,1)} async-done(((bf16[4,96,3712]{2,1,0:T(8,128)(2,1)}), bf16[4,96,3712]{2,1,0:T(8,128)(2,1)}, u32[]{:S(2)}, u32[]{:S(2)}) %all-to-all-start.2) | async-done | bytes 2850848 | tf_op jit(solution)/shard_map/all_to_all | solution.py:24
  106.4 4.4 %fusion.11 = f32[4,4,24,384]{3,2,0,1:T(8,128)S(1)} fusion(bf16[4,4,24,3712]{3,2,1,0:T(8,128)(2,1)} %bitcast.26, bf16[384,3712]{1,0:T(8,128)(2,1)} %fusion.8), kind=kOutput, calls=%fused_computation.25 | convolution fusion | flops 1094713344 | bytes 6291456 | tf_op jit(solution)/shard_map/rd,hd->rh/dot_general | solution.py:70
  110.9 2.6 %fusion.28 = (bf16[384]{0:T(512)(128)(2,1)S(1)}, bf16[384,128]{1,0:T(8,128)(2,1)S(1)}, bf16[384,128]{1,0:T(8,128)(2,1)S(1)}, bf16[384,128]{1,0:T(8,128)(2,1)S(1)}) fusion(f32[384,384]{1,0:T(8,128)S(1)} %bitcast.105, f32[384,128]{1,0:T(8,128)S(1)} %fusion.23, bf16[384,2560]{1,0:T(8,128)(2,1)} %all-gather.5.cloned.1.call-done.low_ref, ...), kind=kOutput, calls=%fused_computation.49 | convolution fusion | flops 252640896 | bytes 3703552 | tf_op jit(solution)/shard_map/rd,hd->rh/dot_general | solution.py:70
  113.7 3.2 %convolution_convert_fusion = bf16[384,3712]{1,0:T(8,128)(2,1)} fusion(bf16[384,3712]{1,0:T(8,128)(2,1)S(1)} %copy-done.3, bf16[384,128]{1,0:T(8,128)(2,1)S(1)} %broadcast_in_dim.114, bf16[384,128]{1,0:T(8,128)(2,1)S(1)} %get-tuple-element.45, bf16[384,128]{1,0:T(8,128)(2,1)S(1)} %get-tuple-element.46), kind=kOutput, calls=%fused_computation.8 | convolution fusion | flops 1097023488 | bytes 5996544 | tf_op jit(solution)/shard_map/rh,hd->rd/dot_general | solution.py:70
  116.9 4.4 %all-to-all-start.3 = ((bf16[8,48,3712]{2,1,0:T(8,128)(2,1)}), bf16[8,48,3712]{2,1,0:T(8,128)(2,1)}, u32[]{:S(2)}, u32[]{:S(2)}) async-start(bf16[8,48,3712]{2,1,0:T(8,128)(2,1)} %bitcast.88), calls=%async_computation.4 | async-start | bytes 5701632 | tf_op jit(solution)/shard_map/all_to_all | solution.py:168
  121.4 1.5 copy-done.2
  123.0 6.6 %weight_grads.1 = bf16[3584,384]{1,0:T(8,128)(2,1)S(1)} custom-call(bf16[384,3712]{1,0:T(8,128)(2,1)} %bitcast.25.x_ref, bf16[384,2560]{1,0:T(8,128)(2,1)S(1)} %copy-done.2, bf16[384,1024]{1,0:T(8,128)(2,1)S(1)} %all_gather.15.high_ref, bf16[384,256]{1,0:T(8,128)(2,1)S(1)} %bitcast.87, bf16[384,128]{1,0:T(8,128)(2,1)S(1)} %fusion.27.h_ref), custom_call_target="tpu_custom_call" | custom-call | flops 1056964608 | bytes 8257536 | tf_op jit(solution)/shard_map/weight_grads/pallas_call | solution.py:47
  129.6 1.5 copy-done.1
  131.3 24.5 %all-to-all-done.3 = bf16[8,48,3712]{2,1,0:T(8,128)(2,1)} async-done(((bf16[8,48,3712]{2,1,0:T(8,128)(2,1)}), bf16[8,48,3712]{2,1,0:T(8,128)(2,1)}, u32[]{:S(2)}, u32[]{:S(2)}) %all-to-all-start.3) | async-done | bytes 2850848 | tf_op jit(solution)/shard_map/all_to_all | solution.py:168
  155.7 3.3 %fusion.6 = bf16[8,8,3712]{2,1,0:T(8,128)(2,1)} fusion(bf16[8,48,3712]{2,1,0:T(8,128)(2,1)} %all-to-all-done.3, bf16[64,48]{0,1:T(8,128)(2,1)S(1)} %fusion.31), kind=kOutput, calls=%fused_computation.12 | convolution fusion | flops 182689792 | bytes 3332096 | tf_op jit(solution)/shard_map/ck,kd->cd/dot_general | solution.py:70
  159.0 7.6 %all-to-all-start.4 = ((bf16[8,8,3712]{2,1,0:T(8,128)(2,1)}), bf16[8,8,3712]{2,1,0:T(8,128)(2,1)S(1)}, u32[]{:S(2)}, u32[]{:S(2)}) async-start(bf16[8,8,3712]{2,1,0:T(8,128)(2,1)} %fusion.6), calls=%async_computation.5 | async-start | bytes 950272 | tf_op jit(solution)/shard_map/all_to_all | solution.py:174
  166.7 1.0 dynamic-slice_bitcast_fusion.2
  168.5 1.1 dynamic-slice_bitcast_fusion
  171.1 14.1 %reduce-scatter.2.cloned.1.call-done = bf16[448,384]{1,0:T(8,128)(2,1)} async-done(((bf16[3584,384]{1,0:T(8,128)(2,1)}), bf16[448,384]{1,0:T(8,128)(2,1)}) %reduce-scatter.2.cloned.1.call-update) | async-done | bytes 344080 | tf_op jit(solution)/shard_map/reduce_scatter | solution.py:164
  185.2 1.0 convert_element_type.95
  187.2 1.4 convolution_convert_fusion.1
  (60 shorter events, 11.0 us)
Async XLA Ops:
  7.2 4.4 %copy-start = (bf16[128,3584]{1,0:T(8,128)(2,1)S(1)}, bf16[128,3584]{1,0:T(8,128)(2,1)}, u32[]{:S(2)}) copy-start(bf16[128,3584]{1,0:T(8,128)(2,1)} %param.8) | copy-start | bytes 2752516
  7.2 56.0 %all-gather.3.cloned.1.call-start = ((), (), s32[]{:S(2)}) async-start(), calls=%async_computation.6 | async-start | bytes 1720320 | tf_op jit(solution)/shard_map/all_gather | solution.py:78
  14.3 21.7 %all-to-all-start = ((bf16[4,8,7296]{2,1,0:T(8,128)(2,1)}), bf16[4,8,7296]{2,1,0:T(8,128)(2,1)S(1)}, u32[]{:S(2)}, u32[]{:S(2)}) async-start(bf16[4,8,7296]{2,1,0:T(8,128)(2,1)} %maximum_bitcast_fusion), calls=%async_computation | async-start | bytes 933888 | tf_op jit(solution)/shard_map/all_to_all | solution.py:100
  37.1 26.1 %all-to-all-start.1 = ((bf16[4,24,3584]{2,1,0:T(8,128)(2,1)}), bf16[4,24,3584]{2,1,0:T(8,128)(2,1)S(1)}, u32[]{:S(2)}, u32[]{:S(2)}) async-start(bf16[4,24,3584]{2,1,0:T(8,128)(2,1)} %broadcast_in_dim.64), calls=%async_computation.1 | async-start | bytes 1376256 | tf_op jit(solution)/shard_map/all_to_all | solution.py:24
  63.2 23.3 %collective-permute-start = (bf16[192,3584]{1,0:T(8,128)(2,1)}, bf16[192,3584]{1,0:T(8,128)(2,1)}, u32[]{:S(2)}, u32[]{:S(2)}) collective-permute-start(bf16[192,3584]{1,0:T(8,128)(2,1)} %all-gather.3.cloned.1.call-done), channel_id=1, source_target_pairs={{0,64},{64,0},{1,65},{65,1},{2,66},{66,2},{3,67},{67,3},{4,68},{68... | collective-permute-start | bytes 4128776 | tf_op jit(solution)/shard_map/ppermute | solution.py:117
  67.8 38.6 %all-to-all-start.2 = ((bf16[4,96,3712]{2,1,0:T(8,128)(2,1)}), bf16[4,96,3712]{2,1,0:T(8,128)(2,1)}, u32[]{:S(2)}, u32[]{:S(2)}) async-start(bf16[4,96,3712]{2,1,0:T(8,128)(2,1)} %broadcast_in_dim.109), calls=%async_computation.2 | async-start | bytes 5701632 | tf_op jit(solution)/shard_map/all_to_all | solution.py:24
  72.4 38.5 %all-gather.5.cloned.1.call-start = ((), (), s32[]{:S(2)}) async-start(), calls=%async_computation.7 | async-start | bytes 2457600 | tf_op jit(solution)/shard_map/all_gather | solution.py:115
  89.0 1.5 copy-start.5
  89.2 0.9 copy-start.4
  89.2 7.0 %copy-start.6 = (bf16[8,1,16,3584]{3,2,0,1:T(8,128)(2,1)}, bf16[8,1,16,3584]{3,2,0,1:T(8,128)(2,1)S(1)}, u32[]{:S(2)}) copy-start(bf16[8,1,16,3584]{3,2,0,1:T(8,128)(2,1)S(1)} %get-tuple-element.40) | copy-start | bytes 2752516
  110.9 2.8 %copy-start.3 = (bf16[384,3712]{1,0:T(8,128)(2,1)S(1)}, bf16[384,3712]{1,0:T(8,128)(2,1)}, u32[]{:S(2)}) copy-start(bf16[384,3712]{1,0:T(8,128)(2,1)} %fusion.8) | copy-start | bytes 8552452
  116.9 38.8 %all-to-all-start.3 = ((bf16[8,48,3712]{2,1,0:T(8,128)(2,1)}), bf16[8,48,3712]{2,1,0:T(8,128)(2,1)}, u32[]{:S(2)}, u32[]{:S(2)}) async-start(bf16[8,48,3712]{2,1,0:T(8,128)(2,1)} %bitcast.88), calls=%async_computation.4 | async-start | bytes 5701632 | tf_op jit(solution)/shard_map/all_to_all | solution.py:168
  121.3 63.9 %reduce-scatter.2.cloned.1.call-start = ((), (), s32[]{:S(2)}) async-start(), calls=%async_computation.8 | async-start | bytes 3096576 | tf_op jit(solution)/shard_map/reduce_scatter | solution.py:164
  121.4 1.5 copy-start.2
  129.6 1.5 copy-start.1
  159.0 28.1 %all-to-all-start.4 = ((bf16[8,8,3712]{2,1,0:T(8,128)(2,1)}), bf16[8,8,3712]{2,1,0:T(8,128)(2,1)S(1)}, u32[]{:S(2)}, u32[]{:S(2)}) async-start(bf16[8,8,3712]{2,1,0:T(8,128)(2,1)} %fusion.6), calls=%async_computation.5 | async-start | bytes 950272 | tf_op jit(solution)/shard_map/all_to_all | solution.py:174
  166.7 22.1 %copy-start.7 = (s32[128,8]{0,1:T(8,128)S(1)}, s32[128,8]{0,1:T(8,128)}, u32[]{:S(2)}) copy-start(s32[128,8]{0,1:T(8,128)} %param.9) | copy-start | bytes 12292
Sparse Core Ops, SparseCore 0:
  10.1 52.0 all-gather.2
  75.3 34.8 all-gather.4
  131.3 53.8 reduce-scatter.1

commit v10 on v6

--- a/solution.py
+++ b/solution.py
@@ -56,7 +56,7 @@
         ],
         out_specs=pl.BlockSpec((CHUNK, 3 * LANES), lambda j: (j, 0)),
         out_shape=jax.ShapeDtypeStruct((features, 3 * LANES), BF),
-        compiler_params=pltpu.CompilerParams(vmem_limit_bytes=32 << 20),
+        compiler_params=pltpu.CompilerParams(vmem_limit_bytes=58 << 20),
         cost_estimate=pl.CostEstimate(
             flops=2 * rows * features * 3 * LANES,
             bytes_accessed=2 * features * (2 * rows + 3 * LANES),
@@ -153,8 +153,7 @@
     grads = weight_grads(
         slot_all, cot_low, cot_high, reorder(left[:, : 2 * LANES]), hidden_gated, features
     )
-    grads = lax.psum_scatter(grads, DP, scatter_dimension=0, tiled=True).astype(F32)
-    grads = [grads[None, :, LANES * j : LANES * (j + 1)] for j in range(3)]
+    grads = lax.psum_scatter(grads, DP, scatter_dimension=0, tiled=True)
 
     back = back.reshape(8, 2 * block, wide)
     back = lax.all_to_all(back, ("x", "zl"), split_axis=0, concat_axis=0, tiled=True)
@@ -175,6 +174,9 @@
     score_token = jnp.sum(jnp.where(pick, score_slots, 0.0), axis=1)
     gate_grad = jnp.sum(jnp.where(hits, score_token[:, None, :], 0.0), axis=0).T
 
+    token_grad, gate_grad, grads = lax.optimization_barrier((token_grad, gate_grad, grads))
+    grads = [grads[None, :, LANES * j : LANES * (j + 1)].astype(F32) for j in range(3)]
+
     start = lax.axis_index(DP) * (features // n_dp)
     relaid = [
         lax.dynamic_slice_in_dim(w, start, features // n_dp, axis=1).T[None] for w in slab

time: 196 us -> 195 us (level)
  waiting for transfers between devices: 68.2 us -> 64.5 us
  local copies, waits for them, and re-layouts: 14.3 us -> 11 us
    reduce_scatter x1, waiting for transfers between devices: 14.4 us -> 0.7 us  [shards(): grads = lax.psum_scatter(grads, DP, scatter_dimension=0, tiled=True)]
    all_to_all x1, waiting for transfers between devices: 0.01 us -> 11.7 us  [shards(): lax.all_to_all(home.reshape(2 * EXPERTS, PAD, wide), ('ex', 'yl'), split_...]
    unnamed x17 -> x13, local copies, waits for them, and re-layouts: 5.41 us -> 2.32 us
  transfers between devices with their start and end apart: 8 -> 8, of which waited for: 6 -> 6; matrix products, arithmetic and copies ran while one was open for 16% -> 17% of each run, Pallas kernels for 3% -> 4%
where the time goes in v10:
time: 195 us; the launch traced here: 193 us
  waiting for transfers between devices  64.5 us (33%)
  starting transfers between devices  37.2 us (19%)
  blocking collectives  25 us (13%)
  matrix products  19.1 us (10%)
  between operations  13.9 us (7%)
  other arithmetic  13.6 us (7%)
  local copies, waits for them, and re-layouts  11 us (6%)
  Pallas kernels  8.44 us (4%)
    all_to_all x1, waiting for transfers between devices, shards(): lax.all_to_all(back, ('x', 'zl'), split_axis=0, concat_axis=0, tiled=True)  24.4 us
    dot_general x11, matrix products, dot(): return jnp.einsum(eq, a, b, preferred_element_type=F32)  19.1 us
    all_to_all x2, waiting for transfers between devices, spread(): got = lax.all_to_all(copies, axes, split_axis=0, concat_axis=0, tiled=True)  16.8 us
    all_gather x1, blocking collectives, shards(): tok_half = lax.all_gather(tok_rows, 'x', axis=0, tiled=True)  12.8 us
    all_to_all x2, starting transfers between devices, spread(): got = lax.all_to_all(copies, axes, split_axis=0, concat_axis=0, tiled=True)  12.3 us
    all_gather x1, blocking collectives, shards(): cot_high = lax.all_gather(cot_half[:, SPLIT:], 'x', axis=0, tiled=True)  12.1 us
    all_to_all x1, waiting for transfers between devices, shards(): lax.all_to_all(home.reshape(2 * EXPERTS, PAD, wide), ('ex', 'yl'), split_...  11.7 us
    all_to_all x1, starting transfers between devices, shards(): rows = lax.all_to_all(rows, 'ex', split_axis=0, concat_axis=0, tiled=True)  10.8 us
  transfers between devices with their start and end apart: 8, of which 6 were waited for; matrix products, arithmetic and copies ran while one was open for 17% of the time, Pallas kernels for 4%

profile of v10, /device:TPU:1, one launch (start us, length us, event | category | flops | bytes accessed | tf_op | source)
XLA Modules:
  0.0 192.7 jit_solution(12366950325429938660)
XLA Ops:
  7.2 1.9 pad_maximum_fusion
  10.8 0.8 fusion.64
  11.9 1.5 convolution_convert_fusion.3
  13.5 0.8 maximum_bitcast_fusion
  14.3 10.8 %all-to-all-start = ((bf16[4,8,7296]{2,1,0:T(8,128)(2,1)}), bf16[4,8,7296]{2,1,0:T(8,128)(2,1)S(1)}, u32[]{:S(2)}, u32[]{:S(2)}) async-start(bf16[4,8,7296]{2,1,0:T(8,128)(2,1)} %maximum_bitcast_fusion), calls=%async_computation | async-start | bytes 933888 | tf_op jit(solution)/shard_map/all_to_all | solution.py:100
  25.2 10.8 %all-to-all-done = bf16[4,8,7296]{2,1,0:T(8,128)(2,1)S(1)} async-done(((bf16[4,8,7296]{2,1,0:T(8,128)(2,1)}), bf16[4,8,7296]{2,1,0:T(8,128)(2,1)S(1)}, u32[]{:S(2)}, u32[]{:S(2)}) %all-to-all-start) | async-done | bytes 466976 | tf_op jit(solution)/shard_map/all_to_all | solution.py:100
  36.2 0.9 broadcast_in_dim.58
  37.1 7.7 %all-to-all-start.1 = ((bf16[4,24,3584]{2,1,0:T(8,128)(2,1)}), bf16[4,24,3584]{2,1,0:T(8,128)(2,1)S(1)}, u32[]{:S(2)}, u32[]{:S(2)}) async-start(bf16[4,24,3584]{2,1,0:T(8,128)(2,1)} %broadcast_in_dim.58), calls=%async_computation.1 | async-start | bytes 1376256 | tf_op jit(solution)/shard_map/all_to_all | solution.py:24
  45.1 12.8 %all_gather.13 = bf16[96,3712]{1,0:T(8,128)(2,1)S(1)} all-gather(bf16[24,3712]{1,0:T(8,128)(2,1)S(1)} %convolution_convert_fusion.4), channel_id=1, replica_groups=mesh['yh'=4,'core'=2,'ex'=4,'zl'=2,'x'=4,'yl'=2] {'x'}, dimensions={0}, use_global_device_ids=true | all-gather | bytes 890880 | tf_op jit(solution)/shard_map/all_gather | solution.py:111
  57.9 5.4 %all-to-all-done.1 = bf16[4,24,3584]{2,1,0:T(8,128)(2,1)S(1)} async-done(((bf16[4,24,3584]{2,1,0:T(8,128)(2,1)}), bf16[4,24,3584]{2,1,0:T(8,128)(2,1)S(1)}, u32[]{:S(2)}, u32[]{:S(2)}) %all-to-all-start.1) | async-done | bytes 688160 | tf_op jit(solution)/shard_map/all_to_all | solution.py:24
  63.2 1.8 broadcast_in_dim.63
  65.1 4.6 %all-to-all-start.2 = ((bf16[4,96,3712]{2,1,0:T(8,128)(2,1)}), bf16[4,96,3712]{2,1,0:T(8,128)(2,1)}, u32[]{:S(2)}, u32[]{:S(2)}) async-start(bf16[4,96,3712]{2,1,0:T(8,128)(2,1)} %broadcast_in_dim.63), calls=%async_computation.2 | async-start | bytes 5701632 | tf_op jit(solution)/shard_map/all_to_all | solution.py:24
  69.8 0.8 slice.59
  70.7 1.9 fusion.63
  72.7 5.7 %fusion.8 = bf16[384,3712]{1,0:T(8,128)(2,1)} fusion(bf16[128,3584]{1,0:T(8,128)(2,1)S(1)} %bitcast.89, bf16[128,3584]{1,0:T(8,128)(2,1)S(1)} %bitcast.91, bf16[128,3712]{1,0:T(8,128)(2,1)S(1)} %pad_convert_fusion), kind=kLoop, calls=%fused_computation.18 | loop fusion | flops 17104896 | bytes 5636096 | tf_op jit(solution)/shard_map/concatenate | solution.py:126
  78.3 12.1 %all_gather.15.high_ref = bf16[384,1024]{1,0:T(8,128)(2,1)S(1)} all-gather(bf16[96,1024]{1,0:T(8,128)(2,1)S(1)} %slice.61), channel_id=1, replica_groups=mesh['yh'=4,'core'=2,'ex'=4,'zl'=2,'x'=4,'yl'=2] {'x'}, dimensions={0}, use_global_device_ids=true | all-gather | bytes 983040 | tf_op jit(solution)/shard_map/all_gather | solution.py:116
  90.5 1.1 fusion.23
  91.5 11.4 %all-to-all-done.2 = bf16[4,96,3712]{2,1,0:T(8,128)(2,1)} async-done(((bf16[4,96,3712]{2,1,0:T(8,128)(2,1)}), bf16[4,96,3712]{2,1,0:T(8,128)(2,1)}, u32[]{:S(2)}, u32[]{:S(2)}) %all-to-all-start.2) | async-done | bytes 2850848 | tf_op jit(solution)/shard_map/all_to_all | solution.py:24
  102.9 4.4 %fusion.11 = f32[4,4,24,384]{3,2,0,1:T(8,128)S(1)} fusion(bf16[4,4,24,3712]{3,2,1,0:T(8,128)(2,1)} %bitcast.24, bf16[384,3712]{1,0:T(8,128)(2,1)} %fusion.8), kind=kOutput, calls=%fused_computation.22 | convolution fusion | flops 1094713344 | bytes 6291456 | tf_op jit(solution)/shard_map/rd,hd->rh/dot_general | solution.py:70
  107.4 0.9 copy.38
  108.3 3.4 %multiply_convert_fusion.2 = (bf16[384,128]{1,0:T(8,128)(2,1)S(1)}, bf16[384,128]{1,0:T(8,128)(2,1)S(1)}, bf16[384,128]{1,0:T(8,128)(2,1)}, bf16[384,128]{1,0:T(8,128)(2,1)S(1)}, f32[384,128]{1,0:T(8,128)S(1)}) fusion(f32[384,384]{1,0:T(8,128)} %bitcast.105, f32[384,128]{1,0:T(8,128)} %fusion.23, ...), kind=kOutput, calls=%fused_computation.47 | convolution fusion | flops 252641280 | bytes 3997696 | tf_op jit(solution)/shard_map/rd,hd->rh/dot_general | solution.py:70
  111.9 3.2 %convolution_convert_fusion = bf16[384,3712]{1,0:T(8,128)(2,1)} fusion(bf16[384,3712]{1,0:T(8,128)(2,1)S(1)} %copy-done.1, bf16[384,128]{1,0:T(8,128)(2,1)S(1)} %broadcast_in_dim.64, bf16[384,128]{1,0:T(8,128)(2,1)S(1)} %get-tuple-element.48, bf16[384,128]{1,0:T(8,128)(2,1)S(1)} %get-tuple-element.47), kind=kOutput, calls=%fused_computation.8 | convolution fusion | flops 1097023488 | bytes 5996544 | tf_op jit(solution)/shard_map/rh,hd->rd/dot_general | solution.py:70
  115.2 4.4 %all-to-all-start.3 = ((bf16[8,48,3712]{2,1,0:T(8,128)(2,1)}), bf16[8,48,3712]{2,1,0:T(8,128)(2,1)}, u32[]{:S(2)}, u32[]{:S(2)}) async-start(bf16[8,48,3712]{2,1,0:T(8,128)(2,1)} %bitcast.88), calls=%async_computation.3 | async-start | bytes 5701632 | tf_op jit(solution)/shard_map/all_to_all | solution.py:159
  120.4 8.4 %weight_grads.1 = bf16[3584,384]{1,0:T(8,128)(2,1)} custom-call(bf16[384,3712]{1,0:T(8,128)(2,1)} %bitcast.34.x_ref, bf16[384,2560]{1,0:T(8,128)(2,1)} %all-gather.5.cloned.1.call-done.low_ref, bf16[384,1024]{1,0:T(8,128)(2,1)} %copy-done.2, bf16[384,256]{1,0:T(8,128)(2,1)} %bitcast.104, bf16[384,128]{1,0:T(8,128)(2,1)} %get-tuple-element.49.h_ref), custom_call_target="tpu_custom_call" | custom-call | flops 1056964608 | bytes 8257536 | tf_op jit(solution)/shard_map/weight_grads/pallas_call | solution.py:47
  128.9 24.4 %all-to-all-done.3 = bf16[8,48,3712]{2,1,0:T(8,128)(2,1)} async-done(((bf16[8,48,3712]{2,1,0:T(8,128)(2,1)}), bf16[8,48,3712]{2,1,0:T(8,128)(2,1)}, u32[]{:S(2)}, u32[]{:S(2)}) %all-to-all-start.3) | async-done | bytes 2850848 | tf_op jit(solution)/shard_map/all_to_all | solution.py:159
  153.3 3.2 %fusion.6 = bf16[8,8,3712]{2,1,0:T(8,128)(2,1)} fusion(bf16[8,48,3712]{2,1,0:T(8,128)(2,1)} %all-to-all-done.3, bf16[64,48]{0,1:T(8,128)(2,1)S(1)} %fusion.31), kind=kOutput, calls=%fused_computation.12 | convolution fusion | flops 182689792 | bytes 3332096 | tf_op jit(solution)/shard_map/ck,kd->cd/dot_general | solution.py:70
  156.5 9.6 %all-to-all-start.4 = ((bf16[8,8,3712]{2,1,0:T(8,128)(2,1)}), bf16[8,8,3712]{2,1,0:T(8,128)(2,1)S(1)}, u32[]{:S(2)}, u32[]{:S(2)}) async-start(bf16[8,8,3712]{2,1,0:T(8,128)(2,1)} %fusion.6), calls=%async_computation.4 | async-start | bytes 950272 | tf_op jit(solution)/shard_map/all_to_all | solution.py:165
  166.2 0.8 copy.42
  167.0 1.1 dynamic-slice_bitcast_fusion
  169.6 11.7 %all-to-all-done.4 = bf16[8,8,3712]{2,1,0:T(8,128)(2,1)S(1)} async-done(((bf16[8,8,3712]{2,1,0:T(8,128)(2,1)}), bf16[8,8,3712]{2,1,0:T(8,128)(2,1)S(1)}, u32[]{:S(2)}, u32[]{:S(2)}) %all-to-all-start.4) | async-done | bytes 475168 | tf_op jit(solution)/shard_map/all_to_all | solution.py:165
  182.2 1.4 convolution_convert_fusion.1
  184.3 1.9 bitcast_convert_fusion
  (48 shorter events, 7.2 us)
Async XLA Ops:
  7.2 4.5 %copy-start = (bf16[128,3584]{1,0:T(8,128)(2,1)S(1)}, bf16[128,3584]{1,0:T(8,128)(2,1)}, u32[]{:S(2)}) copy-start(bf16[128,3584]{1,0:T(8,128)(2,1)} %param.8) | copy-start | bytes 2752516
  7.2 62.6 %all-gather.3.cloned.1.call-start = ((), (), s32[]{:S(2)}) async-start(), calls=%async_computation.6 | async-start | bytes 3096576 | tf_op jit(solution)/shard_map/all_gather | solution.py:78
  14.3 21.7 %all-to-all-start = ((bf16[4,8,7296]{2,1,0:T(8,128)(2,1)}), bf16[4,8,7296]{2,1,0:T(8,128)(2,1)S(1)}, u32[]{:S(2)}, u32[]{:S(2)}) async-start(bf16[4,8,7296]{2,1,0:T(8,128)(2,1)} %maximum_bitcast_fusion), calls=%async_computation | async-start | bytes 933888 | tf_op jit(solution)/shard_map/all_to_all | solution.py:100
  37.1 26.1 %all-to-all-start.1 = ((bf16[4,24,3584]{2,1,0:T(8,128)(2,1)}), bf16[4,24,3584]{2,1,0:T(8,128)(2,1)S(1)}, u32[]{:S(2)}, u32[]{:S(2)}) async-start(bf16[4,24,3584]{2,1,0:T(8,128)(2,1)} %broadcast_in_dim.58), calls=%async_computation.1 | async-start | bytes 1376256 | tf_op jit(solution)/shard_map/all_to_all | solution.py:24
  65.1 37.9 %all-to-all-start.2 = ((bf16[4,96,3712]{2,1,0:T(8,128)(2,1)}), bf16[4,96,3712]{2,1,0:T(8,128)(2,1)}, u32[]{:S(2)}, u32[]{:S(2)}) async-start(bf16[4,96,3712]{2,1,0:T(8,128)(2,1)} %broadcast_in_dim.63), calls=%async_computation.2 | async-start | bytes 5701632 | tf_op jit(solution)/shard_map/all_to_all | solution.py:24
  69.7 38.6 %all-gather.5.cloned.1.call-start = ((), (), s32[]{:S(2)}) async-start(), calls=%async_computation.7 | async-start | bytes 2457600 | tf_op jit(solution)/shard_map/all_gather | solution.py:115
  72.6 17.8 %copy-start.3 = (bf16[8,1,16,3584]{3,2,1,0:T(8,128)(2,1)}, bf16[8,1,16,3584]{3,2,1,0:T(8,128)(2,1)S(1)}, u32[]{:S(2)}) copy-start(bf16[8,1,16,3584]{3,2,1,0:T(8,128)(2,1)S(1)} %get-tuple-element.44) | copy-start | bytes 2752516
  90.4 16.9 %copy-start.2 = (bf16[384,1024]{1,0:T(8,128)(2,1)}, bf16[384,1024]{1,0:T(8,128)(2,1)S(1)}, u32[]{:S(2)}) copy-start(bf16[384,1024]{1,0:T(8,128)(2,1)S(1)} %all_gather.15.high_ref) | copy-start | bytes 2359300
  108.3 3.6 %copy-start.1 = (bf16[384,3712]{1,0:T(8,128)(2,1)S(1)}, bf16[384,3712]{1,0:T(8,128)(2,1)}, u32[]{:S(2)}) copy-start(bf16[384,3712]{1,0:T(8,128)(2,1)} %fusion.8) | copy-start | bytes 8552452
  115.2 38.1 %all-to-all-start.3 = ((bf16[8,48,3712]{2,1,0:T(8,128)(2,1)}), bf16[8,48,3712]{2,1,0:T(8,128)(2,1)}, u32[]{:S(2)}, u32[]{:S(2)}) async-start(bf16[8,48,3712]{2,1,0:T(8,128)(2,1)} %bitcast.88), calls=%async_computation.3 | async-start | bytes 5701632 | tf_op jit(solution)/shard_map/all_to_all | solution.py:159
  119.6 64.7 %reduce-scatter.2.cloned.1.call-start = ((), (), s32[]{:S(2)}) async-start(), calls=%async_computation.8 | async-start | bytes 3096576 | tf_op jit(solution)/shard_map/reduce_scatter | solution.py:156
  128.9 52.6 %copy-start.4 = (s32[128,8]{0,1:T(8,128)S(1)}, s32[128,8]{0,1:T(8,128)}, u32[]{:S(2)}) copy-start(s32[128,8]{0,1:T(8,128)} %param.9) | copy-start | bytes 12292
  156.5 24.8 %all-to-all-start.4 = ((bf16[8,8,3712]{2,1,0:T(8,128)(2,1)}), bf16[8,8,3712]{2,1,0:T(8,128)(2,1)S(1)}, u32[]{:S(2)}, u32[]{:S(2)}) async-start(bf16[8,8,3712]{2,1,0:T(8,128)(2,1)} %fusion.6), calls=%async_computation.4 | async-start | bytes 950272 | tf_op jit(solution)/shard_map/all_to_all | solution.py:165
Sparse Core Ops, SparseCore 0:
  10.1 54.1 all-gather.2
  72.6 35.6 all-gather.4
  129.0 55.3 reduce-scatter.1

commit v11 on v10

--- a/solution.py
+++ b/solution.py
@@ -56,7 +56,7 @@
         ],
         out_specs=pl.BlockSpec((CHUNK, 3 * LANES), lambda j: (j, 0)),
         out_shape=jax.ShapeDtypeStruct((features, 3 * LANES), BF),
-        compiler_params=pltpu.CompilerParams(vmem_limit_bytes=58 << 20),
+        compiler_params=pltpu.CompilerParams(vmem_limit_bytes=52 << 20),
         cost_estimate=pl.CostEstimate(
             flops=2 * rows * features * 3 * LANES,
             bytes_accessed=2 * features * (2 * rows + 3 * LANES),

time: 195 us -> 193 us (0.990)
  no operation moved by 1% of the time
where the time goes in v11:
time: 193 us; the launch traced here: 192 us
  waiting for transfers between devices  66.2 us (34%)
  starting transfers between devices  36.5 us (19%)
  blocking collectives  25 us (13%)
  matrix products  18.3 us (9%)
  between operations  14 us (7%)
  other arithmetic  13.6 us (7%)
  local copies, waits for them, and re-layouts  10.4 us (5%)
  Pallas kernels  8.16 us (4%)
    all_to_all x1, waiting for transfers between devices, shards(): lax.all_to_all(back, ('x', 'zl'), split_axis=0, concat_axis=0, tiled=True)  26.1 us
    dot_general x11, matrix products, dot(): return jnp.einsum(eq, a, b, preferred_element_type=F32)  18.3 us
    all_to_all x2, waiting for transfers between devices, spread(): got = lax.all_to_all(copies, axes, split_axis=0, concat_axis=0, tiled=True)  16.8 us
    all_gather x1, blocking collectives, shards(): tok_half = lax.all_gather(tok_rows, 'x', axis=0, tiled=True)  12.8 us
    all_to_all x2, starting transfers between devices, spread(): got = lax.all_to_all(copies, axes, split_axis=0, concat_axis=0, tiled=True)  12.3 us
    all_gather x1, blocking collectives, shards(): cot_high = lax.all_gather(cot_half[:, SPLIT:], 'x', axis=0, tiled=True)  12.1 us
    all_to_all x1, waiting for transfers between devices, shards(): lax.all_to_all(home.reshape(2 * EXPERTS, PAD, wide), ('ex', 'yl'), split_...  11.6 us
    all_to_all x1, starting transfers between devices, shards(): rows = lax.all_to_all(rows, 'ex', split_axis=0, concat_axis=0, tiled=True)  10.8 us
  transfers between devices with their start and end apart: 8, of which 6 were waited for; matrix products, arithmetic and copies ran while one was open for 17% of the time, Pallas kernels for 4%

profile of v11, /device:TPU:1, one launch (start us, length us, event | category | flops | bytes accessed | tf_op | source)
XLA Modules:
  0.0 192.0 jit_solution(1335068473474463102)
XLA Ops:
  7.2 1.9 pad_maximum_fusion
  10.8 0.8 fusion.64
  11.9 1.5 convolution_convert_fusion.3
  13.5 0.8 maximum_bitcast_fusion
  14.3 10.8 %all-to-all-start = ((bf16[4,8,7296]{2,1,0:T(8,128)(2,1)}), bf16[4,8,7296]{2,1,0:T(8,128)(2,1)S(1)}, u32[]{:S(2)}, u32[]{:S(2)}) async-start(bf16[4,8,7296]{2,1,0:T(8,128)(2,1)} %maximum_bitcast_fusion), calls=%async_computation | async-start | bytes 933888 | tf_op jit(solution)/shard_map/all_to_all | solution.py:100
  25.2 10.8 %all-to-all-done = bf16[4,8,7296]{2,1,0:T(8,128)(2,1)S(1)} async-done(((bf16[4,8,7296]{2,1,0:T(8,128)(2,1)}), bf16[4,8,7296]{2,1,0:T(8,128)(2,1)S(1)}, u32[]{:S(2)}, u32[]{:S(2)}) %all-to-all-start) | async-done | bytes 466976 | tf_op jit(solution)/shard_map/all_to_all | solution.py:100
  36.2 0.9 broadcast_in_dim.58
  37.1 7.7 %all-to-all-start.1 = ((bf16[4,24,3584]{2,1,0:T(8,128)(2,1)}), bf16[4,24,3584]{2,1,0:T(8,128)(2,1)S(1)}, u32[]{:S(2)}, u32[]{:S(2)}) async-start(bf16[4,24,3584]{2,1,0:T(8,128)(2,1)} %broadcast_in_dim.58), calls=%async_computation.1 | async-start | bytes 1376256 | tf_op jit(solution)/shard_map/all_to_all | solution.py:24
  45.1 12.8 %all_gather.13 = bf16[96,3712]{1,0:T(8,128)(2,1)S(1)} all-gather(bf16[24,3712]{1,0:T(8,128)(2,1)S(1)} %convolution_convert_fusion.4), channel_id=1, replica_groups=mesh['yh'=4,'core'=2,'ex'=4,'zl'=2,'x'=4,'yl'=2] {'x'}, dimensions={0}, use_global_device_ids=true | all-gather | bytes 890880 | tf_op jit(solution)/shard_map/all_gather | solution.py:111
  57.9 5.4 %all-to-all-done.1 = bf16[4,24,3584]{2,1,0:T(8,128)(2,1)S(1)} async-done(((bf16[4,24,3584]{2,1,0:T(8,128)(2,1)}), bf16[4,24,3584]{2,1,0:T(8,128)(2,1)S(1)}, u32[]{:S(2)}, u32[]{:S(2)}) %all-to-all-start.1) | async-done | bytes 688160 | tf_op jit(solution)/shard_map/all_to_all | solution.py:24
  63.2 1.8 broadcast_in_dim.63
  65.1 4.6 %all-to-all-start.2 = ((bf16[4,96,3712]{2,1,0:T(8,128)(2,1)}), bf16[4,96,3712]{2,1,0:T(8,128)(2,1)}, u32[]{:S(2)}, u32[]{:S(2)}) async-start(bf16[4,96,3712]{2,1,0:T(8,128)(2,1)} %broadcast_in_dim.63), calls=%async_computation.2 | async-start | bytes 5701632 | tf_op jit(solution)/shard_map/all_to_all | solution.py:24
  69.8 0.8 slice.59
  70.7 1.9 fusion.63
  72.7 5.7 %fusion.8 = bf16[384,3712]{1,0:T(8,128)(2,1)} fusion(bf16[128,3584]{1,0:T(8,128)(2,1)S(1)} %bitcast.90, bf16[128,3584]{1,0:T(8,128)(2,1)S(1)} %bitcast.92, bf16[128,3712]{1,0:T(8,128)(2,1)S(1)} %pad_convert_fusion), kind=kLoop, calls=%fused_computation.18 | loop fusion | flops 17104896 | bytes 5636096 | tf_op jit(solution)/shard_map/concatenate | solution.py:126
  78.3 12.1 %all_gather.15.high_ref = bf16[384,1024]{1,0:T(8,128)(2,1)S(1)} all-gather(bf16[96,1024]{1,0:T(8,128)(2,1)S(1)} %slice.61), channel_id=1, replica_groups=mesh['yh'=4,'core'=2,'ex'=4,'zl'=2,'x'=4,'yl'=2] {'x'}, dimensions={0}, use_global_device_ids=true | all-gather | bytes 983040 | tf_op jit(solution)/shard_map/all_gather | solution.py:116
  90.5 1.1 fusion.23
  91.5 11.4 %all-to-all-done.2 = bf16[4,96,3712]{2,1,0:T(8,128)(2,1)} async-done(((bf16[4,96,3712]{2,1,0:T(8,128)(2,1)}), bf16[4,96,3712]{2,1,0:T(8,128)(2,1)}, u32[]{:S(2)}, u32[]{:S(2)}) %all-to-all-start.2) | async-done | bytes 2850848 | tf_op jit(solution)/shard_map/all_to_all | solution.py:24
  102.9 4.4 %fusion.11 = f32[4,4,24,384]{3,2,0,1:T(8,128)S(1)} fusion(bf16[4,4,24,3712]{3,2,1,0:T(8,128)(2,1)} %bitcast.24, bf16[384,3712]{1,0:T(8,128)(2,1)} %fusion.8), kind=kOutput, calls=%fused_computation.22 | convolution fusion | flops 1094713344 | bytes 6291456 | tf_op jit(solution)/shard_map/rd,hd->rh/dot_general | solution.py:70
  107.4 0.9 all-gather.5.cloned.1.call-done.low_ref
  108.3 2.6 %multiply_convert_fusion.2 = (bf16[384,128]{1,0:T(8,128)(2,1)S(1)}, bf16[384,128]{1,0:T(8,128)(2,1)S(1)}, bf16[384,128]{1,0:T(8,128)(2,1)S(1)}, bf16[384,128]{1,0:T(8,128)(2,1)S(1)}, f32[384,128]{1,0:T(8,128)S(1)}) fusion(f32[384,384]{1,0:T(8,128)S(1)} %bitcast.105, f32[384,128]{1,0:T(8,128)} %fusion.23, ...), kind=kOutput, calls=%fused_computation.47 | convolution fusion | flops 252641280 | bytes 3997696 | tf_op jit(solution)/shard_map/rd,hd->rh/dot_general | solution.py:70
  111.2 3.2 %convolution_convert_fusion = bf16[384,3712]{1,0:T(8,128)(2,1)} fusion(bf16[384,3712]{1,0:T(8,128)(2,1)S(1)} %copy-done.1, bf16[384,128]{1,0:T(8,128)(2,1)S(1)} %broadcast_in_dim.64, bf16[384,128]{1,0:T(8,128)(2,1)S(1)} %get-tuple-element.48, bf16[384,128]{1,0:T(8,128)(2,1)S(1)} %get-tuple-element.47), kind=kOutput, calls=%fused_computation.8 | convolution fusion | flops 1097023488 | bytes 5996544 | tf_op jit(solution)/shard_map/rh,hd->rd/dot_general | solution.py:70
  114.4 4.4 %all-to-all-start.3 = ((bf16[8,48,3712]{2,1,0:T(8,128)(2,1)}), bf16[8,48,3712]{2,1,0:T(8,128)(2,1)}, u32[]{:S(2)}, u32[]{:S(2)}) async-start(bf16[8,48,3712]{2,1,0:T(8,128)(2,1)} %bitcast.89), calls=%async_computation.3 | async-start | bytes 5701632 | tf_op jit(solution)/shard_map/all_to_all | solution.py:159
  118.9 8.2 %weight_grads.1 = bf16[3584,384]{1,0:T(8,128)(2,1)} custom-call(bf16[384,3712]{1,0:T(8,128)(2,1)} %bitcast.34.x_ref, bf16[384,2560]{1,0:T(8,128)(2,1)} %all-gather.5.cloned.1.call-done.low_ref, bf16[384,1024]{1,0:T(8,128)(2,1)S(1)} %all_gather.15.high_ref, bf16[384,256]{1,0:T(8,128)(2,1)S(1)} %bitcast.88, bf16[384,128]{1,0:T(8,128)(2,1)S(1)} %get-tuple-element.49.h_ref), custom_call_target="tpu_custom_call" | custom-call | flops 1056964608 | bytes 8257536 | tf_op jit(solution)/shard_map/weight_grads/pallas_call | solution.py:47
  127.2 26.1 %all-to-all-done.3 = bf16[8,48,3712]{2,1,0:T(8,128)(2,1)} async-done(((bf16[8,48,3712]{2,1,0:T(8,128)(2,1)}), bf16[8,48,3712]{2,1,0:T(8,128)(2,1)}, u32[]{:S(2)}, u32[]{:S(2)}) %all-to-all-start.3) | async-done | bytes 2850848 | tf_op jit(solution)/shard_map/all_to_all | solution.py:159
  153.3 3.2 %fusion.6 = bf16[8,8,3712]{2,1,0:T(8,128)(2,1)} fusion(bf16[8,48,3712]{2,1,0:T(8,128)(2,1)} %all-to-all-done.3, bf16[64,48]{0,1:T(8,128)(2,1)S(1)} %fusion.31), kind=kOutput, calls=%fused_computation.12 | convolution fusion | flops 182689792 | bytes 3332096 | tf_op jit(solution)/shard_map/ck,kd->cd/dot_general | solution.py:70
  156.5 8.8 %all-to-all-start.4 = ((bf16[8,8,3712]{2,1,0:T(8,128)(2,1)}), bf16[8,8,3712]{2,1,0:T(8,128)(2,1)S(1)}, u32[]{:S(2)}, u32[]{:S(2)}) async-start(bf16[8,8,3712]{2,1,0:T(8,128)(2,1)} %fusion.6), calls=%async_computation.4 | async-start | bytes 950272 | tf_op jit(solution)/shard_map/all_to_all | solution.py:165
  165.4 1.0 dynamic-slice_bitcast_fusion.2
  167.2 1.1 dynamic-slice_bitcast_fusion
  169.8 11.6 %all-to-all-done.4 = bf16[8,8,3712]{2,1,0:T(8,128)(2,1)S(1)} async-done(((bf16[8,8,3712]{2,1,0:T(8,128)(2,1)}), bf16[8,8,3712]{2,1,0:T(8,128)(2,1)S(1)}, u32[]{:S(2)}, u32[]{:S(2)}) %all-to-all-start.4) | async-done | bytes 475168 | tf_op jit(solution)/shard_map/all_to_all | solution.py:165
  182.3 1.4 convolution_convert_fusion.1
  183.6 1.9 bitcast_convert_fusion
  (48 shorter events, 6.5 us)
Async XLA Ops:
  7.2 4.5 %copy-start = (bf16[128,3584]{1,0:T(8,128)(2,1)S(1)}, bf16[128,3584]{1,0:T(8,128)(2,1)}, u32[]{:S(2)}) copy-start(bf16[128,3584]{1,0:T(8,128)(2,1)} %param.8) | copy-start | bytes 2752516
  7.2 62.6 %all-gather.3.cloned.1.call-start = ((), (), s32[]{:S(2)}) async-start(), calls=%async_computation.6 | async-start | bytes 3096576 | tf_op jit(solution)/shard_map/all_gather | solution.py:78
  14.3 21.7 %all-to-all-start = ((bf16[4,8,7296]{2,1,0:T(8,128)(2,1)}), bf16[4,8,7296]{2,1,0:T(8,128)(2,1)S(1)}, u32[]{:S(2)}, u32[]{:S(2)}) async-start(bf16[4,8,7296]{2,1,0:T(8,128)(2,1)} %maximum_bitcast_fusion), calls=%async_computation | async-start | bytes 933888 | tf_op jit(solution)/shard_map/all_to_all | solution.py:100
  37.1 26.1 %all-to-all-start.1 = ((bf16[4,24,3584]{2,1,0:T(8,128)(2,1)}), bf16[4,24,3584]{2,1,0:T(8,128)(2,1)S(1)}, u32[]{:S(2)}, u32[]{:S(2)}) async-start(bf16[4,24,3584]{2,1,0:T(8,128)(2,1)} %broadcast_in_dim.58), calls=%async_computation.1 | async-start | bytes 1376256 | tf_op jit(solution)/shard_map/all_to_all | solution.py:24
  65.1 37.9 %all-to-all-start.2 = ((bf16[4,96,3712]{2,1,0:T(8,128)(2,1)}), bf16[4,96,3712]{2,1,0:T(8,128)(2,1)}, u32[]{:S(2)}, u32[]{:S(2)}) async-start(bf16[4,96,3712]{2,1,0:T(8,128)(2,1)} %broadcast_in_dim.63), calls=%async_computation.2 | async-start | bytes 5701632 | tf_op jit(solution)/shard_map/all_to_all | solution.py:24
  69.7 38.6 %all-gather.5.cloned.1.call-start = ((), (), s32[]{:S(2)}) async-start(), calls=%async_computation.7 | async-start | bytes 2457600 | tf_op jit(solution)/shard_map/all_gather | solution.py:115
  72.6 17.8 %copy-start.2 = (bf16[8,1,16,3584]{3,2,1,0:T(8,128)(2,1)}, bf16[8,1,16,3584]{3,2,1,0:T(8,128)(2,1)S(1)}, u32[]{:S(2)}) copy-start(bf16[8,1,16,3584]{3,2,1,0:T(8,128)(2,1)S(1)} %get-tuple-element.46) | copy-start | bytes 2752516
  72.7 17.8 %copy-start.3 = (bf16[8,1,16,3584]{3,2,1,0:T(8,128)(2,1)}, bf16[8,1,16,3584]{3,2,1,0:T(8,128)(2,1)S(1)}, u32[]{:S(2)}) copy-start(bf16[8,1,16,3584]{3,2,1,0:T(8,128)(2,1)S(1)} %get-tuple-element.44) | copy-start | bytes 2752516
  108.3 2.9 %copy-start.1 = (bf16[384,3712]{1,0:T(8,128)(2,1)S(1)}, bf16[384,3712]{1,0:T(8,128)(2,1)}, u32[]{:S(2)}) copy-start(bf16[384,3712]{1,0:T(8,128)(2,1)} %fusion.8) | copy-start | bytes 8552452
  114.4 38.9 %all-to-all-start.3 = ((bf16[8,48,3712]{2,1,0:T(8,128)(2,1)}), bf16[8,48,3712]{2,1,0:T(8,128)(2,1)}, u32[]{:S(2)}, u32[]{:S(2)}) async-start(bf16[8,48,3712]{2,1,0:T(8,128)(2,1)} %bitcast.89), calls=%async_computation.3 | async-start | bytes 5701632 | tf_op jit(solution)/shard_map/all_to_all | solution.py:159
  118.8 64.8 %reduce-scatter.2.cloned.1.call-start = ((), (), s32[]{:S(2)}) async-start(), calls=%async_computation.8 | async-start | bytes 3096576 | tf_op jit(solution)/shard_map/reduce_scatter | solution.py:156
  127.2 54.4 %copy-start.4 = (s32[128,8]{0,1:T(8,128)S(1)}, s32[128,8]{0,1:T(8,128)}, u32[]{:S(2)}) copy-start(s32[128,8]{0,1:T(8,128)} %param.9) | copy-start | bytes 12292
  156.5 24.8 %all-to-all-start.4 = ((bf16[8,8,3712]{2,1,0:T(8,128)(2,1)}), bf16[8,8,3712]{2,1,0:T(8,128)(2,1)S(1)}, u32[]{:S(2)}, u32[]{:S(2)}) async-start(bf16[8,8,3712]{2,1,0:T(8,128)(2,1)} %fusion.6), calls=%async_computation.4 | async-start | bytes 950272 | tf_op jit(solution)/shard_map/all_to_all | solution.py:165
Sparse Core Ops, SparseCore 0:
  10.1 54.1 all-gather.2
  72.6 35.6 all-gather.4
  127.2 56.0 reduce-scatter.1

commit v12 on v11

--- a/solution.py
+++ b/solution.py
@@ -132,10 +132,10 @@
         axis=0,
     )
     wide_slab = lax.optimization_barrier(wide_slab)
-    both = reorder(dot("rd,hd->rh", slot_all, wide_slab))
+    both = reorder(dot("rd,hd->rh", slot_all, wide_slab[: 2 * LANES]))
     pre_gate = both[:, :LANES]
-    pre_up = both[:, LANES : 2 * LANES]
-    slot_gates = both[:, 2 * LANES :]
+    pre_up = both[:, LANES:]
+    slot_gates = reorder(slot_all[:, features:]).astype(F32)
     sigmoid_gate = jax.nn.sigmoid(pre_gate)
     activation = pre_gate * sigmoid_gate
     hidden = (activation * pre_up).astype(BF)

time: 193 us -> 195 us (1.010)
  no operation moved by 1% of the time
where the time goes in v12:
time: 195 us; the launch traced here: 194 us
  waiting for transfers between devices  67.7 us (35%)
  starting transfers between devices  36.9 us (19%)
  blocking collectives  25 us (13%)
  matrix products  16.6 us (9%)
  between operations  14 us (7%)
  other arithmetic  13.6 us (7%)
  local copies, waits for them, and re-layouts  12 us (6%)
  Pallas kernels  8.16 us (4%)
    all_to_all x1, waiting for transfers between devices, shards(): lax.all_to_all(back, ('x', 'zl'), split_axis=0, concat_axis=0, tiled=True)  25.6 us
    all_to_all x2, waiting for transfers between devices, spread(): got = lax.all_to_all(copies, axes, split_axis=0, concat_axis=0, tiled=True)  17.5 us
    dot_general x11, matrix products, dot(): return jnp.einsum(eq, a, b, preferred_element_type=F32)  16.6 us
    all_to_all x1, waiting for transfers between devices, shards(): lax.all_to_all(home.reshape(2 * EXPERTS, PAD, wide), ('ex', 'yl'), split_...  13.4 us
    all_gather x1, blocking collectives, shards(): tok_half = lax.all_gather(tok_rows, 'x', axis=0, tiled=True)  12.8 us
    all_to_all x2, starting transfers between devices, spread(): got = lax.all_to_all(copies, axes, split_axis=0, concat_axis=0, tiled=True)  12.3 us
    all_gather x1, blocking collectives, shards(): cot_high = lax.all_gather(cot_half[:, SPLIT:], 'x', axis=0, tiled=True)  12.1 us
    all_to_all x1, starting transfers between devices, shards(): rows = lax.all_to_all(rows, 'ex', split_axis=0, concat_axis=0, tiled=True)  10.8 us
  transfers between devices with their start and end apart: 8, of which 6 were waited for; matrix products, arithmetic and copies ran while one was open for 17% of the time, Pallas kernels for 4%

profile of v12, /device:TPU:1, one launch (start us, length us, event | category | flops | bytes accessed | tf_op | source)
XLA Modules:
  0.0 193.8 jit_solution(1055499173973820012)
XLA Ops:
  7.2 1.9 pad_maximum_fusion
  10.8 0.8 fusion.61
  11.9 1.5 convolution_convert_fusion.3
  13.5 0.8 maximum_bitcast_fusion
  14.3 10.8 %all-to-all-start = ((bf16[4,8,7296]{2,1,0:T(8,128)(2,1)}), bf16[4,8,7296]{2,1,0:T(8,128)(2,1)S(1)}, u32[]{:S(2)}, u32[]{:S(2)}) async-start(bf16[4,8,7296]{2,1,0:T(8,128)(2,1)} %maximum_bitcast_fusion), calls=%async_computation | async-start | bytes 933888 | tf_op jit(solution)/shard_map/all_to_all | solution.py:100
  25.2 10.8 %all-to-all-done = bf16[4,8,7296]{2,1,0:T(8,128)(2,1)S(1)} async-done(((bf16[4,8,7296]{2,1,0:T(8,128)(2,1)}), bf16[4,8,7296]{2,1,0:T(8,128)(2,1)S(1)}, u32[]{:S(2)}, u32[]{:S(2)}) %all-to-all-start) | async-done | bytes 466976 | tf_op jit(solution)/shard_map/all_to_all | solution.py:100
  36.2 0.9 broadcast_in_dim.58
  37.1 7.7 %all-to-all-start.1 = ((bf16[4,24,3584]{2,1,0:T(8,128)(2,1)}), bf16[4,24,3584]{2,1,0:T(8,128)(2,1)S(1)}, u32[]{:S(2)}, u32[]{:S(2)}) async-start(bf16[4,24,3584]{2,1,0:T(8,128)(2,1)} %broadcast_in_dim.58), calls=%async_computation.1 | async-start | bytes 1376256 | tf_op jit(solution)/shard_map/all_to_all | solution.py:24
  45.1 12.8 %all_gather.13 = bf16[96,3712]{1,0:T(8,128)(2,1)S(1)} all-gather(bf16[24,3712]{1,0:T(8,128)(2,1)S(1)} %convolution_convert_fusion.4), channel_id=1, replica_groups=mesh['yh'=4,'core'=2,'ex'=4,'zl'=2,'x'=4,'yl'=2] {'x'}, dimensions={0}, use_global_device_ids=true | all-gather | bytes 890880 | tf_op jit(solution)/shard_map/all_gather | solution.py:111
  57.9 5.4 %all-to-all-done.1 = bf16[4,24,3584]{2,1,0:T(8,128)(2,1)S(1)} async-done(((bf16[4,24,3584]{2,1,0:T(8,128)(2,1)}), bf16[4,24,3584]{2,1,0:T(8,128)(2,1)S(1)}, u32[]{:S(2)}, u32[]{:S(2)}) %all-to-all-start.1) | async-done | bytes 688160 | tf_op jit(solution)/shard_map/all_to_all | solution.py:24
  63.2 1.8 broadcast_in_dim.63
  65.1 4.6 %all-to-all-start.2 = ((bf16[4,96,3712]{2,1,0:T(8,128)(2,1)}), bf16[4,96,3712]{2,1,0:T(8,128)(2,1)}, u32[]{:S(2)}, u32[]{:S(2)}) async-start(bf16[4,96,3712]{2,1,0:T(8,128)(2,1)} %broadcast_in_dim.63), calls=%async_computation.2 | async-start | bytes 5701632 | tf_op jit(solution)/shard_map/all_to_all | solution.py:24
  69.8 0.8 slice.62
  70.7 1.9 fusion.60
  72.7 5.7 %fusion.8 = bf16[384,3712]{1,0:T(8,128)(2,1)} fusion(bf16[128,3584]{1,0:T(8,128)(2,1)S(1)} %bitcast.101, bf16[128,3584]{1,0:T(8,128)(2,1)S(1)} %bitcast.103, bf16[128,3712]{1,0:T(8,128)(2,1)S(1)} %pad_convert_fusion), kind=kLoop, calls=%fused_computation.18 | loop fusion | flops 17104896 | bytes 5636096 | tf_op jit(solution)/shard_map/concatenate | solution.py:126
  78.3 12.1 %all_gather.15.high_ref = bf16[384,1024]{1,0:T(8,128)(2,1)S(1)} all-gather(bf16[96,1024]{1,0:T(8,128)(2,1)S(1)} %slice.64), channel_id=1, replica_groups=mesh['yh'=4,'core'=2,'ex'=4,'zl'=2,'x'=4,'yl'=2] {'x'}, dimensions={0}, use_global_device_ids=true | all-gather | bytes 983040 | tf_op jit(solution)/shard_map/all_gather | solution.py:116
  90.9 12.1 %all-to-all-done.2 = bf16[4,96,3712]{2,1,0:T(8,128)(2,1)} async-done(((bf16[4,96,3712]{2,1,0:T(8,128)(2,1)}), bf16[4,96,3712]{2,1,0:T(8,128)(2,1)}, u32[]{:S(2)}, u32[]{:S(2)}) %all-to-all-start.2) | async-done | bytes 2850848 | tf_op jit(solution)/shard_map/all_to_all | solution.py:24
  102.9 3.4 %fusion.10 = f32[4,4,24,256]{3,2,0,1:T(8,128)S(1)} fusion(bf16[4,4,24,3712]{3,2,1,0:T(8,128)(2,1)} %bitcast.28, bf16[384,3712]{1,0:T(8,128)(2,1)} %fusion.8), kind=kOutput, calls=%fused_computation.22 | convolution fusion | flops 729808896 | bytes 5144576 | tf_op jit(solution)/shard_map/rd,hd->rh/dot_general | solution.py:70
  106.4 0.9 slice.79
  108.3 2.6 %multiply_convert_fusion.2 = (bf16[384,128]{1,0:T(8,128)(2,1)S(1)}, bf16[384,128]{1,0:T(8,128)(2,1)S(1)}, bf16[384,128]{1,0:T(8,128)(2,1)S(1)}, bf16[384,128]{1,0:T(8,128)(2,1)S(1)}, f32[384,128]{1,0:T(8,128)S(1)}) fusion(f32[384,256]{1,0:T(8,128)S(1)} %bitcast.116, f32[4,4,24,128]{3,2,0,1:T(8,128)} %copy.42, f32[384,128]{1,0:T(8,128)S(1)} %fusion.20, ...), kind=kOutput, calls=%fused_computation.48 | convolution fusion | flops 252641280 | bytes 3997696 | tf_op jit(solution)/shard_map/rd,hd->rh/dot_general | solution.py:70
  111.2 3.2 %convolution_convert_fusion = bf16[384,3712]{1,0:T(8,128)(2,1)} fusion(bf16[384,3712]{1,0:T(8,128)(2,1)S(1)} %copy-done.1, bf16[384,128]{1,0:T(8,128)(2,1)S(1)} %broadcast_in_dim.64, bf16[384,128]{1,0:T(8,128)(2,1)S(1)} %get-tuple-element.56, bf16[384,128]{1,0:T(8,128)(2,1)S(1)} %get-tuple-element.55), kind=kOutput, calls=%fused_computation.8 | convolution fusion | flops 1097023488 | bytes 5996544 | tf_op jit(solution)/shard_map/rh,hd->rd/dot_general | solution.py:70
  114.4 4.4 %all-to-all-start.3 = ((bf16[8,48,3712]{2,1,0:T(8,128)(2,1)}), bf16[8,48,3712]{2,1,0:T(8,128)(2,1)}, u32[]{:S(2)}, u32[]{:S(2)}) async-start(bf16[8,48,3712]{2,1,0:T(8,128)(2,1)} %bitcast.100), calls=%async_computation.3 | async-start | bytes 5701632 | tf_op jit(solution)/shard_map/all_to_all | solution.py:159
  118.9 8.2 %weight_grads.1 = bf16[3584,384]{1,0:T(8,128)(2,1)} custom-call(bf16[384,3712]{1,0:T(8,128)(2,1)} %bitcast.24.x_ref, bf16[384,2560]{1,0:T(8,128)(2,1)} %all-gather.5.cloned.1.call-done.low_ref, bf16[384,1024]{1,0:T(8,128)(2,1)S(1)} %all_gather.15.high_ref, bf16[384,256]{1,0:T(8,128)(2,1)S(1)} %bitcast.99, bf16[384,128]{1,0:T(8,128)(2,1)S(1)} %get-tuple-element.57.h_ref), custom_call_target="tpu_custom_call" | custom-call | flops 1056964608 | bytes 8257536 | tf_op jit(solution)/shard_map/weight_grads/pallas_call | solution.py:47
  127.2 25.6 %all-to-all-done.3 = bf16[8,48,3712]{2,1,0:T(8,128)(2,1)} async-done(((bf16[8,48,3712]{2,1,0:T(8,128)(2,1)}), bf16[8,48,3712]{2,1,0:T(8,128)(2,1)}, u32[]{:S(2)}, u32[]{:S(2)}) %all-to-all-start.3) | async-done | bytes 2850848 | tf_op jit(solution)/shard_map/all_to_all | solution.py:159
  152.8 3.3 %fusion.6 = bf16[8,8,3712]{2,1,0:T(8,128)(2,1)} fusion(bf16[8,48,3712]{2,1,0:T(8,128)(2,1)} %all-to-all-done.3, bf16[64,48]{0,1:T(8,128)(2,1)S(1)} %fusion.28), kind=kOutput, calls=%fused_computation.12 | convolution fusion | flops 182689792 | bytes 3332096 | tf_op jit(solution)/shard_map/ck,kd->cd/dot_general | solution.py:70
  156.1 9.3 %all-to-all-start.4 = ((bf16[8,8,3712]{2,1,0:T(8,128)(2,1)}), bf16[8,8,3712]{2,1,0:T(8,128)(2,1)S(1)}, u32[]{:S(2)}, u32[]{:S(2)}) async-start(bf16[8,8,3712]{2,1,0:T(8,128)(2,1)} %fusion.6), calls=%async_computation.4 | async-start | bytes 950272 | tf_op jit(solution)/shard_map/all_to_all | solution.py:165
  165.4 1.0 dynamic-slice_bitcast_fusion.2
  166.4 0.8 copy.47
  167.2 1.1 dynamic-slice_bitcast_fusion
  169.8 13.4 %all-to-all-done.4 = bf16[8,8,3712]{2,1,0:T(8,128)(2,1)S(1)} async-done(((bf16[8,8,3712]{2,1,0:T(8,128)(2,1)}), bf16[8,8,3712]{2,1,0:T(8,128)(2,1)S(1)}, u32[]{:S(2)}, u32[]{:S(2)}) %all-to-all-start.4) | async-done | bytes 475168 | tf_op jit(solution)/shard_map/all_to_all | solution.py:165
  184.1 1.4 convolution_convert_fusion.1
  185.4 1.9 bitcast_convert_fusion
  (50 shorter events, 7.1 us)
Async XLA Ops:
  7.2 4.5 %copy-start = (bf16[128,3584]{1,0:T(8,128)(2,1)S(1)}, bf16[128,3584]{1,0:T(8,128)(2,1)}, u32[]{:S(2)}) copy-start(bf16[128,3584]{1,0:T(8,128)(2,1)} %param.8) | copy-start | bytes 2752516
  7.2 62.6 %all-gather.3.cloned.1.call-start = ((), (), s32[]{:S(2)}) async-start(), calls=%async_computation.6 | async-start | bytes 3096576 | tf_op jit(solution)/shard_map/all_gather | solution.py:78
  14.3 21.7 %all-to-all-start = ((bf16[4,8,7296]{2,1,0:T(8,128)(2,1)}), bf16[4,8,7296]{2,1,0:T(8,128)(2,1)S(1)}, u32[]{:S(2)}, u32[]{:S(2)}) async-start(bf16[4,8,7296]{2,1,0:T(8,128)(2,1)} %maximum_bitcast_fusion), calls=%async_computation | async-start | bytes 933888 | tf_op jit(solution)/shard_map/all_to_all | solution.py:100
  37.1 26.1 %all-to-all-start.1 = ((bf16[4,24,3584]{2,1,0:T(8,128)(2,1)}), bf16[4,24,3584]{2,1,0:T(8,128)(2,1)S(1)}, u32[]{:S(2)}, u32[]{:S(2)}) async-start(bf16[4,24,3584]{2,1,0:T(8,128)(2,1)} %broadcast_in_dim.58), calls=%async_computation.1 | async-start | bytes 1376256 | tf_op jit(solution)/shard_map/all_to_all | solution.py:24
  65.1 37.9 %all-to-all-start.2 = ((bf16[4,96,3712]{2,1,0:T(8,128)(2,1)}), bf16[4,96,3712]{2,1,0:T(8,128)(2,1)}, u32[]{:S(2)}, u32[]{:S(2)}) async-start(bf16[4,96,3712]{2,1,0:T(8,128)(2,1)} %broadcast_in_dim.63), calls=%async_computation.2 | async-start | bytes 5701632 | tf_op jit(solution)/shard_map/all_to_all | solution.py:24
  69.7 38.6 %all-gather.5.cloned.1.call-start = ((), (), s32[]{:S(2)}) async-start(), calls=%async_computation.7 | async-start | bytes 2457600 | tf_op jit(solution)/shard_map/all_gather | solution.py:115
  72.6 17.8 %copy-start.2 = (bf16[8,1,16,3584]{3,2,1,0:T(8,128)(2,1)}, bf16[8,1,16,3584]{3,2,1,0:T(8,128)(2,1)S(1)}, u32[]{:S(2)}) copy-start(bf16[8,1,16,3584]{3,2,1,0:T(8,128)(2,1)S(1)} %get-tuple-element.54) | copy-start | bytes 2752516
  72.7 17.8 %copy-start.3 = (bf16[8,1,16,3584]{3,2,1,0:T(8,128)(2,1)}, bf16[8,1,16,3584]{3,2,1,0:T(8,128)(2,1)S(1)}, u32[]{:S(2)}) copy-start(bf16[8,1,16,3584]{3,2,1,0:T(8,128)(2,1)S(1)} %get-tuple-element.52) | copy-start | bytes 2752516
  108.3 2.9 %copy-start.1 = (bf16[384,3712]{1,0:T(8,128)(2,1)S(1)}, bf16[384,3712]{1,0:T(8,128)(2,1)}, u32[]{:S(2)}) copy-start(bf16[384,3712]{1,0:T(8,128)(2,1)} %fusion.8) | copy-start | bytes 8552452
  114.4 38.4 %all-to-all-start.3 = ((bf16[8,48,3712]{2,1,0:T(8,128)(2,1)}), bf16[8,48,3712]{2,1,0:T(8,128)(2,1)}, u32[]{:S(2)}, u32[]{:S(2)}) async-start(bf16[8,48,3712]{2,1,0:T(8,128)(2,1)} %bitcast.100), calls=%async_computation.3 | async-start | bytes 5701632 | tf_op jit(solution)/shard_map/all_to_all | solution.py:159
  118.8 66.6 %reduce-scatter.2.cloned.1.call-start = ((), (), s32[]{:S(2)}) async-start(), calls=%async_computation.8 | async-start | bytes 3096576 | tf_op jit(solution)/shard_map/reduce_scatter | solution.py:156
  127.2 56.2 %copy-start.4 = (s32[128,8]{0,1:T(8,128)S(1)}, s32[128,8]{0,1:T(8,128)}, u32[]{:S(2)}) copy-start(s32[128,8]{0,1:T(8,128)} %param.9) | copy-start | bytes 12292
  156.1 27.1 %all-to-all-start.4 = ((bf16[8,8,3712]{2,1,0:T(8,128)(2,1)}), bf16[8,8,3712]{2,1,0:T(8,128)(2,1)S(1)}, u32[]{:S(2)}, u32[]{:S(2)}) async-start(bf16[8,8,3712]{2,1,0:T(8,128)(2,1)} %fusion.6), calls=%async_computation.4 | async-start | bytes 950272 | tf_op jit(solution)/shard_map/all_to_all | solution.py:165
Sparse Core Ops, SparseCore 0:
  10.1 54.1 all-gather.2
  72.6 35.6 all-gather.4
  127.2 56.0 reduce-scatter.1
